TPU v7x, 512 devices: a whole 4x8x8 slice. The times are simulated.
512 devices in a mesh: tm: 4 (over x), space: 128 (over z, y, core).
Axes of the slice: x: 4, y: 8, z: 8, core: 2. Of those that a mesh axis runs over, the one named last changes fastest.
Arguments:
- q_start: float32 [5, 512, 64, 128], P(None, 'space'), may hold values from -3.6 to 3.6
- guess: float32 [4, 5, 512, 64, 128], P('tm', None, 'space'), may hold values from -3.6 to 3.6
Outputs:
- corrected: float32 [4, 5, 512, 64, 128], P('tm', None, 'space')
- residual: float32 [4, 5, 512, 64, 128], P('tm', None, 'space')
All inputs are finite; a program needn't handle non-finite values.
Results may differ from a plain program's by a relative error of at most 0.00011.
Values sent between devices are 32-bit elements; how exact they have to be, the bound alone decides.
No kernel may reach another device: no remote copies, remote signals or barrier semaphores. Data moves between devices by JAX's collectives and lax.ppermute only.
A program may use at most 64 MiB of HBM per device.

v0:
```python
import jax
import jax.numpy as jnp
from jax import lax
from jax.sharding import PartitionSpec as P

NZ = 128
COMP = 5
STEPS_SLAB = 2
SWEEPS = 2
BLK = 4


time_step = 0.1
cross = 8.0
axial = 2.0
linear_rate = 0.1
quadratic_rate = 0.5
cubic_rate = 1.0


def with_halo(block, sides, width):
    for axis, dim in sides:
        count = lax.axis_size(axis)
        forward = [(i, i + 1) for i in range(count - 1)]
        backward = [(target, source) for source, target in forward]
        low = lax.ppermute(
            lax.slice_in_dim(block, block.shape[dim] - width, None, axis=dim), axis, forward
        )
        high = lax.ppermute(lax.slice_in_dim(block, 0, width, axis=dim), axis, backward)
        block = jnp.concatenate([low, block, high], axis=dim)
    return block


def passed_along(block, axis, distance):
    devices = range(lax.axis_size(axis))
    route = [(i - distance, i) for i in devices if i - distance in devices]
    return lax.ppermute(block, axis, route)


def prefix(part, axis, combine, identity):
    place = lax.axis_index(axis)
    gathered = jax.tree.map(lambda a: lax.all_gather(a, axis), part)
    state = jax.tree.map(lambda a, e: jnp.zeros_like(a) + jnp.asarray(e, a.dtype), part, identity)

    def one(turn, state):
        return combine(
            state, jax.tree.map(lambda a: lax.dynamic_index_in_dim(a, turn, 0, False), gathered)
        )

    return lax.fori_loop(0, place, one, state)


def bulk_terms(field):
    first, second, third, fourth, fifth = (field[0], field[1], field[2], field[3], field[4])
    sixth = -first - fourth
    s_aa = first * first + second * second + third * third
    s_ab = first * second + second * fourth + third * fifth
    s_ac = first * third + second * fifth + third * sixth
    s_bb = second * second + fourth * fourth + fifth * fifth
    s_bc = second * third + fourth * fifth + fifth * sixth
    trace = (
        first * first
        + fourth * fourth
        + sixth * sixth
        + 2.0 * (second * second + third * third + fifth * fifth)
    )
    quad = jnp.stack([s_aa - trace / 3.0, s_ab, s_ac, s_bb - trace / 3.0, s_bc])
    source = field + time_step * quadratic_rate * quad
    diagonal = 1.0 + time_step * (linear_rate + cubic_rate * trace) + 2.0 * (2.0 * cross + axial)
    return (source, diagonal)


def jacobi(extended, source, diagonal):
    inner = extended[:, 1:-1]
    along_x = extended[:, :-2] + extended[:, 2:]
    padded_y = jnp.pad(inner, ((0, 0), (0, 0), (1, 1), (0, 0)))
    along_y = padded_y[:, :, :-2] + padded_y[:, :, 2:]
    along_z = jnp.roll(inner, 1, 3) + jnp.roll(inner, -1, 3)
    return (source + cross * (along_x + along_y) + axial * along_z) / diagonal[None]


def extend(field, margin):
    return with_halo(field, (("space", 1),), margin)


def propagate(field):
    for step in range(STEPS_SLAB):
        source, diagonal = bulk_terms(field)
        current = field
        for sweep in range(SWEEPS):
            current = jacobi(extend(current, 1), source, diagonal)
        field = current
    return field


def chain_combine(earlier, later):
    return (earlier[0] * later[0], later[0] * earlier[1] + later[1])


def per_device(q_start, guess):
    own = guess[0]
    position = lax.axis_index("tm")
    prior = passed_along(own, "tm", 1)
    start = jnp.where(position == 0, q_start, prior)
    relaxed = propagate(start)
    moved = passed_along(relaxed, "tm", 1)
    start_two = jnp.where(position == 0, q_start, moved)
    again = propagate(start_two)
    residual = again - relaxed
    change = again - own
    cells_total = change.shape[1] * change.shape[2] * lax.axis_size("space")
    partial_sum = jnp.sum(change, axis=(1, 2))
    partial_sum = partial_sum.reshape(COMP, NZ // BLK, BLK).sum(axis=2)
    totals = lax.psum(partial_sum, "space")
    coarse = totals / (cells_total * BLK)
    decay = 1.0 / (1.0 + STEPS_SLAB * time_step * linear_rate)
    factor = jnp.full((), decay, jnp.float32)
    identity = (jnp.ones((), jnp.float32), jnp.zeros_like(coarse))
    passed = prefix((factor, coarse), "tm", chain_combine, identity)
    error = decay * passed[1] + coarse
    spread = jnp.broadcast_to(error[:, None, None, :, None], (COMP, 1, 1, NZ // BLK, BLK))
    spread = spread.reshape(COMP, 1, 1, NZ)
    corrected = relaxed + spread
    return (corrected[None], residual[None])


def solution(mesh):
    return jax.shard_map(
        per_device,
        mesh=mesh,
        in_specs=(P(None, "space", None, None), P("tm", None, "space", None, None)),
        out_specs=(P("tm", None, "space", None, None), P("tm", None, "space", None, None)),
        check_vma=False,
    )
```

profile of v0, /device:TPU:262, one launch (start us, length us, event | category | flops | bytes accessed | tf_op | source)
XLA Modules:
  0.0 409.1 jit_solution(18188361148212606499)
XLA Ops:
  0.6 1.3 collective-permute-start
  1.9 17.3 %collective-permute-done = f32[5,4,64,128]{3,2,1,0:T(8,128)S(1)} collective-permute-done((f32[5,4,64,128]{3,2,1,0:T(8,128)}, f32[5,4,64,128]{3,2,1,0:T(8,128)S(1)}, u32[]{:S(2)}, u32[]{:S(2)}) %collective-permute-start) | collective-permute-done | bytes 655392 | tf_op jit(solution)/shard_map/ppermute | solution.py:37
  19.4 0.2 fusion.90
  19.6 0.3 fusion.91
  20.1 1.9 collective-permute-start.1
  22.0 7.0 %collective-permute-start.2 = (f32[5,1,64,128]{3,2,1,0:T(8,128)S(1)}, f32[5,1,64,128]{3,2,1,0:T(8,128)S(1)}, u32[]{:S(2)}, u32[]{:S(2)}) collective-permute-start(f32[5,1,64,128]{3,2,1,0:T(8,128)S(1)} %get-tuple-element.114), channel_id=1, source_target_pairs={{1,0},{2,1},{3,2},{4,3},{5,4},{6,5},{7,6},{8,7},{9,8},{10,9},{11,1... | collective-permute-start | bytes 491528 | tf_op jit(solution)/shard_map/ppermute | solution.py:29
  29.0 1.0 collective-permute-done.1
  30.0 1.8 collective-permute-done.2
  31.8 0.6 fusion.5
  32.4 0.2 fusion.87
  32.7 1.9 collective-permute-start.3
  34.6 7.1 %collective-permute-start.4 = (f32[5,1,64,128]{3,2,1,0:T(8,128)S(1)}, f32[5,1,64,128]{3,2,1,0:T(8,128)S(1)}, u32[]{:S(2)}, u32[]{:S(2)}) collective-permute-start(f32[5,1,64,128]{3,2,1,0:T(8,128)S(1)} %get-tuple-element.108), channel_id=1, source_target_pairs={{1,0},{2,1},{3,2},{4,3},{5,4},{6,5},{7,6},{8,7},{9,8},{10,9},{11,1... | collective-permute-start | bytes 491528 | tf_op jit(solution)/shard_map/ppermute | solution.py:29
  41.7 0.2 fusion.88
  42.0 0.8 collective-permute-done.3
  42.8 1.8 collective-permute-done.4
  44.6 0.6 fusion.11
  45.3 0.2 fusion.85
  45.5 0.3 fusion.84
  46.0 1.9 collective-permute-start.5
  47.9 7.1 %collective-permute-start.6 = (f32[5,1,64,128]{3,2,1,0:T(8,128)S(1)}, f32[5,1,64,128]{3,2,1,0:T(8,128)S(1)}, u32[]{:S(2)}, u32[]{:S(2)}) collective-permute-start(f32[5,1,64,128]{3,2,1,0:T(8,128)S(1)} %get-tuple-element.102), channel_id=1, source_target_pairs={{1,0},{2,1},{3,2},{4,3},{5,4},{6,5},{7,6},{8,7},{9,8},{10,9},{11,1... | collective-permute-start | bytes 491528 | tf_op jit(solution)/shard_map/ppermute | solution.py:29
  55.1 1.0 collective-permute-done.5
  56.1 1.8 collective-permute-done.6
  57.9 0.6 fusion.17
  58.7 1.9 collective-permute-start.7
  60.7 7.1 %collective-permute-start.8 = (f32[5,1,64,128]{3,2,1,0:T(8,128)S(1)}, f32[5,1,64,128]{3,2,1,0:T(8,128)S(1)}, u32[]{:S(2)}, u32[]{:S(2)}) collective-permute-start(f32[5,1,64,128]{3,2,1,0:T(8,128)S(1)} %get-tuple-element.96), channel_id=1, source_target_pairs={{1,0},{2,1},{3,2},{4,3},{5,4},{6,5},{7,6},{8,7},{9,8},{10,9},{11,1... | collective-permute-start | bytes 491528 | tf_op jit(solution)/shard_map/ppermute | solution.py:29
  68.1 0.8 collective-permute-done.7
  68.9 1.8 collective-permute-done.8
  70.6 0.6 fusion.23
  71.3 1.3 collective-permute-start.9
  72.6 1.3 dynamic-slice
  73.8 0.8 dynamic-update-slice
  74.6 11.7 %all-reduce.8 = f32[4]{0:T(128)S(1)} all-reduce(f32[4]{0:T(128)S(1)} %dynamic-update-slice), channel_id=1, replica_groups=mesh['tm'=4,'space'=128] {'tm'}, use_global_device_ids=true, to_apply=%add.8 | all-reduce | flops 4 | bytes 32
  86.7 0.3 fusion.79
  87.1 1.9 collective-permute-start.10
  89.1 7.9 %collective-permute-start.11 = (f32[5,1,64,128]{3,2,1,0:T(8,128)S(1)}, f32[5,1,64,128]{3,2,1,0:T(8,128)S(1)}, u32[]{:S(2)}, u32[]{:S(2)}) collective-permute-start(f32[5,1,64,128]{3,2,1,0:T(8,128)S(1)} %get-tuple-element.90), channel_id=1, source_target_pairs={{1,0},{2,1},{3,2},{4,3},{5,4},{6,5},{7,6},{8,7},{9,8},{10,9},{11,1... | collective-permute-start | bytes 491528 | tf_op jit(solution)/shard_map/ppermute | solution.py:29
  97.0 1.0 collective-permute-done.10
  98.1 1.8 collective-permute-done.11
  99.8 0.6 fusion.29
  100.7 1.9 collective-permute-start.12
  102.6 7.1 %collective-permute-start.13 = (f32[5,1,64,128]{3,2,1,0:T(8,128)S(1)}, f32[5,1,64,128]{3,2,1,0:T(8,128)S(1)}, u32[]{:S(2)}, u32[]{:S(2)}) collective-permute-start(f32[5,1,64,128]{3,2,1,0:T(8,128)S(1)} %get-tuple-element.84), channel_id=1, source_target_pairs={{1,0},{2,1},{3,2},{4,3},{5,4},{6,5},{7,6},{8,7},{9,8},{10,9},{11,1... | collective-permute-start | bytes 491528 | tf_op jit(solution)/shard_map/ppermute | solution.py:29
  110.0 0.8 collective-permute-done.12
  110.8 1.8 collective-permute-done.13
  112.6 0.7 fusion.35
  113.6 0.3 fusion.73
  114.0 1.9 collective-permute-start.14
  116.0 7.1 %collective-permute-start.15 = (f32[5,1,64,128]{3,2,1,0:T(8,128)S(1)}, f32[5,1,64,128]{3,2,1,0:T(8,128)S(1)}, u32[]{:S(2)}, u32[]{:S(2)}) collective-permute-start(f32[5,1,64,128]{3,2,1,0:T(8,128)S(1)} %get-tuple-element.78), channel_id=1, source_target_pairs={{1,0},{2,1},{3,2},{4,3},{5,4},{6,5},{7,6},{8,7},{9,8},{10,9},{11,1... | collective-permute-start | bytes 491528 | tf_op jit(solution)/shard_map/ppermute | solution.py:29
  123.2 1.0 collective-permute-done.14
  124.2 1.8 collective-permute-done.15
  125.9 0.6 fusion.41
  126.8 1.9 collective-permute-start.16
  128.7 7.1 %collective-permute-start.17 = (f32[5,1,64,128]{3,2,1,0:T(8,128)S(1)}, f32[5,1,64,128]{3,2,1,0:T(8,128)S(1)}, u32[]{:S(2)}, u32[]{:S(2)}) collective-permute-start(f32[5,1,64,128]{3,2,1,0:T(8,128)S(1)} %get-tuple-element.68), channel_id=1, source_target_pairs={{1,0},{2,1},{3,2},{4,3},{5,4},{6,5},{7,6},{8,7},{9,8},{10,9},{11,1... | collective-permute-start | bytes 491528 | tf_op jit(solution)/shard_map/ppermute | solution.py:29
  136.1 0.8 collective-permute-done.16
  136.9 1.8 collective-permute-done.17
  138.7 1.5 subtract_bitcast_fusion
  140.5 252.0 %psum.7 = f32[5,32]{1,0:T(8,128)S(1)} all-reduce(f32[5,32]{1,0:T(8,128)S(1)} %reduce_sum.19), channel_id=1, replica_groups=mesh['tm'=4,'space'=128] {'space'}, use_global_device_ids=true, to_apply=%region_2.3 | all-reduce | flops 160 | bytes 1280 | tf_op jit(solution)/shard_map/psum | solution.py:114
  392.6 11.9 %all-gather.1 = f32[4,5,32]{2,1,0:T(8,128)S(1)} all-gather(f32[1,5,32]{2,1,0:T(8,128)S(1)} %multiply_bitcast_fusion), channel_id=2, replica_groups=mesh['tm'=4,'space'=128] {'tm'}, dimensions={0}, use_global_device_ids=true | all-gather | bytes 3200 | tf_op jit(solution)/shard_map/all_gather | solution.py:42
  404.5 3.5 while.12
  404.5 0.6 dynamic_slice.14
  405.1 0.6 bitcast_add_fusion.2
  405.7 0.6 dynamic_slice.14
  406.3 0.6 bitcast_add_fusion.2
  406.9 0.6 dynamic_slice.14
  407.4 0.6 bitcast_add_fusion.2
  408.2 0.9 add_bitcast_fusion
  (56 shorter events, 3.9 us)
Async XLA Ops:
  0.6 18.6 %collective-permute-start = (f32[5,4,64,128]{3,2,1,0:T(8,128)}, f32[5,4,64,128]{3,2,1,0:T(8,128)S(1)}, u32[]{:S(2)}, u32[]{:S(2)}) collective-permute-start(f32[5,4,64,128]{3,2,1,0:T(8,128)} %bitcast.24), channel_id=1, source_target_pairs={{0,128},{128,256},{256,384},{1,129},{129,257},{257,385},{2,130},{1... | collective-permute-start | bytes 1966088 | tf_op jit(solution)/shard_map/ppermute | solution.py:37
  20.1 10.0 %collective-permute-start.1 = (f32[5,1,64,128]{3,2,1,0:T(8,128)S(1)}, f32[5,1,64,128]{3,2,1,0:T(8,128)S(1)}, u32[]{:S(2)}, u32[]{:S(2)}) collective-permute-start(f32[5,1,64,128]{3,2,1,0:T(8,128)S(1)} %get-tuple-element.113), channel_id=1, source_target_pairs={{0,1},{1,2},{2,3},{3,4},{4,5},{5,6},{6,7},{7,8},{8,9},{9,10},{10,1... | collective-permute-start | bytes 491528 | tf_op jit(solution)/shard_map/ppermute | solution.py:26
  22.0 9.8 %collective-permute-start.2 = (f32[5,1,64,128]{3,2,1,0:T(8,128)S(1)}, f32[5,1,64,128]{3,2,1,0:T(8,128)S(1)}, u32[]{:S(2)}, u32[]{:S(2)}) collective-permute-start(f32[5,1,64,128]{3,2,1,0:T(8,128)S(1)} %get-tuple-element.114), channel_id=1, source_target_pairs={{1,0},{2,1},{3,2},{4,3},{5,4},{6,5},{7,6},{8,7},{9,8},{10,9},{11,1... | collective-permute-start | bytes 491528 | tf_op jit(solution)/shard_map/ppermute | solution.py:29
  32.7 10.1 %collective-permute-start.3 = (f32[5,1,64,128]{3,2,1,0:T(8,128)S(1)}, f32[5,1,64,128]{3,2,1,0:T(8,128)S(1)}, u32[]{:S(2)}, u32[]{:S(2)}) collective-permute-start(f32[5,1,64,128]{3,2,1,0:T(8,128)S(1)} %get-tuple-element.107), channel_id=1, source_target_pairs={{0,1},{1,2},{2,3},{3,4},{4,5},{5,6},{6,7},{7,8},{8,9},{9,10},{10,1... | collective-permute-start | bytes 491528 | tf_op jit(solution)/shard_map/ppermute | solution.py:26
  34.6 10.0 %collective-permute-start.4 = (f32[5,1,64,128]{3,2,1,0:T(8,128)S(1)}, f32[5,1,64,128]{3,2,1,0:T(8,128)S(1)}, u32[]{:S(2)}, u32[]{:S(2)}) collective-permute-start(f32[5,1,64,128]{3,2,1,0:T(8,128)S(1)} %get-tuple-element.108), channel_id=1, source_target_pairs={{1,0},{2,1},{3,2},{4,3},{5,4},{6,5},{7,6},{8,7},{9,8},{10,9},{11,1... | collective-permute-start | bytes 491528 | tf_op jit(solution)/shard_map/ppermute | solution.py:29
  46.0 10.1 %collective-permute-start.5 = (f32[5,1,64,128]{3,2,1,0:T(8,128)S(1)}, f32[5,1,64,128]{3,2,1,0:T(8,128)S(1)}, u32[]{:S(2)}, u32[]{:S(2)}) collective-permute-start(f32[5,1,64,128]{3,2,1,0:T(8,128)S(1)} %get-tuple-element.101), channel_id=1, source_target_pairs={{0,1},{1,2},{2,3},{3,4},{4,5},{5,6},{6,7},{7,8},{8,9},{9,10},{10,1... | collective-permute-start | bytes 491528 | tf_op jit(solution)/shard_map/ppermute | solution.py:26
  47.9 10.0 %collective-permute-start.6 = (f32[5,1,64,128]{3,2,1,0:T(8,128)S(1)}, f32[5,1,64,128]{3,2,1,0:T(8,128)S(1)}, u32[]{:S(2)}, u32[]{:S(2)}) collective-permute-start(f32[5,1,64,128]{3,2,1,0:T(8,128)S(1)} %get-tuple-element.102), channel_id=1, source_target_pairs={{1,0},{2,1},{3,2},{4,3},{5,4},{6,5},{7,6},{8,7},{9,8},{10,9},{11,1... | collective-permute-start | bytes 491528 | tf_op jit(solution)/shard_map/ppermute | solution.py:29
  58.7 10.1 %collective-permute-start.7 = (f32[5,1,64,128]{3,2,1,0:T(8,128)S(1)}, f32[5,1,64,128]{3,2,1,0:T(8,128)S(1)}, u32[]{:S(2)}, u32[]{:S(2)}) collective-permute-start(f32[5,1,64,128]{3,2,1,0:T(8,128)S(1)} %get-tuple-element.95), channel_id=1, source_target_pairs={{0,1},{1,2},{2,3},{3,4},{4,5},{5,6},{6,7},{7,8},{8,9},{9,10},{10,1... | collective-permute-start | bytes 491528 | tf_op jit(solution)/shard_map/ppermute | solution.py:26
  60.7 10.0 %collective-permute-start.8 = (f32[5,1,64,128]{3,2,1,0:T(8,128)S(1)}, f32[5,1,64,128]{3,2,1,0:T(8,128)S(1)}, u32[]{:S(2)}, u32[]{:S(2)}) collective-permute-start(f32[5,1,64,128]{3,2,1,0:T(8,128)S(1)} %get-tuple-element.96), channel_id=1, source_target_pairs={{1,0},{2,1},{3,2},{4,3},{5,4},{6,5},{7,6},{8,7},{9,8},{10,9},{11,1... | collective-permute-start | bytes 491528 | tf_op jit(solution)/shard_map/ppermute | solution.py:29
  70.6 15.6 %copy-start = (f32[5,4,64,128]{3,2,1,0:T(8,128)S(1)}, f32[5,4,64,128]{3,2,1,0:T(8,128)}, u32[]{:S(2)}) copy-start(f32[5,4,64,128]{3,2,1,0:T(8,128)} %param.4) | copy-start | bytes 1966084
  71.3 15.0 %collective-permute-start.9 = (f32[5,4,64,128]{3,2,1,0:T(8,128)S(1)}, f32[5,4,64,128]{3,2,1,0:T(8,128)S(1)}, u32[]{:S(2)}, u32[]{:S(2)}) collective-permute-start(f32[5,4,64,128]{3,2,1,0:T(8,128)S(1)} %fusion.23), channel_id=1, source_target_pairs={{0,128},{128,256},{256,384},{1,129},{129,257},{257,385},{2,130},{1... | collective-permute-start | bytes 1966088 | tf_op jit(solution)/shard_map/ppermute | solution.py:37
  87.1 10.9 %collective-permute-start.10 = (f32[5,1,64,128]{3,2,1,0:T(8,128)S(1)}, f32[5,1,64,128]{3,2,1,0:T(8,128)S(1)}, u32[]{:S(2)}, u32[]{:S(2)}) collective-permute-start(f32[5,1,64,128]{3,2,1,0:T(8,128)S(1)} %get-tuple-element.89), channel_id=1, source_target_pairs={{0,1},{1,2},{2,3},{3,4},{4,5},{5,6},{6,7},{7,8},{8,9},{9,10},{10,1... | collective-permute-start | bytes 491528 | tf_op jit(solution)/shard_map/ppermute | solution.py:26
  89.1 10.7 %collective-permute-start.11 = (f32[5,1,64,128]{3,2,1,0:T(8,128)S(1)}, f32[5,1,64,128]{3,2,1,0:T(8,128)S(1)}, u32[]{:S(2)}, u32[]{:S(2)}) collective-permute-start(f32[5,1,64,128]{3,2,1,0:T(8,128)S(1)} %get-tuple-element.90), channel_id=1, source_target_pairs={{1,0},{2,1},{3,2},{4,3},{5,4},{6,5},{7,6},{8,7},{9,8},{10,9},{11,1... | collective-permute-start | bytes 491528 | tf_op jit(solution)/shard_map/ppermute | solution.py:29
  100.7 10.1 %collective-permute-start.12 = (f32[5,1,64,128]{3,2,1,0:T(8,128)S(1)}, f32[5,1,64,128]{3,2,1,0:T(8,128)S(1)}, u32[]{:S(2)}, u32[]{:S(2)}) collective-permute-start(f32[5,1,64,128]{3,2,1,0:T(8,128)S(1)} %get-tuple-element.83), channel_id=1, source_target_pairs={{0,1},{1,2},{2,3},{3,4},{4,5},{5,6},{6,7},{7,8},{8,9},{9,10},{10,1... | collective-permute-start | bytes 491528 | tf_op jit(solution)/shard_map/ppermute | solution.py:26
  102.6 10.0 %collective-permute-start.13 = (f32[5,1,64,128]{3,2,1,0:T(8,128)S(1)}, f32[5,1,64,128]{3,2,1,0:T(8,128)S(1)}, u32[]{:S(2)}, u32[]{:S(2)}) collective-permute-start(f32[5,1,64,128]{3,2,1,0:T(8,128)S(1)} %get-tuple-element.84), channel_id=1, source_target_pairs={{1,0},{2,1},{3,2},{4,3},{5,4},{6,5},{7,6},{8,7},{9,8},{10,9},{11,1... | collective-permute-start | bytes 491528 | tf_op jit(solution)/shard_map/ppermute | solution.py:29
  114.0 10.1 %collective-permute-start.14 = (f32[5,1,64,128]{3,2,1,0:T(8,128)S(1)}, f32[5,1,64,128]{3,2,1,0:T(8,128)S(1)}, u32[]{:S(2)}, u32[]{:S(2)}) collective-permute-start(f32[5,1,64,128]{3,2,1,0:T(8,128)S(1)} %get-tuple-element.77), channel_id=1, source_target_pairs={{0,1},{1,2},{2,3},{3,4},{4,5},{5,6},{6,7},{7,8},{8,9},{9,10},{10,1... | collective-permute-start | bytes 491528 | tf_op jit(solution)/shard_map/ppermute | solution.py:26
  116.0 10.0 %collective-permute-start.15 = (f32[5,1,64,128]{3,2,1,0:T(8,128)S(1)}, f32[5,1,64,128]{3,2,1,0:T(8,128)S(1)}, u32[]{:S(2)}, u32[]{:S(2)}) collective-permute-start(f32[5,1,64,128]{3,2,1,0:T(8,128)S(1)} %get-tuple-element.78), channel_id=1, source_target_pairs={{1,0},{2,1},{3,2},{4,3},{5,4},{6,5},{7,6},{8,7},{9,8},{10,9},{11,1... | collective-permute-start | bytes 491528 | tf_op jit(solution)/shard_map/ppermute | solution.py:29
  126.8 10.1 %collective-permute-start.16 = (f32[5,1,64,128]{3,2,1,0:T(8,128)S(1)}, f32[5,1,64,128]{3,2,1,0:T(8,128)S(1)}, u32[]{:S(2)}, u32[]{:S(2)}) collective-permute-start(f32[5,1,64,128]{3,2,1,0:T(8,128)S(1)} %get-tuple-element.67), channel_id=1, source_target_pairs={{0,1},{1,2},{2,3},{3,4},{4,5},{5,6},{6,7},{7,8},{8,9},{9,10},{10,1... | collective-permute-start | bytes 491528 | tf_op jit(solution)/shard_map/ppermute | solution.py:26
  128.7 10.0 %collective-permute-start.17 = (f32[5,1,64,128]{3,2,1,0:T(8,128)S(1)}, f32[5,1,64,128]{3,2,1,0:T(8,128)S(1)}, u32[]{:S(2)}, u32[]{:S(2)}) collective-permute-start(f32[5,1,64,128]{3,2,1,0:T(8,128)S(1)} %get-tuple-element.68), channel_id=1, source_target_pairs={{1,0},{2,1},{3,2},{4,3},{5,4},{6,5},{7,6},{8,7},{9,8},{10,9},{11,1... | collective-permute-start | bytes 491528 | tf_op jit(solution)/shard_map/ppermute | solution.py:29
  138.7 1.5 copy-start.1
where the time goes:
time: 410 us; the launch traced here: 409 us
  blocking collectives  276 us (67%)
  starting transfers between devices  75.6 us (18%)
  waiting for transfers between devices  38.6 us (9%)
  other arithmetic  9.83 us (2%)
  local copies, waits for them, and re-layouts  8.23 us (2%)
    psum x1, blocking collectives, per_device(): totals = lax.psum(partial_sum, 'space')  252 us
    ppermute x8, starting transfers between devices, with_halo(): lax.ppermute(lax.slice_in_dim(block, 0, width, axis=dim), axis, backward)  57.7 us
    ppermute x2, waiting for transfers between devices, passed_along(): return lax.ppermute(block, axis, route)  17.3 us
    ppermute x8, starting transfers between devices, with_halo(): lax.ppermute(lax.slice_in_dim(block, block.shape[dim] - width, None, axis...  15.4 us
    ppermute x8, waiting for transfers between devices, with_halo(): lax.ppermute(lax.slice_in_dim(block, 0, width, axis=dim), axis, backward)  14 us
    all_gather x1, blocking collectives, prefix(): gathered = jax.tree.map(lambda a: lax.all_gather(a, axis), part)  11.9 us
    unnamed x1, blocking collectives  11.7 us
  transfers between devices with their start and end apart: 18, of which 17 were waited for; matrix products, arithmetic and copies ran while one was open for 1% of the time, Pallas kernels for 0%

commit v1 on v0

v1 whole, which is shorter than its diff:
```python
import jax
import jax.numpy as jnp
import numpy as np
from jax import lax
from jax.experimental import pallas as pl
from jax.experimental.pallas import tpu as pltpu
from jax.sharding import Mesh
from jax.sharding import PartitionSpec as P

COMP = 5
STEPS_SLAB = 2
BLK = 4
ROWS = 4
PAD = 8
GROUP = 16

time_step = 0.1
cross = 8.0
axial = 2.0
linear_rate = 0.1
quadratic_rate = 0.5
cubic_rate = 1.0

SPACE = ("outer", "inner")


def phi_rows(first, last, w, v, src, rdg, emit, ny):
    ys = pl.ds(PAD, ny)
    low_mask = jnp.where(first, 0.0, 1.0)
    high_mask = jnp.where(last, 0.0, 1.0)

    def bulk(row):
        part = 32
        for y in range(0, ny, part):
            at = pl.ds(PAD + y, part)
            q = [w[c, row, at, :] for c in range(COMP)]
            a, b, c, d, e = q
            f = -a - d
            aa, bb, cc, dd, ee = a * a, b * b, c * c, d * d, e * e
            trace = aa + dd + f * f + 2.0 * (bb + cc + ee)
            third = trace * (1.0 / 3.0)
            quad = (
                aa + bb + cc - third,
                a * b + b * d + c * e,
                a * c + b * e + c * f,
                bb + dd + ee - third,
                b * c + d * e + e * f,
            )
            out = pl.ds(y, part)
            for k in range(COMP):
                src[k, row, out, :] = (1.0 / cross) * q[k] + (time_step * quadratic_rate / cross) * quad[k]
            scale = cross
            if row < ROWS:
                scale = cross * low_mask
            if row >= 2 * ROWS:
                scale = cross * high_mask
            diagonal = (1.0 + time_step * linear_rate + 2.0 * (2.0 * cross + axial)) + (time_step * cubic_rate) * trace
            rdg[row, out, :] = scale / diagonal

    def sweep(a, rows, store):
        for row in rows:
            rd = rdg[row]
            for k in range(COMP):
                here = a[k, row, ys, :]
                along_x = a[k, row - 1, ys, :] + a[k, row + 1, ys, :]
                along_y = a[k, row, pl.ds(PAD - 1, ny), :] + a[k, row, pl.ds(PAD + 1, ny), :]
                along_z = pltpu.roll(here, 1, 1) + pltpu.roll(here, here.shape[1] - 1, 1)
                store(k, row, (src[k, row] + (along_x + along_y) + (axial / cross) * along_z) * rd)

    def into(buf):
        def store(k, row, value):
            buf[k, row, ys, :] = value

        return store

    for row in range(1, 3 * ROWS - 1):
        bulk(row)
    sweep(w, range(1, 11), into(v))
    sweep(v, range(2, 10), into(w))
    for row in range(3, 9):
        bulk(row)
    sweep(w, range(3, 9), into(v))
    sweep(v, range(4, 8), emit)


def place():
    outer, inner = lax.axis_index("outer"), lax.axis_index("inner")
    count = lax.axis_size("outer") * lax.axis_size("inner")
    index = outer * lax.axis_size("inner") + inner
    return index, count


def gather_rows(own, near, far, w, v, sems, ny):
    index, count = place()
    odd = index % 2
    near_at = jnp.where(odd == 1, 0, 2 * ROWS)
    far_at = jnp.where(odd == 1, 2 * ROWS, 0)
    ys = pl.ds(PAD, ny)
    copies = [
        pltpu.make_async_copy(own, w.at[:, pl.ds(ROWS, ROWS), ys, :], sems.at[0]),
        pltpu.make_async_copy(near, w.at[:, pl.ds(near_at, ROWS), ys, :], sems.at[1]),
        pltpu.make_async_copy(far, w.at[:, pl.ds(far_at, ROWS), ys, :], sems.at[2]),
    ]
    for copy in copies:
        copy.start()
    zero = jnp.zeros((COMP, 3 * ROWS, PAD, w.shape[3]), jnp.float32)
    for buf in (w, v):
        buf[:, :, pl.ds(0, PAD), :] = zero
        buf[:, :, pl.ds(PAD + ny, PAD), :] = zero
    for copy in copies:
        copy.wait()
    return index == 0, index == count - 1


def first_kernel(own, near, far, out, w, v, src, rdg, sems):
    ny = out.shape[2]
    first, last = gather_rows(own, near, far, w, v, sems, ny)

    def emit(k, row, value):
        out[k, row - ROWS] = value

    phi_rows(first, last, w, v, src, rdg, emit, ny)


def exact_dot(a, b):
    return jnp.dot(a, b, precision=lax.Precision.HIGHEST, preferred_element_type=jnp.float32)


def second_kernel(own, near, far, guess, weights, out, share, w, v, src, rdg, sems):
    ny, nz = out.shape[2], out.shape[3]
    first, last = gather_rows(own, near, far, w, v, sems, ny)
    sums = []
    for k in range(COMP):
        mine = [w[k, ROWS + r, pl.ds(PAD, ny), :] for r in range(ROWS)]
        sums.append(
            (
                jnp.sum(sum(mine[1:], mine[0]), axis=0, keepdims=True),
                jnp.sum(jnp.sum(guess[0, k], axis=0), axis=0, keepdims=True),
            )
        )
    total = [jnp.zeros((ny, nz), jnp.float32) for _ in range(COMP)]

    def emit(k, row, value):
        out[k, row - ROWS] = value
        total[k] = total[k] + value

    phi_rows(first, last, w, v, src, rdg, emit, ny)
    none = jnp.zeros((8 - COMP, nz), jnp.float32)

    def rows(parts):
        return jnp.concatenate(parts + [none], axis=0)

    slab = lax.axis_index("tm")
    blocks = nz // BLK
    cell = lax.broadcasted_iota(jnp.int32, (nz, nz), 0) // BLK
    slot = lax.broadcasted_iota(jnp.int32, (nz, nz), 1) % blocks
    pick = jnp.where(cell == slot, 1.0, 0.0)
    again = exact_dot(rows([jnp.sum(t, axis=0, keepdims=True) for t in total]), pick)
    relaxed = exact_dot(rows([s[0] for s in sums]), pick)
    old = exact_dot(rows([s[1] for s in sums]), pick)
    weight = weights[slab]
    value = weight[0:1] * again + weight[1:2] * relaxed + weight[2:3] * old
    for i in range(share.shape[0]):
        share[i] = value


def relay_kernel(parts, share):
    value = parts[0]
    for i in range(1, parts.shape[0]):
        value = value + parts[i]
    for i in range(share.shape[0]):
        share[i] = value


def last_kernel(parts, relaxed, again, corrected, residual, error):
    nz = relaxed.shape[3]
    slab = lax.axis_index("tm")
    k = pl.program_id(0)

    @pl.when(k == 0)
    def _():
        value = parts[0]
        for i in range(1, parts.shape[0]):
            value = value + parts[i]
        blocks = nz // BLK
        slot = lax.broadcasted_iota(jnp.int32, (nz, nz), 0)
        cell = lax.broadcasted_iota(jnp.int32, (nz, nz), 1) // BLK
        error[...] = exact_dot(value, jnp.where(slot == slab * blocks + cell, 1.0, 0.0))

    mine = relaxed[0]
    other = jnp.where(slab == 0, mine, again[0])
    corrected[0, 0] = mine + error[pl.ds(k, 1), :][None]
    residual[0, 0] = other - mine


def slot_weights(slabs, nz, cells):
    decay = 1.0 / (1.0 + STEPS_SLAB * time_step * linear_rate)
    table = np.zeros((slabs, 8, nz))
    blocks = nz // BLK
    for own in range(slabs):
        chain = (own + 1) % slabs
        slots = {2: (own, -1.0)}
        if chain + 1 < slabs:
            slots[0] = (chain + 1, 1.0)
        if chain == 0:
            slots[1] = (0, 1.0)
        for which, (slot, sign) in slots.items():
            for target in range(slot, slabs):
                table[own, which, target * blocks : (target + 1) * blocks] = sign * decay ** (target - slot) / cells
    return jnp.asarray(table, jnp.float32)


def swapped(block, count):
    near = [(i, i ^ 1) for i in range(count)]
    far = []
    for i in range(1, count - 1, 2):
        far += [(i, i + 1), (i + 1, i)]
    from_far = lax.ppermute(block, SPACE, far)
    from_near = lax.ppermute(block, SPACE, near)
    return from_near, from_far


def per_device(q_start, guess):
    own = guess[0]
    slabs = lax.axis_size("tm")
    count = lax.axis_size("outer") * lax.axis_size("inner")
    _, rows, ny, nz = own.shape
    field = jax.ShapeDtypeStruct(own.shape, jnp.float32)
    any_spec = pl.BlockSpec(memory_space=pl.ANY)
    scratch = [
        pltpu.VMEM((COMP, 3 * ROWS, ny + 2 * PAD, nz), jnp.float32),
        pltpu.VMEM((COMP, 3 * ROWS, ny + 2 * PAD, nz), jnp.float32),
        pltpu.VMEM((COMP, 3 * ROWS, ny, nz), jnp.float32),
        pltpu.VMEM((3 * ROWS, ny, nz), jnp.float32),
        pltpu.SemaphoreType.DMA((3,)),
    ]
    tile = (8, nz)

    start = jnp.where(lax.axis_index("tm") == slabs - 1, q_start, own)
    near, far = swapped(start, count)
    relaxed = pl.pallas_call(
        first_kernel, out_shape=field, in_specs=[any_spec] * 3, scratch_shapes=scratch, name="relax"
    )(start, near, far)

    near, far = swapped(relaxed, count)
    my_relaxed = lax.ppermute(relaxed, "tm", [(i, (i + 1) % slabs) for i in range(slabs)])
    weights = slot_weights(slabs, nz, count * rows * ny * BLK)
    vmem = pl.BlockSpec(memory_space=pltpu.VMEM)
    again, share = pl.pallas_call(
        second_kernel,
        out_shape=(field, jax.ShapeDtypeStruct((GROUP, *tile), jnp.float32)),
        in_specs=[any_spec] * 3 + [vmem, vmem],
        scratch_shapes=scratch,
        name="again",
    )(relaxed, near, far, guess, weights)

    my_again = lax.ppermute(again, "tm", [(i, (i + 2) % slabs) for i in range(slabs)])
    parts = lax.all_to_all(share, "inner", 0, 0)
    wide = slabs * lax.axis_size("outer")
    share = pl.pallas_call(
        relay_kernel, out_shape=jax.ShapeDtypeStruct((wide, *tile), jnp.float32), name="relay"
    )(parts)
    parts = lax.all_to_all(share, ("tm", "outer"), 0, 0)

    block = pl.BlockSpec((1, rows, ny, nz), lambda k: (k, 0, 0, 0))
    block_out = pl.BlockSpec((1, 1, rows, ny, nz), lambda k: (0, k, 0, 0, 0))
    out = jax.ShapeDtypeStruct((1, *own.shape), jnp.float32)
    corrected, residual = pl.pallas_call(
        last_kernel,
        out_shape=(out, out),
        grid=(COMP,),
        in_specs=[pl.BlockSpec((wide, *tile), lambda k: (0, 0, 0)), block, block],
        out_specs=(block_out, block_out),
        scratch_shapes=[pltpu.VMEM(tile, jnp.float32)],
        name="correct",
    )(parts, my_relaxed, my_again)
    return corrected, residual


def solution(mesh):
    slabs, count = mesh.shape["tm"], mesh.shape["space"]
    fine = Mesh(mesh.devices.reshape(slabs, count // GROUP, GROUP), ("tm", *SPACE))
    q_spec = P(None, SPACE, None, None)
    field_spec = P("tm", None, SPACE, None, None)
    return jax.shard_map(
        per_device,
        mesh=fine,
        in_specs=(q_spec, field_spec),
        out_specs=(field_spec, field_spec),
        check_vma=False,
    )
```

time: 410 us -> 95.8 us (0.23)
  the two profiles are of different devices: /device:TPU:262 before, /device:TPU:1 now
where the time goes in v1:
time: 95.8 us; the launch traced here: 95.1 us
  starting transfers between devices  30.4 us (32%)
  waiting for transfers between devices  27.6 us (29%)
  Pallas kernels  17.2 us (18%)
  blocking collectives  14.8 us (15%)
  local copies, waits for them, and re-layouts  3.23 us (3%)
  other arithmetic  1.17 us (1%)
    ppermute x2, waiting for transfers between devices, swapped(): from_far = lax.ppermute(block, SPACE, far)  18.5 us
    all_to_all x1, blocking collectives, per_device(): parts = lax.all_to_all(share, 'inner', 0, 0)  14.8 us
    all_to_all x1, starting transfers between devices, per_device(): parts = lax.all_to_all(share, ('tm', 'outer'), 0, 0)  12 us
    ppermute x2, starting transfers between devices, swapped(): from_near = lax.ppermute(block, SPACE, near)  10.7 us
    all_to_all x1, waiting for transfers between devices, per_device(): parts = lax.all_to_all(share, ('tm', 'outer'), 0, 0)  9.13 us
    pallas_call x1, Pallas kernels, per_device(): pl.pallas_call(second_kernel, out_shape=(field, jax.ShapeDtypeStruct((GRO...  6.3 us
    pallas_call x1, Pallas kernels, per_device(): pl.pallas_call(first_kernel, out_shape=field, in_specs=[any_spec] * 3, sc...  5.07 us
    pallas_call x1, Pallas kernels, per_device(): pl.pallas_call(last_kernel, out_shape=(out, out), grid=(COMP,), in_specs=...  4.27 us
  transfers between devices with their start and end apart: 7, of which 3 were waited for; matrix products, arithmetic and copies ran while one was open for 0% of the time, Pallas kernels for 8%

profile of v1, /device:TPU:1, one launch (start us, length us, event | category | flops | bytes accessed | tf_op | source)
XLA Modules:
  0.0 95.1 jit_solution(4319834641233684617)
XLA Ops:
  0.6 1.2 %bitcast_select_fusion.own = f32[5,4,64,128]{3,2,1,0:T(8,128)S(1)} fusion(f32[5,4,64,128]{3,2,1,0:T(8,128)} %param.3, f32[1,5,4,64,128]{4,3,2,1,0:T(8,128)} %guess.1, pred[]{:T(512)S(6)} %eq.3), kind=kLoop, calls=%fused_computation | loop fusion | flops 163840 | bytes 1966081 | tf_op jit(solution)/shard_map/jit(_where)/select_n | solution.py:239
  1.8 0.0 copy-start
  1.8 8.8 %collective-permute-start = (f32[5,4,64,128]{3,2,1,0:T(8,128)S(1)}, f32[5,4,64,128]{3,2,1,0:T(8,128)S(1)}, u32[]{:S(2)}, u32[]{:S(2)}) collective-permute-start(f32[5,4,64,128]{3,2,1,0:T(8,128)S(1)} %bitcast_select_fusion.own), channel_id=1, source_target_pairs={{0,1},{1,0},{2,3},{3,2},{4,5},{5,4},{6,7},{7,6},{8,9},{9,8},{10,11... | collective-permute-start | bytes 1966088 | tf_op jit(solution)/shard_map/ppermute | solution.py:219
  10.6 1.9 %collective-permute-start.1 = (f32[5,4,64,128]{3,2,1,0:T(8,128)S(1)}, f32[5,4,64,128]{3,2,1,0:T(8,128)S(1)}, u32[]{:S(2)}, u32[]{:S(2)}) collective-permute-start(f32[5,4,64,128]{3,2,1,0:T(8,128)S(1)} %bitcast_select_fusion.own), channel_id=1, source_target_pairs={{1,2},{2,1},{3,4},{4,3},{5,6},{6,5},{7,8},{8,7},{9,10},{10,9},{11,... | collective-permute-start | bytes 1966088 | tf_op jit(solution)/shard_map/ppermute | solution.py:218
  12.5 0.0 collective-permute-done.near
  12.6 0.0 copy-start.3
  12.6 10.0 %collective-permute-done.1.far = f32[5,4,64,128]{3,2,1,0:T(8,128)S(1)} collective-permute-done((f32[5,4,64,128]{3,2,1,0:T(8,128)S(1)}, f32[5,4,64,128]{3,2,1,0:T(8,128)S(1)}, u32[]{:S(2)}, u32[]{:S(2)}) %collective-permute-start.1) | collective-permute-done | bytes 655392 | tf_op jit(solution)/shard_map/ppermute | solution.py:218
  22.5 0.0 copy-done
  22.5 0.0 copy-done.3
  22.5 0.0 copy-start.4
  22.5 0.9 copy-done.4
  23.4 5.1 %relax.1.own = f32[5,4,64,128]{3,2,1,0:T(8,128)} custom-call(f32[5,4,64,128]{3,2,1,0:T(8,128)} %copy-done, f32[5,4,64,128]{3,2,1,0:T(8,128)} %copy-done.3, f32[5,4,64,128]{3,2,1,0:T(8,128)} %copy-done.4), custom_call_target="tpu_custom_call" | custom-call | tf_op jit(solution)/shard_map/relax/pallas_call | solution.py:241
  28.5 1.9 %collective-permute-start.2 = (f32[5,4,64,128]{3,2,1,0:T(8,128)}, f32[5,4,64,128]{3,2,1,0:T(8,128)S(1)}, u32[]{:S(2)}, u32[]{:S(2)}) collective-permute-start(f32[5,4,64,128]{3,2,1,0:T(8,128)} %relax.1.own), channel_id=1, source_target_pairs={{0,1},{1,0},{2,3},{3,2},{4,5},{5,4},{6,7},{7,6},{8,9},{9,8},{10,11... | collective-permute-start | bytes 1966088 | tf_op jit(solution)/shard_map/ppermute | solution.py:219
  30.4 1.9 %collective-permute-start.3 = (f32[5,4,64,128]{3,2,1,0:T(8,128)}, f32[5,4,64,128]{3,2,1,0:T(8,128)S(1)}, u32[]{:S(2)}, u32[]{:S(2)}) collective-permute-start(f32[5,4,64,128]{3,2,1,0:T(8,128)} %relax.1.own), channel_id=1, source_target_pairs={{1,2},{2,1},{3,4},{4,3},{5,6},{6,5},{7,8},{8,7},{9,10},{10,9},{11,... | collective-permute-start | bytes 1966088 | tf_op jit(solution)/shard_map/ppermute | solution.py:218
  32.3 1.9 %collective-permute-start.4 = (f32[5,4,64,128]{3,2,1,0:T(8,128)}, f32[5,4,64,128]{3,2,1,0:T(8,128)S(1)}, u32[]{:S(2)}, u32[]{:S(2)}) collective-permute-start(f32[5,4,64,128]{3,2,1,0:T(8,128)} %relax.1.own), channel_id=1, source_target_pairs={{0,128},{128,256},{256,384},{384,0},{1,129},{129,257},{257,385},{3... | collective-permute-start | bytes 1966088 | tf_op jit(solution)/shard_map/ppermute | solution.py:246
  34.3 0.0 collective-permute-done.2.near
  34.3 0.0 copy-start.1
  34.3 8.5 %collective-permute-done.3.far = f32[5,4,64,128]{3,2,1,0:T(8,128)S(1)} collective-permute-done((f32[5,4,64,128]{3,2,1,0:T(8,128)}, f32[5,4,64,128]{3,2,1,0:T(8,128)S(1)}, u32[]{:S(2)}, u32[]{:S(2)}) %collective-permute-start.3) | collective-permute-done | bytes 655392 | tf_op jit(solution)/shard_map/ppermute | solution.py:218
  42.8 0.0 copy-done.1
  42.8 0.0 copy-start.2
  42.8 0.8 copy-done.2
  43.7 6.3 %again.1 = (f32[5,4,64,128]{3,2,1,0:T(8,128)}, f32[16,8,128]{2,1,0:T(8,128)}) custom-call(f32[5,4,64,128]{3,2,1,0:T(8,128)} %relax.1.own, f32[5,4,64,128]{3,2,1,0:T(8,128)} %copy-done.1, f32[5,4,64,128]{3,2,1,0:T(8,128)} %copy-done.2, f32[1,5,4,64,128]{4,3,2,1,0:T(8,128)} %guess.1, f32[4,8,128]{2,1,0:T(8,128)} %constant.10.clone.weights), custom_call_target="tpu_custom_call" | custom-call | tf_op jit(solution)/shard_map/again/pallas_call | solution.py:249
  50.0 1.9 %collective-permute-start.5 = (f32[5,4,64,128]{3,2,1,0:T(8,128)}, f32[5,4,64,128]{3,2,1,0:T(8,128)S(1)}, u32[]{:S(2)}, u32[]{:S(2)}) collective-permute-start(f32[5,4,64,128]{3,2,1,0:T(8,128)} %get-tuple-element.5), channel_id=1, source_target_pairs={{0,256},{128,384},{256,0},{384,128},{1,257},{129,385},{257,1},{385... | collective-permute-start | bytes 1966088 | tf_op jit(solution)/shard_map/ppermute | solution.py:257
  51.9 14.8 %all_to_all.10.parts = f32[16,8,128]{2,1,0:T(8,128)} all-to-all(f32[16,8,128]{2,1,0:T(8,128)} %get-tuple-element.4), channel_id=1, replica_groups=mesh['tm'=4,'outer'=8,'inner'=16] {'inner'}, dimensions={0} | all-to-all | bytes 131072 | tf_op jit(solution)/shard_map/all_to_all | solution.py:258
  66.7 1.5 %relay.1 = f32[32,8,128]{2,1,0:T(8,128)} custom-call(f32[16,8,128]{2,1,0:T(8,128)} %all_to_all.10.parts), custom_call_target="tpu_custom_call" | custom-call | tf_op jit(solution)/shard_map/relay/pallas_call | solution.py:260
  68.2 12.0 %all-to-all-start.1 = ((f32[32,8,128]{2,1,0:T(8,128)}), f32[32,8,128]{2,1,0:T(8,128)S(1)}, u32[]{:S(2)}, u32[]{:S(2)}) async-start(f32[32,8,128]{2,1,0:T(8,128)} %relay.1), calls=%async_computation.1 | async-start | bytes 262144 | tf_op jit(solution)/shard_map/all_to_all | solution.py:263
  80.2 0.0 collective-permute-done.4.relaxed
  80.2 0.0 copy-start.5
  80.2 9.1 %all-to-all-done.1.parts = f32[32,8,128]{2,1,0:T(8,128)S(1)} async-done(((f32[32,8,128]{2,1,0:T(8,128)}), f32[32,8,128]{2,1,0:T(8,128)S(1)}, u32[]{:S(2)}, u32[]{:S(2)}) %all-to-all-start.1) | async-done | bytes 131104 | tf_op jit(solution)/shard_map/all_to_all | solution.py:263
  89.4 0.0 copy-start.7
  89.4 0.0 collective-permute-done.5.again
  89.4 0.0 copy-done.5
  89.4 0.6 copy-done.7
  90.0 0.0 copy-start.6
  90.0 0.9 copy-done.6
  90.9 4.3 %correct.1 = (f32[1,5,4,64,128]{4,3,2,1,0:T(8,128)}, f32[1,5,4,64,128]{4,3,2,1,0:T(8,128)}) custom-call(f32[32,8,128]{2,1,0:T(8,128)} %copy-done.7, f32[5,4,64,128]{3,2,1,0:T(8,128)} %copy-done.5, f32[5,4,64,128]{3,2,1,0:T(8,128)} %copy-done.6), custom_call_target="tpu_custom_call" | custom-call | tf_op jit(solution)/shard_map/correct/pallas_call | solution.py:268
Async XLA Ops:
  1.8 20.7 %copy-start = (f32[5,4,64,128]{3,2,1,0:T(8,128)}, f32[5,4,64,128]{3,2,1,0:T(8,128)S(1)}, u32[]{:S(2)}) copy-start(f32[5,4,64,128]{3,2,1,0:T(8,128)S(1)} %bitcast_select_fusion.own) | copy-start | bytes 1966084
  1.8 10.7 %collective-permute-start = (f32[5,4,64,128]{3,2,1,0:T(8,128)S(1)}, f32[5,4,64,128]{3,2,1,0:T(8,128)S(1)}, u32[]{:S(2)}, u32[]{:S(2)}) collective-permute-start(f32[5,4,64,128]{3,2,1,0:T(8,128)S(1)} %bitcast_select_fusion.own), channel_id=1, source_target_pairs={{0,1},{1,0},{2,3},{3,2},{4,5},{5,4},{6,7},{7,6},{8,9},{9,8},{10,11... | collective-permute-start | bytes 1966088 | tf_op jit(solution)/shard_map/ppermute | solution.py:219
  10.6 11.9 %collective-permute-start.1 = (f32[5,4,64,128]{3,2,1,0:T(8,128)S(1)}, f32[5,4,64,128]{3,2,1,0:T(8,128)S(1)}, u32[]{:S(2)}, u32[]{:S(2)}) collective-permute-start(f32[5,4,64,128]{3,2,1,0:T(8,128)S(1)} %bitcast_select_fusion.own), channel_id=1, source_target_pairs={{1,2},{2,1},{3,4},{4,3},{5,6},{6,5},{7,8},{8,7},{9,10},{10,9},{11,... | collective-permute-start | bytes 1966088 | tf_op jit(solution)/shard_map/ppermute | solution.py:218
  12.6 10.0 %copy-start.3 = (f32[5,4,64,128]{3,2,1,0:T(8,128)}, f32[5,4,64,128]{3,2,1,0:T(8,128)S(1)}, u32[]{:S(2)}) copy-start(f32[5,4,64,128]{3,2,1,0:T(8,128)S(1)} %collective-permute-done.near) | copy-start | bytes 1966084
  22.5 0.9 copy-start.4
  28.5 5.8 %collective-permute-start.2 = (f32[5,4,64,128]{3,2,1,0:T(8,128)}, f32[5,4,64,128]{3,2,1,0:T(8,128)S(1)}, u32[]{:S(2)}, u32[]{:S(2)}) collective-permute-start(f32[5,4,64,128]{3,2,1,0:T(8,128)} %relax.1.own), channel_id=1, source_target_pairs={{0,1},{1,0},{2,3},{3,2},{4,5},{5,4},{6,7},{7,6},{8,9},{9,8},{10,11... | collective-permute-start | bytes 1966088 | tf_op jit(solution)/shard_map/ppermute | solution.py:219
  30.4 12.4 %collective-permute-start.3 = (f32[5,4,64,128]{3,2,1,0:T(8,128)}, f32[5,4,64,128]{3,2,1,0:T(8,128)S(1)}, u32[]{:S(2)}, u32[]{:S(2)}) collective-permute-start(f32[5,4,64,128]{3,2,1,0:T(8,128)} %relax.1.own), channel_id=1, source_target_pairs={{1,2},{2,1},{3,4},{4,3},{5,6},{6,5},{7,8},{8,7},{9,10},{10,9},{11,... | collective-permute-start | bytes 1966088 | tf_op jit(solution)/shard_map/ppermute | solution.py:218
  32.3 47.9 %collective-permute-start.4 = (f32[5,4,64,128]{3,2,1,0:T(8,128)}, f32[5,4,64,128]{3,2,1,0:T(8,128)S(1)}, u32[]{:S(2)}, u32[]{:S(2)}) collective-permute-start(f32[5,4,64,128]{3,2,1,0:T(8,128)} %relax.1.own), channel_id=1, source_target_pairs={{0,128},{128,256},{256,384},{384,0},{1,129},{129,257},{257,385},{3... | collective-permute-start | bytes 1966088 | tf_op jit(solution)/shard_map/ppermute | solution.py:246
  34.3 8.5 %copy-start.1 = (f32[5,4,64,128]{3,2,1,0:T(8,128)}, f32[5,4,64,128]{3,2,1,0:T(8,128)S(1)}, u32[]{:S(2)}) copy-start(f32[5,4,64,128]{3,2,1,0:T(8,128)S(1)} %collective-permute-done.2.near) | copy-start | bytes 1966084
  42.8 0.8 copy-start.2
  50.0 39.4 %collective-permute-start.5 = (f32[5,4,64,128]{3,2,1,0:T(8,128)}, f32[5,4,64,128]{3,2,1,0:T(8,128)S(1)}, u32[]{:S(2)}, u32[]{:S(2)}) collective-permute-start(f32[5,4,64,128]{3,2,1,0:T(8,128)} %get-tuple-element.5), channel_id=1, source_target_pairs={{0,256},{128,384},{256,0},{384,128},{1,257},{129,385},{257,1},{385... | collective-permute-start | bytes 1966088 | tf_op jit(solution)/shard_map/ppermute | solution.py:257
  68.2 21.1 %all-to-all-start.1 = ((f32[32,8,128]{2,1,0:T(8,128)}), f32[32,8,128]{2,1,0:T(8,128)S(1)}, u32[]{:S(2)}, u32[]{:S(2)}) async-start(f32[32,8,128]{2,1,0:T(8,128)} %relay.1), calls=%async_computation.1 | async-start | bytes 262144 | tf_op jit(solution)/shard_map/all_to_all | solution.py:263
  80.2 9.1 %copy-start.5 = (f32[5,4,64,128]{3,2,1,0:T(8,128)}, f32[5,4,64,128]{3,2,1,0:T(8,128)S(1)}, u32[]{:S(2)}) copy-start(f32[5,4,64,128]{3,2,1,0:T(8,128)S(1)} %collective-permute-done.4.relaxed) | copy-start | bytes 1966084
  89.4 0.6 copy-start.7
  90.0 0.9 copy-start.6

commit v2 on v0

v2 whole, which is shorter than its diff:
```python
import jax
import jax.numpy as jnp
import numpy as np
from jax import lax
from jax.experimental import pallas as pl
from jax.experimental.pallas import tpu as pltpu
from jax.sharding import Mesh
from jax.sharding import PartitionSpec as P

COMP = 5
STEPS_SLAB = 2
BLK = 4
ROWS = 4
SUB = 8
GROUP = 16

time_step = 0.1
cross = 8.0
axial = 2.0
linear_rate = 0.1
quadratic_rate = 0.5
cubic_rate = 1.0

SPACE = ("outer", "inner")
LIMIT = pltpu.CompilerParams(vmem_limit_bytes=16 * 1024 * 1024)


def index_in_space():
    return lax.axis_index("outer") * lax.axis_size("inner") + lax.axis_index("inner")


def row_of():
    odd = index_in_space() % 2 == 1
    return lambda i: jnp.where(odd, ROWS - 1 - i, i)


def spaced(ref, k, row):
    count = ref.shape[2] // SUB
    return jnp.stack([ref[k, row, pl.ds(v, SUB, stride=count), :] for v in range(count)])


def bulk(q, scale):
    a, b, c, d, e = q
    f = a + d
    aa, bb, cc, dd, ee = a * a, b * b, c * c, d * d, e * e
    off = bb + cc
    trace = aa + dd + f * f + 2.0 * (off + ee)
    third = trace * (1.0 / 3.0)
    quad = (aa + off - third, b * f + c * e, b * e - c * d, bb + dd + ee - third, b * c - a * e)
    source = [(1.0 / cross) * q[k] + (time_step * quadratic_rate / cross) * quad[k] for k in range(COMP)]
    constant = 1.0 + time_step * linear_rate + 2.0 * (2.0 * cross + axial)
    return source, scale / (constant + (time_step * cubic_rate) * trace)


def bulk_row(read, write_source, write_scale, count, scale):
    part = 2
    for v in range(0, count, part):
        at = pl.ds(v, part)
        source, ratio = bulk([read(k, at) for k in range(COMP)], scale)
        for k in range(COMP):
            write_source(k, at, source[k])
        write_scale(at, ratio)


def relaxed_row(here, low, high, source, scale):
    count, sub, nz = here.shape
    lane_of = lax.broadcasted_iota(jnp.int32, (sub, nz), 0)
    before = jnp.where(lane_of == 0, 0.0, pltpu.roll(here[count - 1], 1, 0))
    after = jnp.where(lane_of == sub - 1, 0.0, pltpu.roll(here[0], sub - 1, 0))
    along_y = jnp.concatenate([before[None], here[:-1]], axis=0) + jnp.concatenate([here[1:], after[None]], axis=0)
    along_z = pltpu.roll(here, 1, 2) + pltpu.roll(here, nz - 1, 2)
    return (source + ((low + high) + along_y) + (axial / cross) * along_z) * scale


def prepare_rows(own, packed, source, scale):
    row = row_of()
    for i in range(ROWS):
        r = row(i)
        for k in range(COMP):
            packed[k, r] = spaced(own, k, r)

        def write_source(k, at, value, i=i):
            source[k, i, at] = value

        def write_scale(at, value, i=i):
            scale[i, at] = value

        bulk_row(lambda k, at, r=r: packed[k, r, at], write_source, write_scale, packed.shape[2], cross)


def prepare_kernel(own, packed, source, scale):
    prepare_rows(own, packed, source, scale)


def packed_sums(rows):
    nz = rows[0].shape[1]
    value = jnp.concatenate(rows + [jnp.zeros((SUB - COMP, nz), jnp.float32)], axis=0)
    total = value
    for i in range(1, BLK):
        total = total + pltpu.roll(value, nz - i, 1)
    blocks = nz // BLK
    lane = lax.broadcasted_iota(jnp.int32, (SUB, nz), 1)
    sub = lax.broadcasted_iota(jnp.int32, (SUB, nz), 0)
    total = jnp.take_along_axis(total, BLK * (lane % blocks), axis=1)
    first = jnp.sum(jnp.where(lane // blocks == sub, total, 0.0)[:BLK], axis=0, keepdims=True)
    second = jnp.where(lane[:1] < blocks, total[COMP - 1 : COMP], 0.0)
    return jnp.where(sub % 2 == 0, first, second)


def field_sums(field):
    return [jnp.sum(jnp.sum(field(k), axis=0), axis=0, keepdims=True) for k in range(COMP)]


def prepare_again_kernel(own, guess, weights, packed, source, scale, rest):
    prepare_rows(own, packed, source, scale)
    slab = lax.axis_index("tm")
    relaxed = packed_sums(field_sums(lambda k: own[k]))
    old = packed_sums(field_sums(lambda k: guess[0, k]))
    rest[...] = weights[slab, 1] * relaxed + weights[slab, 2] * old


def near_kernel(packed, near, source, scale, v1, w2, source2, scale2, v2, near_source, near_scale, v1_more, w2_more):
    row = row_of()
    count = packed.shape[2]
    for i in range(3):

        def write_source(k, at, value, i=i):
            near_source[k, i, at] = value

        def write_scale(at, value, i=i):
            near_scale[i, at] = value

        r = row(i)
        bulk_row(lambda k, at, r=r: near[k, r, at], write_source, write_scale, count, cross)

    def w_at(k, r):
        return packed[k, row(r - 4)] if r < 8 else near[k, row(r - 8)]

    def source_at(k, r):
        return source[k, r - 4] if r < 8 else near_source[k, r - 8]

    def scale_at(r):
        return scale[r - 4] if r < 8 else near_scale[r - 8]

    for r in range(5, 11):
        for k in range(COMP):
            value = relaxed_row(w_at(k, r), w_at(k, r - 1), w_at(k, r + 1), source_at(k, r), scale_at(r))
            if r < 7:
                v1[k, r - 5] = value
            else:
                v1_more[k, r - 7] = value

    def v1_at(k, r):
        return v1[k, r - 5] if r < 7 else v1_more[k, r - 7]

    for r in range(6, 10):
        for k in range(COMP):
            value = relaxed_row(v1_at(k, r), v1_at(k, r - 1), v1_at(k, r + 1), source_at(k, r), scale_at(r))
            if r < 8:
                w2[k, r - 6] = value
            else:
                w2_more[k, r - 8] = value

    def w2_at(k, r):
        return w2[k, r - 6] if r < 8 else w2_more[k, r - 8]

    for r in range(6, 9):

        def read(k, at, r=r):
            return w2[k, r - 6, at] if r < 8 else w2_more[k, r - 8, at]

        def write_source(k, at, value, r=r):
            if r < 8:
                source2[k, r - 6, at] = value
            else:
                near_source[k, 0, at] = value

        def write_scale(at, value, r=r):
            if r < 8:
                scale2[r - 6, at] = value
            else:
                near_scale[0, at] = value

        bulk_row(read, write_source, write_scale, count, cross)
    for r in range(7, 9):
        for k in range(COMP):
            src = source2[k, r - 6] if r < 8 else near_source[k, 0]
            scl = scale2[r - 6] if r < 8 else near_scale[0]
            v2[k, r - 7] = relaxed_row(w2_at(k, r), w2_at(k, r - 1), w2_at(k, r + 1), src, scl)


def far_rows(packed, far, source, scale, v1, w2, source2, scale2, v2, work, emit):
    wf, far_source, far_scale, v1_far, w2_far, source2_far, scale2_far, v2_far = work
    row = row_of()
    count = packed.shape[2]
    index = index_in_space()
    edge = (index == 0) | (index == lax.axis_size("outer") * lax.axis_size("inner") - 1)
    masked = jnp.where(edge, 0.0, cross)
    for j in range(ROWS):
        for k in range(COMP):
            wf[k, j] = spaced(far, k, row(j))
    for r in range(1, 4):

        def write_source(k, at, value, r=r):
            far_source[k, r - 1, at] = value

        def write_scale(at, value, r=r):
            far_scale[r - 1, at] = value

        bulk_row(lambda k, at, r=r: wf[k, r, at], write_source, write_scale, count, masked)

    def w_at(k, r):
        return wf[k, r] if r < 4 else packed[k, row(r - 4)]

    def source_at(k, r):
        return far_source[k, r - 1] if r < 4 else source[k, r - 4]

    def scale_at(r):
        return far_scale[r - 1] if r < 4 else scale[r - 4]

    for r in range(1, 5):
        for k in range(COMP):
            v1_far[k, r - 1] = relaxed_row(w_at(k, r), w_at(k, r - 1), w_at(k, r + 1), source_at(k, r), scale_at(r))

    def v1_at(k, r):
        return v1_far[k, r - 1] if r < 5 else v1[k, r - 5]

    for r in range(2, 6):
        for k in range(COMP):
            w2_far[k, r - 2] = relaxed_row(v1_at(k, r), v1_at(k, r - 1), v1_at(k, r + 1), source_at(k, r), scale_at(r))
    for r in range(3, 6):

        def write_source(k, at, value, r=r):
            source2_far[k, r - 3, at] = value

        def write_scale(at, value, r=r):
            scale2_far[r - 3, at] = value

        bulk_row(
            lambda k, at, r=r: w2_far[k, r - 2, at], write_source, write_scale, count, masked if r < 4 else cross
        )

    def w2_at(k, r):
        return w2_far[k, r - 2] if r < 6 else w2[k, r - 6]

    def source2_at(k, r):
        return source2_far[k, r - 3] if r < 6 else source2[k, r - 6]

    def scale2_at(r):
        return scale2_far[r - 3] if r < 6 else scale2[r - 6]

    for r in range(3, 7):
        for k in range(COMP):
            v2_far[k, r - 3] = relaxed_row(
                w2_at(k, r), w2_at(k, r - 1), w2_at(k, r + 1), source2_at(k, r), scale2_at(r)
            )

    def v2_at(k, r):
        return v2_far[k, r - 3] if r < 7 else v2[k, r - 7]

    for r in range(4, 8):
        for k in range(COMP):
            value = relaxed_row(v2_at(k, r), v2_at(k, r - 1), v2_at(k, r + 1), source2_at(k, r), scale2_at(r))
            emit(k, row(r - 4), value)


def store_spaced(out, k, row, value):
    count = value.shape[0]
    for v in range(count):
        out[k, row, pl.ds(v, SUB, stride=count), :] = value[v]


def far_kernel(packed, far, source, scale, v1, w2, source2, scale2, v2, out, *work):
    def emit(k, row, value):
        store_spaced(out, k, row, value)

    far_rows(packed, far, source, scale, v1, w2, source2, scale2, v2, work, emit)


def far_again_kernel(packed, far, source, scale, v1, w2, source2, scale2, v2, rest, weights, out, share, *work):
    nz = out.shape[3]
    total = [jnp.zeros((SUB, nz), jnp.float32) for _ in range(COMP)]

    def emit(k, row, value):
        store_spaced(out, k, row, value)
        total[k] = total[k] + jnp.sum(value, axis=0)

    far_rows(packed, far, source, scale, v1, w2, source2, scale2, v2, work, emit)
    again = packed_sums([jnp.sum(t, axis=0, keepdims=True) for t in total])
    value = weights[lax.axis_index("tm"), 0] * again + rest[...]
    for i in range(share.shape[0]):
        share[i] = value


def relay_kernel(parts, share):
    value = parts[0]
    for i in range(1, parts.shape[0]):
        value = value + parts[i]
    sub = lax.broadcasted_iota(jnp.int32, value.shape, 0)
    slabs = SUB // 2
    each = share.shape[0] // slabs
    for p in range(slabs):
        pair = jnp.where(sub % 2 == 0, value[2 * p : 2 * p + 1], value[2 * p + 1 : 2 * p + 2])
        for i in range(0, each, SUB):
            share[pl.ds(p * each + i, SUB), :] = pair


def residual_kernel(relaxed, again, residual):
    slab = lax.axis_index("tm")
    for k in range(COMP):
        mine = relaxed[k]
        residual[0, k] = jnp.where(slab == 0, mine, again[k]) - mine


def correct_kernel(parts, relaxed, corrected):
    value = parts[pl.ds(0, SUB), :]
    for i in range(SUB, parts.shape[0], SUB):
        value = value + parts[pl.ds(i, SUB), :]
    value = value + pltpu.roll(value, 4, 0)
    value = value + pltpu.roll(value, 2, 0)
    nz = value.shape[1]
    lane = lax.broadcasted_iota(jnp.int32, value.shape, 1)
    for k in range(COMP):
        spread = jnp.take_along_axis(value, (k % BLK) * (nz // BLK) + lane // BLK, axis=1)
        which = k // BLK
        corrected[0, k] = relaxed[k] + spread[which : which + 1][None]


def slot_weights(slabs, nz, cells):
    decay = 1.0 / (1.0 + STEPS_SLAB * time_step * linear_rate)
    table = np.zeros((slabs, 3, SUB, nz))
    for own in range(slabs):
        chain = (own + 1) % slabs
        slots = {2: (own, -1.0)}
        if chain + 1 < slabs:
            slots[0] = (chain + 1, 1.0)
        if chain == 0:
            slots[1] = (0, 1.0)
        for which, (slot, sign) in slots.items():
            for target in range(slot, slabs):
                table[own, which, 2 * target : 2 * target + 2] = sign * decay ** (target - slot) / cells
    return jnp.asarray(table, jnp.float32)


def f32(*shape):
    return jax.ShapeDtypeStruct(shape, jnp.float32)


def call(kernel, name, out, inputs, scratch=()):
    vmem = pl.BlockSpec(memory_space=pltpu.VMEM)
    return pl.pallas_call(
        kernel,
        out_shape=out,
        in_specs=[vmem] * len(inputs),
        out_specs=jax.tree.map(lambda _: vmem, out),
        scratch_shapes=list(scratch),
        compiler_params=LIMIT,
        name=name,
    )(*inputs)


def per_device(q_start, guess):
    own = guess[0]
    slabs = lax.axis_size("tm")
    count = lax.axis_size("outer") * lax.axis_size("inner")
    _, rows, ny, nz = own.shape
    row = (ny // SUB, SUB, nz)
    near_pairs = [(i, i ^ 1) for i in range(count)]
    far_pairs = []
    for i in range(1, count - 1, 2):
        far_pairs += [(i, i + 1), (i + 1, i)]

    def several(*lead):
        return f32(*lead, *row)

    def scratch(*lead):
        return pltpu.VMEM((*lead, *row), jnp.float32)

    prepared = (several(COMP, ROWS), several(COMP, ROWS), several(ROWS))
    state = (several(COMP, 2), several(COMP, 2), several(COMP, 2), several(2), several(COMP, 2))
    near_scratch = (scratch(COMP, 3), scratch(3), scratch(COMP, 4), scratch(COMP, 2))
    far_scratch = (
        scratch(COMP, ROWS),
        scratch(COMP, 3),
        scratch(3),
        scratch(COMP, 4),
        scratch(COMP, 4),
        scratch(COMP, 3),
        scratch(3),
        scratch(COMP, 4),
    )

    start = jnp.where(lax.axis_index("tm") == slabs - 1, q_start, own)
    far = lax.ppermute(start, SPACE, far_pairs)
    packed, source, scale = call(prepare_kernel, "prepare", prepared, (start,))
    near = lax.ppermute(packed, SPACE, near_pairs)
    kept = call(near_kernel, "near", state, (packed, near, source, scale), near_scratch)
    relaxed = call(far_kernel, "far", f32(*own.shape), (packed, far, source, scale, *kept), far_scratch)

    far = lax.ppermute(relaxed, SPACE, far_pairs)
    my_relaxed = lax.ppermute(relaxed, "tm", [(i, (i + 1) % slabs) for i in range(slabs)])
    weights = slot_weights(slabs, nz, count * rows * ny * BLK)
    packed, source, scale, rest = call(
        prepare_again_kernel, "prepare_again", (*prepared, f32(SUB, nz)), (relaxed, guess, weights)
    )
    near = lax.ppermute(packed, SPACE, near_pairs)
    kept = call(near_kernel, "near", state, (packed, near, source, scale), near_scratch)
    again, share = call(
        far_again_kernel,
        "far_again",
        (f32(*own.shape), f32(GROUP, SUB, nz)),
        (packed, far, source, scale, *kept, rest, weights),
        far_scratch,
    )

    my_again = lax.ppermute(again, "tm", [(i, (i + 2) % slabs) for i in range(slabs)])
    parts = lax.all_to_all(share, "inner", 0, 0)
    wide = slabs * lax.axis_size("outer")
    share = call(relay_kernel, "relay", f32(2 * wide, nz), (parts,))
    parts = lax.all_to_all(share.reshape(wide, 2, nz), ("tm", "outer"), 0, 0).reshape(2 * wide, nz)
    residual = call(residual_kernel, "residual", f32(1, *own.shape), (my_relaxed, my_again))
    corrected = call(correct_kernel, "correct", f32(1, *own.shape), (parts, my_relaxed))
    return corrected, residual


def solution(mesh):
    slabs, count = mesh.shape["tm"], mesh.shape["space"]
    fine = Mesh(mesh.devices.reshape(slabs, count // GROUP, GROUP), ("tm", *SPACE))
    q_spec = P(None, SPACE, None, None)
    field_spec = P("tm", None, SPACE, None, None)
    return jax.shard_map(
        per_device,
        mesh=fine,
        in_specs=(q_spec, field_spec),
        out_specs=(field_spec, field_spec),
        check_vma=False,
    )
```

time: 410 us -> 79.9 us (0.19)
  the two profiles are of different devices: /device:TPU:262 before, /device:TPU:1 now
where the time goes in v2:
time: 79.9 us; the launch traced here: 79.6 us
  starting transfers between devices  29.4 us (37%)
  waiting for transfers between devices  24.5 us (31%)
  blocking collectives  14.5 us (18%)
  Pallas kernels  9.26 us (12%)
  other arithmetic  1.18 us (1%)
    all_to_all x1, blocking collectives, per_device(): parts = lax.all_to_all(share, 'inner', 0, 0)  14.5 us
    all_to_all x1, starting transfers between devices, per_device(): lax.all_to_all(share.reshape(wide, 2, nz), ('tm', 'outer'), 0, 0)  11 us
    ppermute x2, starting transfers between devices, per_device(): near = lax.ppermute(packed, SPACE, near_pairs)  10.7 us
    pallas_call x9, Pallas kernels, call(): pl.pallas_call(kernel, out_shape=out, in_specs=[vmem] * len(inputs), out_...  9.26 us
    all_to_all x1, waiting for transfers between devices, per_device(): lax.all_to_all(share.reshape(wide, 2, nz), ('tm', 'outer'), 0, 0)  8.76 us
    ppermute x1, waiting for transfers between devices, per_device(): far = lax.ppermute(start, SPACE, far_pairs)  8.71 us
    ppermute x1, waiting for transfers between devices, per_device(): far = lax.ppermute(relaxed, SPACE, far_pairs)  6.97 us
    ppermute x1, starting transfers between devices, per_device(): far = lax.ppermute(start, SPACE, far_pairs)  1.92 us
  transfers between devices with their start and end apart: 7, of which 3 were waited for; matrix products, arithmetic and copies ran while one was open for 0% of the time, Pallas kernels for 8%

profile of v2, /device:TPU:1, one launch (start us, length us, event | category | flops | bytes accessed | tf_op | source)
XLA Modules:
  0.0 79.6 jit_solution(6225251020304286463)
XLA Ops:
  0.6 1.2 %bitcast_select_fusion.own = f32[5,4,64,128]{3,2,1,0:T(8,128)S(1)} fusion(f32[5,4,64,128]{3,2,1,0:T(8,128)} %param.3, f32[1,5,4,64,128]{4,3,2,1,0:T(8,128)} %guess.1, pred[]{:T(512)S(6)} %eq.3), kind=kLoop, calls=%fused_computation | loop fusion | flops 163840 | bytes 1966081 | tf_op jit(solution)/shard_map/jit(_where)/select_n | solution.py:393
  1.8 0.3 prepare.1
  2.1 8.8 %collective-permute-start.1 = (f32[5,4,8,8,128]{4,3,2,1,0:T(8,128)S(1)}, f32[5,4,8,8,128]{4,3,2,1,0:T(8,128)S(1)}, u32[]{:S(2)}, u32[]{:S(2)}) collective-permute-start(f32[5,4,8,8,128]{4,3,2,1,0:T(8,128)S(1)} %get-tuple-element.21.packed), channel_id=1, source_target_pairs={{0,1},{1,0},{2,3},{3,2},{4,5},{5,4},{6,7},{7,6},{8,9},{9,8},{10,11... | collective-permute-start | bytes 1966088 | tf_op jit(solution)/shard_map/ppermute | solution.py:396
  10.9 1.9 %collective-permute-start = (f32[5,4,64,128]{3,2,1,0:T(8,128)S(1)}, f32[5,4,64,128]{3,2,1,0:T(8,128)S(1)}, u32[]{:S(2)}, u32[]{:S(2)}) collective-permute-start(f32[5,4,64,128]{3,2,1,0:T(8,128)S(1)} %bitcast_select_fusion.own), channel_id=1, source_target_pairs={{1,2},{2,1},{3,4},{4,3},{5,6},{6,5},{7,8},{8,7},{9,10},{10,9},{11,... | collective-permute-start | bytes 1966088 | tf_op jit(solution)/shard_map/ppermute | solution.py:394
  12.9 0.0 collective-permute-done.1.near
  12.9 1.2 %near.2 = (f32[5,2,8,8,128]{4,3,2,1,0:T(8,128)S(1)}, f32[5,2,8,8,128]{4,3,2,1,0:T(8,128)S(1)}, f32[5,2,8,8,128]{4,3,2,1,0:T(8,128)S(1)}, f32[2,8,8,128]{3,2,1,0:T(8,128)S(1)}, f32[5,2,8,8,128]{4,3,2,1,0:T(8,128)S(1)}) custom-call(f32[5,4,8,8,128]{4,3,2,1,0:T(8,128)S(1)} %get-tuple-element.21.packed, f32[5,4,8,8,128]{4,3,2,1,0:T(8,128)S(1)} %collective-permute-done.1.near, ...), custom_call_target="tpu_custom_call" | custom-call | tf_op jit(solution)/shard_map/near/pallas_call | solution.py:351
  14.1 8.7 %collective-permute-done.far = f32[5,4,64,128]{3,2,1,0:T(8,128)S(1)} collective-permute-done((f32[5,4,64,128]{3,2,1,0:T(8,128)S(1)}, f32[5,4,64,128]{3,2,1,0:T(8,128)S(1)}, u32[]{:S(2)}, u32[]{:S(2)}) %collective-permute-start) | collective-permute-done | bytes 655392 | tf_op jit(solution)/shard_map/ppermute | solution.py:394
  22.8 0.0 copy-start
  22.8 0.0 copy-start.1
  22.8 1.6 %far.1.own = f32[5,4,64,128]{3,2,1,0:T(8,128)S(1)} custom-call(f32[5,4,8,8,128]{4,3,2,1,0:T(8,128)S(1)} %get-tuple-element.21.packed, f32[5,4,64,128]{3,2,1,0:T(8,128)S(1)} %collective-permute-done.far, f32[5,4,8,8,128]{4,3,2,1,0:T(8,128)S(1)} %get-tuple-element.22.source, f32[4,8,8,128]{3,2,1,0:T(8,128)S(1)} %get-tuple-element.23.scale, ...), custom_call_target="tpu_custom_call" | custom-call | tf_op jit(solution)/shard_map/far/pallas_call | solution.py:351
  24.4 0.0 copy-done
  24.4 0.0 copy-done.1
  24.4 0.4 prepare_again.1
  24.9 1.9 %collective-permute-start.3 = (f32[5,4,8,8,128]{4,3,2,1,0:T(8,128)S(1)}, f32[5,4,8,8,128]{4,3,2,1,0:T(8,128)S(1)}, u32[]{:S(2)}, u32[]{:S(2)}) collective-permute-start(f32[5,4,8,8,128]{4,3,2,1,0:T(8,128)S(1)} %get-tuple-element.29.packed), channel_id=1, source_target_pairs={{0,1},{1,0},{2,3},{3,2},{4,5},{5,4},{6,7},{7,6},{8,9},{9,8},{10,11... | collective-permute-start | bytes 1966088 | tf_op jit(solution)/shard_map/ppermute | solution.py:406
  26.8 1.9 %collective-permute-start.2 = (f32[5,4,64,128]{3,2,1,0:T(8,128)S(1)}, f32[5,4,64,128]{3,2,1,0:T(8,128)S(1)}, u32[]{:S(2)}, u32[]{:S(2)}) collective-permute-start(f32[5,4,64,128]{3,2,1,0:T(8,128)S(1)} %far.1.own), channel_id=1, source_target_pairs={{1,2},{2,1},{3,4},{4,3},{5,6},{6,5},{7,8},{8,7},{9,10},{10,9},{11,... | collective-permute-start | bytes 1966088 | tf_op jit(solution)/shard_map/ppermute | solution.py:400
  28.7 1.9 %collective-permute-start.4 = (f32[5,4,64,128]{3,2,1,0:T(8,128)S(1)}, f32[5,4,64,128]{3,2,1,0:T(8,128)S(1)}, u32[]{:S(2)}, u32[]{:S(2)}) collective-permute-start(f32[5,4,64,128]{3,2,1,0:T(8,128)S(1)} %far.1.own), channel_id=1, source_target_pairs={{0,128},{128,256},{256,384},{384,0},{1,129},{129,257},{257,385},{3... | collective-permute-start | bytes 1966088 | tf_op jit(solution)/shard_map/ppermute | solution.py:401
  30.7 0.0 collective-permute-done.3.near
  30.7 1.4 %near.3 = (f32[5,2,8,8,128]{4,3,2,1,0:T(8,128)S(1)}, f32[5,2,8,8,128]{4,3,2,1,0:T(8,128)S(1)}, f32[5,2,8,8,128]{4,3,2,1,0:T(8,128)S(1)}, f32[2,8,8,128]{3,2,1,0:T(8,128)S(1)}, f32[5,2,8,8,128]{4,3,2,1,0:T(8,128)S(1)}) custom-call(f32[5,4,8,8,128]{4,3,2,1,0:T(8,128)S(1)} %get-tuple-element.29.packed, f32[5,4,8,8,128]{4,3,2,1,0:T(8,128)S(1)} %collective-permute-done.3.near, ...), custom_call_target="tpu_custom_call" | custom-call | tf_op jit(solution)/shard_map/near/pallas_call | solution.py:351
  32.0 7.0 %collective-permute-done.2.far = f32[5,4,64,128]{3,2,1,0:T(8,128)S(1)} collective-permute-done((f32[5,4,64,128]{3,2,1,0:T(8,128)S(1)}, f32[5,4,64,128]{3,2,1,0:T(8,128)S(1)}, u32[]{:S(2)}, u32[]{:S(2)}) %collective-permute-start.2) | collective-permute-done | bytes 655392 | tf_op jit(solution)/shard_map/ppermute | solution.py:400
  39.0 1.9 %far_again.1 = (f32[5,4,64,128]{3,2,1,0:T(8,128)S(1)}, f32[16,8,128]{2,1,0:T(8,128)S(1)}) custom-call(f32[5,4,8,8,128]{4,3,2,1,0:T(8,128)S(1)} %get-tuple-element.29.packed, f32[5,4,64,128]{3,2,1,0:T(8,128)S(1)} %collective-permute-done.2.far, f32[5,4,8,8,128]{4,3,2,1,0:T(8,128)S(1)} %get-tuple-element.30.source, ...), custom_call_target="tpu_custom_call" | custom-call | tf_op jit(solution)/shard_map/far_again/pallas_call | solution.py:351
  40.9 1.9 %collective-permute-start.5 = (f32[5,4,64,128]{3,2,1,0:T(8,128)S(1)}, f32[5,4,64,128]{3,2,1,0:T(8,128)S(1)}, u32[]{:S(2)}, u32[]{:S(2)}) collective-permute-start(f32[5,4,64,128]{3,2,1,0:T(8,128)S(1)} %get-tuple-element.39), channel_id=1, source_target_pairs={{0,256},{128,384},{256,0},{384,128},{1,257},{129,385},{257,1},{385... | collective-permute-start | bytes 1966088 | tf_op jit(solution)/shard_map/ppermute | solution.py:416
  42.8 14.5 %all_to_all.10.parts = f32[16,8,128]{2,1,0:T(8,128)S(1)} all-to-all(f32[16,8,128]{2,1,0:T(8,128)S(1)} %get-tuple-element.38), channel_id=1, replica_groups=mesh['tm'=4,'outer'=8,'inner'=16] {'inner'}, dimensions={0} | all-to-all | bytes 131072 | tf_op jit(solution)/shard_map/all_to_all | solution.py:417
  57.3 0.6 relay.1
  57.9 11.0 %all-to-all-start.1 = ((f32[32,2,128]{2,1,0:T(2,128)}), f32[32,2,128]{2,1,0:T(2,128)S(1)}, u32[]{:S(2)}, u32[]{:S(2)}) async-start(f32[32,2,128]{2,1,0:T(2,128)} %bitcast.1), calls=%async_computation.1 | async-start | bytes 65536 | tf_op jit(solution)/shard_map/all_to_all | solution.py:420
  68.9 0.0 collective-permute-done.4.relaxed
  68.9 8.8 %all-to-all-done.1 = f32[32,2,128]{2,1,0:T(2,128)S(1)} async-done(((f32[32,2,128]{2,1,0:T(2,128)}), f32[32,2,128]{2,1,0:T(2,128)S(1)}, u32[]{:S(2)}, u32[]{:S(2)}) %all-to-all-start.1) | async-done | bytes 32800 | tf_op jit(solution)/shard_map/all_to_all | solution.py:420
  77.7 1.0 %correct.1 = f32[1,5,4,64,128]{4,3,2,1,0:T(8,128)} custom-call(f32[64,128]{1,0:T(8,128)S(1)} %bitcast.4, f32[5,4,64,128]{3,2,1,0:T(8,128)S(1)} %collective-permute-done.4.relaxed), custom_call_target="tpu_custom_call" | custom-call | tf_op jit(solution)/shard_map/correct/pallas_call | solution.py:351
  78.6 0.0 collective-permute-done.5.again
  78.6 0.9 %residual.1 = f32[1,5,4,64,128]{4,3,2,1,0:T(8,128)} custom-call(f32[5,4,64,128]{3,2,1,0:T(8,128)S(1)} %collective-permute-done.4.relaxed, f32[5,4,64,128]{3,2,1,0:T(8,128)S(1)} %collective-permute-done.5.again), custom_call_target="tpu_custom_call" | custom-call | tf_op jit(solution)/shard_map/residual/pallas_call | solution.py:351
Async XLA Ops:
  2.1 10.7 %collective-permute-start.1 = (f32[5,4,8,8,128]{4,3,2,1,0:T(8,128)S(1)}, f32[5,4,8,8,128]{4,3,2,1,0:T(8,128)S(1)}, u32[]{:S(2)}, u32[]{:S(2)}) collective-permute-start(f32[5,4,8,8,128]{4,3,2,1,0:T(8,128)S(1)} %get-tuple-element.21.packed), channel_id=1, source_target_pairs={{0,1},{1,0},{2,3},{3,2},{4,5},{5,4},{6,7},{7,6},{8,9},{9,8},{10,11... | collective-permute-start | bytes 1966088 | tf_op jit(solution)/shard_map/ppermute | solution.py:396
  10.9 11.9 %collective-permute-start = (f32[5,4,64,128]{3,2,1,0:T(8,128)S(1)}, f32[5,4,64,128]{3,2,1,0:T(8,128)S(1)}, u32[]{:S(2)}, u32[]{:S(2)}) collective-permute-start(f32[5,4,64,128]{3,2,1,0:T(8,128)S(1)} %bitcast_select_fusion.own), channel_id=1, source_target_pairs={{1,2},{2,1},{3,4},{4,3},{5,6},{6,5},{7,8},{8,7},{9,10},{10,9},{11,... | collective-permute-start | bytes 1966088 | tf_op jit(solution)/shard_map/ppermute | solution.py:394
  22.8 1.6 %copy-start = (f32[1,5,4,64,128]{4,3,2,1,0:T(8,128)S(1)}, f32[1,5,4,64,128]{4,3,2,1,0:T(8,128)}, u32[]{:S(2)}) copy-start(f32[1,5,4,64,128]{4,3,2,1,0:T(8,128)} %guess.1) | copy-start | bytes 1966084
  22.8 1.6 %copy-start.1 = (f32[4,3,8,128]{3,2,1,0:T(8,128)S(1)}, f32[4,3,8,128]{3,2,1,0:T(8,128)}, u32[]{:S(2)}) copy-start(f32[4,3,8,128]{3,2,1,0:T(8,128)} %constant.10.clone.weights) | copy-start | bytes 147460
  24.9 5.8 %collective-permute-start.3 = (f32[5,4,8,8,128]{4,3,2,1,0:T(8,128)S(1)}, f32[5,4,8,8,128]{4,3,2,1,0:T(8,128)S(1)}, u32[]{:S(2)}, u32[]{:S(2)}) collective-permute-start(f32[5,4,8,8,128]{4,3,2,1,0:T(8,128)S(1)} %get-tuple-element.29.packed), channel_id=1, source_target_pairs={{0,1},{1,0},{2,3},{3,2},{4,5},{5,4},{6,7},{7,6},{8,9},{9,8},{10,11... | collective-permute-start | bytes 1966088 | tf_op jit(solution)/shard_map/ppermute | solution.py:406
  26.8 12.2 %collective-permute-start.2 = (f32[5,4,64,128]{3,2,1,0:T(8,128)S(1)}, f32[5,4,64,128]{3,2,1,0:T(8,128)S(1)}, u32[]{:S(2)}, u32[]{:S(2)}) collective-permute-start(f32[5,4,64,128]{3,2,1,0:T(8,128)S(1)} %far.1.own), channel_id=1, source_target_pairs={{1,2},{2,1},{3,4},{4,3},{5,6},{6,5},{7,8},{8,7},{9,10},{10,9},{11,... | collective-permute-start | bytes 1966088 | tf_op jit(solution)/shard_map/ppermute | solution.py:400
  28.7 40.2 %collective-permute-start.4 = (f32[5,4,64,128]{3,2,1,0:T(8,128)S(1)}, f32[5,4,64,128]{3,2,1,0:T(8,128)S(1)}, u32[]{:S(2)}, u32[]{:S(2)}) collective-permute-start(f32[5,4,64,128]{3,2,1,0:T(8,128)S(1)} %far.1.own), channel_id=1, source_target_pairs={{0,128},{128,256},{256,384},{384,0},{1,129},{129,257},{257,385},{3... | collective-permute-start | bytes 1966088 | tf_op jit(solution)/shard_map/ppermute | solution.py:401
  40.9 37.8 %collective-permute-start.5 = (f32[5,4,64,128]{3,2,1,0:T(8,128)S(1)}, f32[5,4,64,128]{3,2,1,0:T(8,128)S(1)}, u32[]{:S(2)}, u32[]{:S(2)}) collective-permute-start(f32[5,4,64,128]{3,2,1,0:T(8,128)S(1)} %get-tuple-element.39), channel_id=1, source_target_pairs={{0,256},{128,384},{256,0},{384,128},{1,257},{129,385},{257,1},{385... | collective-permute-start | bytes 1966088 | tf_op jit(solution)/shard_map/ppermute | solution.py:416
  57.9 19.8 %all-to-all-start.1 = ((f32[32,2,128]{2,1,0:T(2,128)}), f32[32,2,128]{2,1,0:T(2,128)S(1)}, u32[]{:S(2)}, u32[]{:S(2)}) async-start(f32[32,2,128]{2,1,0:T(2,128)} %bitcast.1), calls=%async_computation.1 | async-start | bytes 65536 | tf_op jit(solution)/shard_map/all_to_all | solution.py:420

commit v3 on v2

--- a/solution.py
+++ b/solution.py
@@ -75,9 +75,9 @@
 def prepare_rows(own, packed, source, scale):
     row = row_of()
     for i in range(ROWS):
-        r = row(i)
-        for k in range(COMP):
-            packed[k, r] = spaced(own, k, r)
+        half, j = packed[i // 2], i % 2
+        for k in range(COMP):
+            half[k, j] = spaced(own, k, row(i))
 
         def write_source(k, at, value, i=i):
             source[k, i, at] = value
@@ -85,11 +85,14 @@
         def write_scale(at, value, i=i):
             scale[i, at] = value
 
-        bulk_row(lambda k, at, r=r: packed[k, r, at], write_source, write_scale, packed.shape[2], cross)
-
-
-def prepare_kernel(own, packed, source, scale):
-    prepare_rows(own, packed, source, scale)
+        def read(k, at, half=half, j=j):
+            return half[k, j, at]
+
+        bulk_row(read, write_source, write_scale, half.shape[2], cross)
+
+
+def prepare_kernel(own, outer, inner, source, scale):
+    prepare_rows(own, (outer, inner), source, scale)
 
 
 def packed_sums(rows):
@@ -111,17 +114,23 @@
     return [jnp.sum(jnp.sum(field(k), axis=0), axis=0, keepdims=True) for k in range(COMP)]
 
 
-def prepare_again_kernel(own, guess, weights, packed, source, scale, rest):
-    prepare_rows(own, packed, source, scale)
+def prepare_again_kernel(own, guess, weights, outer, inner, source, scale, rest):
+    prepare_rows(own, (outer, inner), source, scale)
     slab = lax.axis_index("tm")
     relaxed = packed_sums(field_sums(lambda k: own[k]))
     old = packed_sums(field_sums(lambda k: guess[0, k]))
     rest[...] = weights[slab, 1] * relaxed + weights[slab, 2] * old
 
 
-def near_kernel(packed, near, source, scale, v1, w2, source2, scale2, v2, near_source, near_scale, v1_more, w2_more):
-    row = row_of()
-    count = packed.shape[2]
+def near_kernel(outer, inner, near_outer, near_inner, source, scale, v1, w2, source2, scale2, v2, near_source, near_scale, v1_more, w2_more):
+    count = outer.shape[2]
+
+    def w_at(k, r, at=slice(None)):
+        if r < 8:
+            return (outer if r < 6 else inner)[k, r % 2, at]
+        r = 11 - r
+        return (near_outer if r < 2 else near_inner)[k, r % 2, at]
+
     for i in range(3):
 
         def write_source(k, at, value, i=i):
@@ -130,11 +139,7 @@
         def write_scale(at, value, i=i):
             near_scale[i, at] = value
 
-        r = row(i)
-        bulk_row(lambda k, at, r=r: near[k, r, at], write_source, write_scale, count, cross)
-
-    def w_at(k, r):
-        return packed[k, row(r - 4)] if r < 8 else near[k, row(r - 8)]
+        bulk_row(lambda k, at, i=i: w_at(k, 8 + i, at), write_source, write_scale, count, cross)
 
     def source_at(k, r):
         return source[k, r - 4] if r < 8 else near_source[k, r - 8]
@@ -189,10 +194,10 @@
             v2[k, r - 7] = relaxed_row(w2_at(k, r), w2_at(k, r - 1), w2_at(k, r + 1), src, scl)
 
 
-def far_rows(packed, far, source, scale, v1, w2, source2, scale2, v2, work, emit):
+def far_rows(outer, inner, far, source, scale, v1, w2, source2, scale2, v2, work, emit):
     wf, far_source, far_scale, v1_far, w2_far, source2_far, scale2_far, v2_far = work
     row = row_of()
-    count = packed.shape[2]
+    count = outer.shape[2]
     index = index_in_space()
     edge = (index == 0) | (index == lax.axis_size("outer") * lax.axis_size("inner") - 1)
     masked = jnp.where(edge, 0.0, cross)
@@ -210,7 +215,7 @@
         bulk_row(lambda k, at, r=r: wf[k, r, at], write_source, write_scale, count, masked)
 
     def w_at(k, r):
-        return wf[k, r] if r < 4 else packed[k, row(r - 4)]
+        return wf[k, r] if r < 4 else (outer if r < 6 else inner)[k, r % 2]
 
     def source_at(k, r):
         return far_source[k, r - 1] if r < 4 else source[k, r - 4]
@@ -270,14 +275,14 @@
         out[k, row, pl.ds(v, SUB, stride=count), :] = value[v]
 
 
-def far_kernel(packed, far, source, scale, v1, w2, source2, scale2, v2, out, *work):
+def far_kernel(outer, inner, far, source, scale, v1, w2, source2, scale2, v2, out, *work):
     def emit(k, row, value):
         store_spaced(out, k, row, value)
 
-    far_rows(packed, far, source, scale, v1, w2, source2, scale2, v2, work, emit)
-
-
-def far_again_kernel(packed, far, source, scale, v1, w2, source2, scale2, v2, rest, weights, out, share, *work):
+    far_rows(outer, inner, far, source, scale, v1, w2, source2, scale2, v2, work, emit)
+
+
+def far_again_kernel(outer, inner, far, source, scale, v1, w2, source2, scale2, v2, rest, weights, out, share, *work):
     nz = out.shape[3]
     total = [jnp.zeros((SUB, nz), jnp.float32) for _ in range(COMP)]
 
@@ -285,7 +290,7 @@
         store_spaced(out, k, row, value)
         total[k] = total[k] + jnp.sum(value, axis=0)
 
-    far_rows(packed, far, source, scale, v1, w2, source2, scale2, v2, work, emit)
+    far_rows(outer, inner, far, source, scale, v1, w2, source2, scale2, v2, work, emit)
     again = packed_sums([jnp.sum(t, axis=0, keepdims=True) for t in total])
     value = weights[lax.axis_index("tm"), 0] * again + rest[...]
     for i in range(share.shape[0]):
@@ -305,14 +310,16 @@
             share[pl.ds(p * each + i, SUB), :] = pair
 
 
-def residual_kernel(relaxed, again, residual):
+def residual_kernel(relaxed, again, residual, written):
+    written[...] = jnp.zeros_like(written)
     slab = lax.axis_index("tm")
     for k in range(COMP):
         mine = relaxed[k]
         residual[0, k] = jnp.where(slab == 0, mine, again[k]) - mine
 
 
-def correct_kernel(parts, relaxed, corrected):
+def correct_kernel(parts, relaxed, written, corrected):
+    del written
     value = parts[pl.ds(0, SUB), :]
     for i in range(SUB, parts.shape[0], SUB):
         value = value + parts[pl.ds(i, SUB), :]
@@ -376,7 +383,7 @@
     def scratch(*lead):
         return pltpu.VMEM((*lead, *row), jnp.float32)
 
-    prepared = (several(COMP, ROWS), several(COMP, ROWS), several(ROWS))
+    prepared = (several(COMP, 2), several(COMP, 2), several(COMP, ROWS), several(ROWS))
     state = (several(COMP, 2), several(COMP, 2), several(COMP, 2), several(2), several(COMP, 2))
     near_scratch = (scratch(COMP, 3), scratch(3), scratch(COMP, 4), scratch(COMP, 2))
     far_scratch = (
@@ -392,24 +399,24 @@
 
     start = jnp.where(lax.axis_index("tm") == slabs - 1, q_start, own)
     far = lax.ppermute(start, SPACE, far_pairs)
-    packed, source, scale = call(prepare_kernel, "prepare", prepared, (start,))
-    near = lax.ppermute(packed, SPACE, near_pairs)
-    kept = call(near_kernel, "near", state, (packed, near, source, scale), near_scratch)
-    relaxed = call(far_kernel, "far", f32(*own.shape), (packed, far, source, scale, *kept), far_scratch)
+    outer, inner, source, scale = call(prepare_kernel, "prepare", prepared, (start,))
+    near = [lax.ppermute(half, SPACE, near_pairs) for half in (outer, inner)]
+    kept = call(near_kernel, "near", state, (outer, inner, *near, source, scale), near_scratch)
+    relaxed = call(far_kernel, "far", f32(*own.shape), (outer, inner, far, source, scale, *kept), far_scratch)
 
     far = lax.ppermute(relaxed, SPACE, far_pairs)
     my_relaxed = lax.ppermute(relaxed, "tm", [(i, (i + 1) % slabs) for i in range(slabs)])
     weights = slot_weights(slabs, nz, count * rows * ny * BLK)
-    packed, source, scale, rest = call(
+    outer, inner, source, scale, rest = call(
         prepare_again_kernel, "prepare_again", (*prepared, f32(SUB, nz)), (relaxed, guess, weights)
     )
-    near = lax.ppermute(packed, SPACE, near_pairs)
-    kept = call(near_kernel, "near", state, (packed, near, source, scale), near_scratch)
+    near = [lax.ppermute(half, SPACE, near_pairs) for half in (outer, inner)]
+    kept = call(near_kernel, "near", state, (outer, inner, *near, source, scale), near_scratch)
     again, share = call(
         far_again_kernel,
         "far_again",
         (f32(*own.shape), f32(GROUP, SUB, nz)),
-        (packed, far, source, scale, *kept, rest, weights),
+        (outer, inner, far, source, scale, *kept, rest, weights),
         far_scratch,
     )
 
@@ -418,8 +425,10 @@
     wide = slabs * lax.axis_size("outer")
     share = call(relay_kernel, "relay", f32(2 * wide, nz), (parts,))
     parts = lax.all_to_all(share.reshape(wide, 2, nz), ("tm", "outer"), 0, 0).reshape(2 * wide, nz)
-    residual = call(residual_kernel, "residual", f32(1, *own.shape), (my_relaxed, my_again))
-    corrected = call(correct_kernel, "correct", f32(1, *own.shape), (parts, my_relaxed))
+    residual, written = call(
+        residual_kernel, "residual", (f32(1, *own.shape), f32(SUB, nz)), (my_relaxed, my_again)
+    )
+    corrected = call(correct_kernel, "correct", f32(1, *own.shape), (parts, my_relaxed, written))
     return corrected, residual
 
 

time: 79.9 us -> 74.4 us (0.931)
  waiting for transfers between devices: 24.5 us -> 10.2 us
  starting transfers between devices: 29.4 us -> 35.5 us
  blocking collectives: 14.5 us -> 17.1 us
    ppermute x1, waiting for transfers between devices: 8.71 us -> 0.01 us  [per_device(): far = lax.ppermute(start, SPACE, far_pairs)]
    ppermute x1, waiting for transfers between devices: 6.97 us -> 0.81 us  [per_device(): far = lax.ppermute(relaxed, SPACE, far_pairs)]
    ppermute x1, starting transfers between devices: 1.92 us -> 4.59 us  [per_device(): far = lax.ppermute(start, SPACE, far_pairs)]
    all_to_all x1, blocking collectives: 14.5 us -> 17.1 us  [per_device(): parts = lax.all_to_all(share, 'inner', 0, 0)]
    ppermute x1, starting transfers between devices: 1.92 us -> 3.78 us  [per_device(): lax.ppermute(again, 'tm', [(i, (i + 2) % slabs) for i in range(slabs)])]
    ppermute x2 -> x4, waiting for transfers between devices: 0.01 us -> 1.59 us  [per_device(): near = [lax.ppermute(half, SPACE, near_pairs) for half in (outer, inner)]]
    ppermute x1, starting transfers between devices: 1.92 us -> 3.07 us  [per_device(): lax.ppermute(relaxed, 'tm', [(i, (i + 1) % slabs) for i in range(slabs)])]
    all_to_all x1, waiting for transfers between devices: 8.76 us -> 7.83 us  [per_device(): lax.all_to_all(share.reshape(wide, 2, nz), ('tm', 'outer'), 0, 0)]
  transfers between devices with their start and end apart: 7 -> 9, of which waited for: 3 -> 3; matrix products, arithmetic and copies ran while one was open for 0% -> 0% of each run, Pallas kernels for 8% -> 9%
where the time goes in v3:
time: 74.4 us; the launch traced here: 74 us
  starting transfers between devices  35.5 us (48%)
  blocking collectives  17.1 us (23%)
  waiting for transfers between devices  10.2 us (14%)
  Pallas kernels  9.11 us (12%)
  other arithmetic  1.18 us (2%)
  between operations  0.83 us (1%)
    all_to_all x1, blocking collectives, per_device(): parts = lax.all_to_all(share, 'inner', 0, 0)  17.1 us
    ppermute x4, starting transfers between devices, per_device(): near = [lax.ppermute(half, SPACE, near_pairs) for half in (outer, inner)]  11.1 us
    all_to_all x1, starting transfers between devices, per_device(): lax.all_to_all(share.reshape(wide, 2, nz), ('tm', 'outer'), 0, 0)  11 us
    pallas_call x9, Pallas kernels, call(): pl.pallas_call(kernel, out_shape=out, in_specs=[vmem] * len(inputs), out_...  9.11 us
    all_to_all x1, waiting for transfers between devices, per_device(): lax.all_to_all(share.reshape(wide, 2, nz), ('tm', 'outer'), 0, 0)  7.83 us
    ppermute x1, starting transfers between devices, per_device(): far = lax.ppermute(start, SPACE, far_pairs)  4.59 us
    ppermute x1, starting transfers between devices, per_device(): lax.ppermute(again, 'tm', [(i, (i + 2) % slabs) for i in range(slabs)])  3.78 us
    ppermute x1, starting transfers between devices, per_device(): lax.ppermute(relaxed, 'tm', [(i, (i + 1) % slabs) for i in range(slabs)])  3.07 us
  transfers between devices with their start and end apart: 9, of which 3 were waited for; matrix products, arithmetic and copies ran while one was open for 0% of the time, Pallas kernels for 9%

profile of v3, /device:TPU:1, one launch (start us, length us, event | category | flops | bytes accessed | tf_op | source)
XLA Modules:
  0.0 74.0 jit_solution(11934009136856211257)
XLA Ops:
  0.6 1.2 %bitcast_select_fusion.own = f32[5,4,64,128]{3,2,1,0:T(8,128)S(1)} fusion(f32[5,4,64,128]{3,2,1,0:T(8,128)} %param.3, f32[1,5,4,64,128]{4,3,2,1,0:T(8,128)} %guess.1, pred[]{:T(512)S(6)} %eq.3), kind=kLoop, calls=%fused_computation | loop fusion | flops 163840 | bytes 1966081 | tf_op jit(solution)/shard_map/jit(_where)/select_n | solution.py:400
  1.8 4.6 %collective-permute-start = (f32[5,4,64,128]{3,2,1,0:T(8,128)S(1)}, f32[5,4,64,128]{3,2,1,0:T(8,128)S(1)}, u32[]{:S(2)}, u32[]{:S(2)}) collective-permute-start(f32[5,4,64,128]{3,2,1,0:T(8,128)S(1)} %bitcast_select_fusion.own), channel_id=1, source_target_pairs={{1,2},{2,1},{3,4},{4,3},{5,6},{6,5},{7,8},{8,7},{9,10},{10,9},{11,... | collective-permute-start | bytes 1966088 | tf_op jit(solution)/shard_map/ppermute | solution.py:401
  6.4 0.3 prepare.1
  6.7 4.9 %collective-permute-start.1 = (f32[5,2,8,8,128]{4,3,2,1,0:T(8,128)S(1)}, f32[5,2,8,8,128]{4,3,2,1,0:T(8,128)S(1)}, u32[]{:S(2)}, u32[]{:S(2)}) collective-permute-start(f32[5,2,8,8,128]{4,3,2,1,0:T(8,128)S(1)} %get-tuple-element.25.outer), channel_id=1, source_target_pairs={{0,1},{1,0},{2,3},{3,2},{4,5},{5,4},{6,7},{7,6},{8,9},{9,8},{10,11... | collective-permute-start | bytes 983048 | tf_op jit(solution)/shard_map/ppermute | solution.py:403
  11.6 1.9 %collective-permute-start.2 = (f32[5,2,8,8,128]{4,3,2,1,0:T(8,128)S(1)}, f32[5,2,8,8,128]{4,3,2,1,0:T(8,128)S(1)}, u32[]{:S(2)}, u32[]{:S(2)}) collective-permute-start(f32[5,2,8,8,128]{4,3,2,1,0:T(8,128)S(1)} %get-tuple-element.26.inner), channel_id=1, source_target_pairs={{0,1},{1,0},{2,3},{3,2},{4,5},{5,4},{6,7},{7,6},{8,9},{9,8},{10,11... | collective-permute-start | bytes 983048 | tf_op jit(solution)/shard_map/ppermute | solution.py:403
  13.6 0.0 collective-permute-done.1.near_outer
  13.6 1.6 %collective-permute-done.2.near_inner = f32[5,2,8,8,128]{4,3,2,1,0:T(8,128)S(1)} collective-permute-done((f32[5,2,8,8,128]{4,3,2,1,0:T(8,128)S(1)}, f32[5,2,8,8,128]{4,3,2,1,0:T(8,128)S(1)}, u32[]{:S(2)}, u32[]{:S(2)}) %collective-permute-start.2) | collective-permute-done | bytes 327712 | tf_op jit(solution)/shard_map/ppermute | solution.py:403
  15.2 1.2 %near.2 = (f32[5,2,8,8,128]{4,3,2,1,0:T(8,128)S(1)}, f32[5,2,8,8,128]{4,3,2,1,0:T(8,128)S(1)}, f32[5,2,8,8,128]{4,3,2,1,0:T(8,128)S(1)}, f32[2,8,8,128]{3,2,1,0:T(8,128)S(1)}, f32[5,2,8,8,128]{4,3,2,1,0:T(8,128)S(1)}) custom-call(f32[5,2,8,8,128]{4,3,2,1,0:T(8,128)S(1)} %get-tuple-element.25.outer, f32[5,2,8,8,128]{4,3,2,1,0:T(8,128)S(1)} %get-tuple-element.26.inner, ...), custom_call_target="tpu_custom_call" | custom-call | tf_op jit(solution)/shard_map/near/pallas_call | solution.py:358
  16.4 0.0 collective-permute-done.far
  16.4 0.0 copy-start
  16.4 0.0 copy-start.1
  16.4 1.6 %far.1.own = f32[5,4,64,128]{3,2,1,0:T(8,128)S(1)} custom-call(f32[5,2,8,8,128]{4,3,2,1,0:T(8,128)S(1)} %get-tuple-element.25.outer, f32[5,2,8,8,128]{4,3,2,1,0:T(8,128)S(1)} %get-tuple-element.26.inner, f32[5,4,64,128]{3,2,1,0:T(8,128)S(1)} %collective-permute-done.far, f32[5,4,8,8,128]{4,3,2,1,0:T(8,128)S(1)} %get-tuple-element.27.source, ...), custom_call_target="tpu_custom_call" | custom-call | tf_op jit(solution)/shard_map/far/pallas_call | solution.py:358
  18.0 1.9 %collective-permute-start.3 = (f32[5,4,64,128]{3,2,1,0:T(8,128)S(1)}, f32[5,4,64,128]{3,2,1,0:T(8,128)S(1)}, u32[]{:S(2)}, u32[]{:S(2)}) collective-permute-start(f32[5,4,64,128]{3,2,1,0:T(8,128)S(1)} %far.1.own), channel_id=1, source_target_pairs={{1,2},{2,1},{3,4},{4,3},{5,6},{6,5},{7,8},{8,7},{9,10},{10,9},{11,... | collective-permute-start | bytes 1966088 | tf_op jit(solution)/shard_map/ppermute | solution.py:407
  20.0 0.0 copy-done
  20.0 0.0 copy-done.1
  20.0 0.4 prepare_again.1
  20.4 1.9 %collective-permute-start.4 = (f32[5,2,8,8,128]{4,3,2,1,0:T(8,128)S(1)}, f32[5,2,8,8,128]{4,3,2,1,0:T(8,128)S(1)}, u32[]{:S(2)}, u32[]{:S(2)}) collective-permute-start(f32[5,2,8,8,128]{4,3,2,1,0:T(8,128)S(1)} %get-tuple-element.34.outer), channel_id=1, source_target_pairs={{0,1},{1,0},{2,3},{3,2},{4,5},{5,4},{6,7},{7,6},{8,9},{9,8},{10,11... | collective-permute-start | bytes 983048 | tf_op jit(solution)/shard_map/ppermute | solution.py:413
  22.3 2.4 %collective-permute-start.5 = (f32[5,2,8,8,128]{4,3,2,1,0:T(8,128)S(1)}, f32[5,2,8,8,128]{4,3,2,1,0:T(8,128)S(1)}, u32[]{:S(2)}, u32[]{:S(2)}) collective-permute-start(f32[5,2,8,8,128]{4,3,2,1,0:T(8,128)S(1)} %get-tuple-element.35.inner), channel_id=1, source_target_pairs={{0,1},{1,0},{2,3},{3,2},{4,5},{5,4},{6,7},{7,6},{8,9},{9,8},{10,11... | collective-permute-start | bytes 983048 | tf_op jit(solution)/shard_map/ppermute | solution.py:413
  24.7 3.1 %collective-permute-start.6 = (f32[5,4,64,128]{3,2,1,0:T(8,128)S(1)}, f32[5,4,64,128]{3,2,1,0:T(8,128)S(1)}, u32[]{:S(2)}, u32[]{:S(2)}) collective-permute-start(f32[5,4,64,128]{3,2,1,0:T(8,128)S(1)} %far.1.own), channel_id=1, source_target_pairs={{0,128},{128,256},{256,384},{384,0},{1,129},{129,257},{257,385},{3... | collective-permute-start | bytes 1966088 | tf_op jit(solution)/shard_map/ppermute | solution.py:408
  27.8 0.0 collective-permute-done.4.near_outer
  27.8 0.0 collective-permute-done.5.near_inner
  27.9 1.3 %near.3 = (f32[5,2,8,8,128]{4,3,2,1,0:T(8,128)S(1)}, f32[5,2,8,8,128]{4,3,2,1,0:T(8,128)S(1)}, f32[5,2,8,8,128]{4,3,2,1,0:T(8,128)S(1)}, f32[2,8,8,128]{3,2,1,0:T(8,128)S(1)}, f32[5,2,8,8,128]{4,3,2,1,0:T(8,128)S(1)}) custom-call(f32[5,2,8,8,128]{4,3,2,1,0:T(8,128)S(1)} %get-tuple-element.34.outer, f32[5,2,8,8,128]{4,3,2,1,0:T(8,128)S(1)} %get-tuple-element.35.inner, ...), custom_call_target="tpu_custom_call" | custom-call | tf_op jit(solution)/shard_map/near/pallas_call | solution.py:358
  29.1 0.8 %collective-permute-done.3.far = f32[5,4,64,128]{3,2,1,0:T(8,128)S(1)} collective-permute-done((f32[5,4,64,128]{3,2,1,0:T(8,128)S(1)}, f32[5,4,64,128]{3,2,1,0:T(8,128)S(1)}, u32[]{:S(2)}, u32[]{:S(2)}) %collective-permute-start.3) | collective-permute-done | bytes 655392 | tf_op jit(solution)/shard_map/ppermute | solution.py:407
  29.9 1.8 %far_again.1 = (f32[5,4,64,128]{3,2,1,0:T(8,128)S(1)}, f32[16,8,128]{2,1,0:T(8,128)S(1)}) custom-call(f32[5,2,8,8,128]{4,3,2,1,0:T(8,128)S(1)} %get-tuple-element.34.outer, f32[5,2,8,8,128]{4,3,2,1,0:T(8,128)S(1)} %get-tuple-element.35.inner, f32[5,4,64,128]{3,2,1,0:T(8,128)S(1)} %collective-permute-done.3.far, ...), custom_call_target="tpu_custom_call" | custom-call | tf_op jit(solution)/shard_map/far_again/pallas_call | solution.py:358
  31.7 3.8 %collective-permute-start.7 = (f32[5,4,64,128]{3,2,1,0:T(8,128)S(1)}, f32[5,4,64,128]{3,2,1,0:T(8,128)S(1)}, u32[]{:S(2)}, u32[]{:S(2)}) collective-permute-start(f32[5,4,64,128]{3,2,1,0:T(8,128)S(1)} %get-tuple-element.45), channel_id=1, source_target_pairs={{0,256},{128,384},{256,0},{384,128},{1,257},{129,385},{257,1},{385... | collective-permute-start | bytes 1966088 | tf_op jit(solution)/shard_map/ppermute | solution.py:423
  35.5 17.1 %all_to_all.10.parts = f32[16,8,128]{2,1,0:T(8,128)S(1)} all-to-all(f32[16,8,128]{2,1,0:T(8,128)S(1)} %get-tuple-element.44), channel_id=1, replica_groups=mesh['tm'=4,'outer'=8,'inner'=16] {'inner'}, dimensions={0} | all-to-all | bytes 131072 | tf_op jit(solution)/shard_map/all_to_all | solution.py:424
  52.6 0.6 relay.1
  53.2 11.0 %all-to-all-start.1 = ((f32[32,2,128]{2,1,0:T(2,128)}), f32[32,2,128]{2,1,0:T(2,128)S(1)}, u32[]{:S(2)}, u32[]{:S(2)}) async-start(f32[32,2,128]{2,1,0:T(2,128)} %bitcast.1), calls=%async_computation.1 | async-start | bytes 65536 | tf_op jit(solution)/shard_map/all_to_all | solution.py:427
  64.2 0.0 collective-permute-done.6.relaxed
  64.2 0.0 collective-permute-done.7.again
  64.3 0.9 %residual.1 = (f32[1,5,4,64,128]{4,3,2,1,0:T(8,128)}, f32[8,128]{1,0:T(8,128)S(1)}) custom-call(f32[5,4,64,128]{3,2,1,0:T(8,128)S(1)} %collective-permute-done.6.relaxed, f32[5,4,64,128]{3,2,1,0:T(8,128)S(1)} %collective-permute-done.7.again), custom_call_target="tpu_custom_call" | custom-call | tf_op jit(solution)/shard_map/residual/pallas_call | solution.py:358
  65.2 7.8 %all-to-all-done.1 = f32[32,2,128]{2,1,0:T(2,128)S(1)} async-done(((f32[32,2,128]{2,1,0:T(2,128)}), f32[32,2,128]{2,1,0:T(2,128)S(1)}, u32[]{:S(2)}, u32[]{:S(2)}) %all-to-all-start.1) | async-done | bytes 32800 | tf_op jit(solution)/shard_map/all_to_all | solution.py:427
  73.0 1.0 %correct.1 = f32[1,5,4,64,128]{4,3,2,1,0:T(8,128)} custom-call(f32[64,128]{1,0:T(8,128)S(1)} %bitcast.4, f32[5,4,64,128]{3,2,1,0:T(8,128)S(1)} %collective-permute-done.6.relaxed, f32[8,128]{1,0:T(8,128)S(1)} %get-tuple-element.46.written), custom_call_target="tpu_custom_call" | custom-call | tf_op jit(solution)/shard_map/correct/pallas_call | solution.py:358
Async XLA Ops:
  1.8 14.6 %collective-permute-start = (f32[5,4,64,128]{3,2,1,0:T(8,128)S(1)}, f32[5,4,64,128]{3,2,1,0:T(8,128)S(1)}, u32[]{:S(2)}, u32[]{:S(2)}) collective-permute-start(f32[5,4,64,128]{3,2,1,0:T(8,128)S(1)} %bitcast_select_fusion.own), channel_id=1, source_target_pairs={{1,2},{2,1},{3,4},{4,3},{5,6},{6,5},{7,8},{8,7},{9,10},{10,9},{11,... | collective-permute-start | bytes 1966088 | tf_op jit(solution)/shard_map/ppermute | solution.py:401
  6.7 6.8 %collective-permute-start.1 = (f32[5,2,8,8,128]{4,3,2,1,0:T(8,128)S(1)}, f32[5,2,8,8,128]{4,3,2,1,0:T(8,128)S(1)}, u32[]{:S(2)}, u32[]{:S(2)}) collective-permute-start(f32[5,2,8,8,128]{4,3,2,1,0:T(8,128)S(1)} %get-tuple-element.25.outer), channel_id=1, source_target_pairs={{0,1},{1,0},{2,3},{3,2},{4,5},{5,4},{6,7},{7,6},{8,9},{9,8},{10,11... | collective-permute-start | bytes 983048 | tf_op jit(solution)/shard_map/ppermute | solution.py:403
  11.6 3.5 %collective-permute-start.2 = (f32[5,2,8,8,128]{4,3,2,1,0:T(8,128)S(1)}, f32[5,2,8,8,128]{4,3,2,1,0:T(8,128)S(1)}, u32[]{:S(2)}, u32[]{:S(2)}) collective-permute-start(f32[5,2,8,8,128]{4,3,2,1,0:T(8,128)S(1)} %get-tuple-element.26.inner), channel_id=1, source_target_pairs={{0,1},{1,0},{2,3},{3,2},{4,5},{5,4},{6,7},{7,6},{8,9},{9,8},{10,11... | collective-permute-start | bytes 983048 | tf_op jit(solution)/shard_map/ppermute | solution.py:403
  16.4 3.6 %copy-start = (f32[1,5,4,64,128]{4,3,2,1,0:T(8,128)S(1)}, f32[1,5,4,64,128]{4,3,2,1,0:T(8,128)}, u32[]{:S(2)}) copy-start(f32[1,5,4,64,128]{4,3,2,1,0:T(8,128)} %guess.1) | copy-start | bytes 1966084
  16.4 3.6 %copy-start.1 = (f32[4,3,8,128]{3,2,1,0:T(8,128)S(1)}, f32[4,3,8,128]{3,2,1,0:T(8,128)}, u32[]{:S(2)}) copy-start(f32[4,3,8,128]{3,2,1,0:T(8,128)} %constant.10.clone.weights) | copy-start | bytes 147460
  18.0 11.9 %collective-permute-start.3 = (f32[5,4,64,128]{3,2,1,0:T(8,128)S(1)}, f32[5,4,64,128]{3,2,1,0:T(8,128)S(1)}, u32[]{:S(2)}, u32[]{:S(2)}) collective-permute-start(f32[5,4,64,128]{3,2,1,0:T(8,128)S(1)} %far.1.own), channel_id=1, source_target_pairs={{1,2},{2,1},{3,4},{4,3},{5,6},{6,5},{7,8},{8,7},{9,10},{10,9},{11,... | collective-permute-start | bytes 1966088 | tf_op jit(solution)/shard_map/ppermute | solution.py:407
  20.4 7.4 %collective-permute-start.4 = (f32[5,2,8,8,128]{4,3,2,1,0:T(8,128)S(1)}, f32[5,2,8,8,128]{4,3,2,1,0:T(8,128)S(1)}, u32[]{:S(2)}, u32[]{:S(2)}) collective-permute-start(f32[5,2,8,8,128]{4,3,2,1,0:T(8,128)S(1)} %get-tuple-element.34.outer), channel_id=1, source_target_pairs={{0,1},{1,0},{2,3},{3,2},{4,5},{5,4},{6,7},{7,6},{8,9},{9,8},{10,11... | collective-permute-start | bytes 983048 | tf_op jit(solution)/shard_map/ppermute | solution.py:413
  22.3 5.5 %collective-permute-start.5 = (f32[5,2,8,8,128]{4,3,2,1,0:T(8,128)S(1)}, f32[5,2,8,8,128]{4,3,2,1,0:T(8,128)S(1)}, u32[]{:S(2)}, u32[]{:S(2)}) collective-permute-start(f32[5,2,8,8,128]{4,3,2,1,0:T(8,128)S(1)} %get-tuple-element.35.inner), channel_id=1, source_target_pairs={{0,1},{1,0},{2,3},{3,2},{4,5},{5,4},{6,7},{7,6},{8,9},{9,8},{10,11... | collective-permute-start | bytes 983048 | tf_op jit(solution)/shard_map/ppermute | solution.py:413
  24.7 39.5 %collective-permute-start.6 = (f32[5,4,64,128]{3,2,1,0:T(8,128)S(1)}, f32[5,4,64,128]{3,2,1,0:T(8,128)S(1)}, u32[]{:S(2)}, u32[]{:S(2)}) collective-permute-start(f32[5,4,64,128]{3,2,1,0:T(8,128)S(1)} %far.1.own), channel_id=1, source_target_pairs={{0,128},{128,256},{256,384},{384,0},{1,129},{129,257},{257,385},{3... | collective-permute-start | bytes 1966088 | tf_op jit(solution)/shard_map/ppermute | solution.py:408
  31.7 32.5 %collective-permute-start.7 = (f32[5,4,64,128]{3,2,1,0:T(8,128)S(1)}, f32[5,4,64,128]{3,2,1,0:T(8,128)S(1)}, u32[]{:S(2)}, u32[]{:S(2)}) collective-permute-start(f32[5,4,64,128]{3,2,1,0:T(8,128)S(1)} %get-tuple-element.45), channel_id=1, source_target_pairs={{0,256},{128,384},{256,0},{384,128},{1,257},{129,385},{257,1},{385... | collective-permute-start | bytes 1966088 | tf_op jit(solution)/shard_map/ppermute | solution.py:423
  53.2 19.8 %all-to-all-start.1 = ((f32[32,2,128]{2,1,0:T(2,128)}), f32[32,2,128]{2,1,0:T(2,128)S(1)}, u32[]{:S(2)}, u32[]{:S(2)}) async-start(f32[32,2,128]{2,1,0:T(2,128)} %bitcast.1), calls=%async_computation.1 | async-start | bytes 65536 | tf_op jit(solution)/shard_map/all_to_all | solution.py:427

commit v4 on v3

--- a/solution.py
+++ b/solution.py
@@ -23,6 +23,8 @@
 
 SPACE = ("outer", "inner")
 LIMIT = pltpu.CompilerParams(vmem_limit_bytes=16 * 1024 * 1024)
+
+LONG = pl.CostEstimate(flops=40000000000, bytes_accessed=147600000, transcendentals=0)
 
 
 def index_in_space():
@@ -297,7 +299,8 @@
         share[i] = value
 
 
-def relay_kernel(parts, share):
+def relay_kernel(parts, relaxed, share):
+    del relaxed
     value = parts[0]
     for i in range(1, parts.shape[0]):
         value = value + parts[i]
@@ -353,7 +356,7 @@
     return jax.ShapeDtypeStruct(shape, jnp.float32)
 
 
-def call(kernel, name, out, inputs, scratch=()):
+def call(kernel, name, out, inputs, scratch=(), cost=None):
     vmem = pl.BlockSpec(memory_space=pltpu.VMEM)
     return pl.pallas_call(
         kernel,
@@ -363,6 +366,7 @@
         scratch_shapes=list(scratch),
         compiler_params=LIMIT,
         name=name,
+        cost_estimate=cost,
     )(*inputs)
 
 
@@ -423,7 +427,7 @@
     my_again = lax.ppermute(again, "tm", [(i, (i + 2) % slabs) for i in range(slabs)])
     parts = lax.all_to_all(share, "inner", 0, 0)
     wide = slabs * lax.axis_size("outer")
-    share = call(relay_kernel, "relay", f32(2 * wide, nz), (parts,))
+    share = call(relay_kernel, "relay", f32(2 * wide, nz), (parts, my_relaxed), (), LONG)
     parts = lax.all_to_all(share.reshape(wide, 2, nz), ("tm", "outer"), 0, 0).reshape(2 * wide, nz)
     residual, written = call(
         residual_kernel, "residual", (f32(1, *own.shape), f32(SUB, nz)), (my_relaxed, my_again)

time: 74.4 us -> 72.6 us (0.976)
  blocking collectives: 17.1 us -> 0 us
  starting transfers between devices: 35.5 us -> 46.6 us
  waiting for transfers between devices: 10.2 us -> 13.8 us
    all_to_all x1 -> x0, blocking collectives: 17.1 us -> none  [per_device(): parts = lax.all_to_all(share, 'inner', 0, 0)]
    all_to_all x0 -> x1, starting transfers between devices: none -> 7.88 us  [per_device(): parts = lax.all_to_all(share, 'inner', 0, 0)]
    all_to_all x0 -> x1, waiting for transfers between devices: none -> 3.12 us  [per_device(): parts = lax.all_to_all(share, 'inner', 0, 0)]
    all_to_all x1, starting transfers between devices: 11 us -> 13.3 us  [per_device(): lax.all_to_all(share.reshape(wide, 2, nz), ('tm', 'outer'), 0, 0)]
    ppermute x4, waiting for transfers between devices: 1.59 us -> 2.81 us  [per_device(): near = [lax.ppermute(half, SPACE, near_pairs) for half in (outer, inner)]]
    ppermute x1, starting transfers between devices: 3.78 us -> 4.67 us  [per_device(): lax.ppermute(again, 'tm', [(i, (i + 2) % slabs) for i in range(slabs)])]
    ppermute x1, waiting for transfers between devices: 0.81 us -> 0.01 us  [per_device(): far = lax.ppermute(relaxed, SPACE, far_pairs)]
  transfers between devices with their start and end apart: 9 -> 10, of which waited for: 3 -> 4; matrix products, arithmetic and copies ran while one was open for 0% -> 0% of each run, Pallas kernels for 9% -> 10%
where the time goes in v4:
time: 72.6 us; the launch traced here: 72.1 us
  starting transfers between devices  46.6 us (64%)
  waiting for transfers between devices  13.8 us (19%)
  Pallas kernels  9.76 us (13%)
  other arithmetic  1.18 us (2%)
  between operations  0.83 us (1%)
    all_to_all x1, starting transfers between devices, per_device(): lax.all_to_all(share.reshape(wide, 2, nz), ('tm', 'outer'), 0, 0)  13.3 us
    ppermute x4, starting transfers between devices, per_device(): near = [lax.ppermute(half, SPACE, near_pairs) for half in (outer, inner)]  11.1 us
    pallas_call x9, Pallas kernels, call(): pl.pallas_call(kernel, out_shape=out, in_specs=[vmem] * len(inputs), out_...  9.76 us
    all_to_all x1, starting transfers between devices, per_device(): parts = lax.all_to_all(share, 'inner', 0, 0)  7.88 us
    all_to_all x1, waiting for transfers between devices, per_device(): lax.all_to_all(share.reshape(wide, 2, nz), ('tm', 'outer'), 0, 0)  7.85 us
    ppermute x1, starting transfers between devices, per_device(): lax.ppermute(again, 'tm', [(i, (i + 2) % slabs) for i in range(slabs)])  4.67 us
    ppermute x1, starting transfers between devices, per_device(): far = lax.ppermute(start, SPACE, far_pairs)  4.59 us
    all_to_all x1, waiting for transfers between devices, per_device(): parts = lax.all_to_all(share, 'inner', 0, 0)  3.12 us
  transfers between devices with their start and end apart: 10, of which 4 were waited for; matrix products, arithmetic and copies ran while one was open for 0% of the time, Pallas kernels for 10%

profile of v4, /device:TPU:1, one launch (start us, length us, event | category | flops | bytes accessed | tf_op | source)
XLA Modules:
  0.0 72.1 jit_solution(4865532418160135678)
XLA Ops:
  0.6 1.2 %bitcast_select_fusion.own = f32[5,4,64,128]{3,2,1,0:T(8,128)S(1)} fusion(f32[5,4,64,128]{3,2,1,0:T(8,128)} %param.3, f32[1,5,4,64,128]{4,3,2,1,0:T(8,128)} %guess.1, pred[]{:T(512)S(6)} %eq.3), kind=kLoop, calls=%fused_computation | loop fusion | flops 163840 | bytes 1966081 | tf_op jit(solution)/shard_map/jit(_where)/select_n | solution.py:404
  1.8 4.6 %collective-permute-start = (f32[5,4,64,128]{3,2,1,0:T(8,128)S(1)}, f32[5,4,64,128]{3,2,1,0:T(8,128)S(1)}, u32[]{:S(2)}, u32[]{:S(2)}) collective-permute-start(f32[5,4,64,128]{3,2,1,0:T(8,128)S(1)} %bitcast_select_fusion.own), channel_id=1, source_target_pairs={{1,2},{2,1},{3,4},{4,3},{5,6},{6,5},{7,8},{8,7},{9,10},{10,9},{11,... | collective-permute-start | bytes 1966088 | tf_op jit(solution)/shard_map/ppermute | solution.py:405
  6.4 0.3 prepare.1
  6.7 4.9 %collective-permute-start.1 = (f32[5,2,8,8,128]{4,3,2,1,0:T(8,128)S(1)}, f32[5,2,8,8,128]{4,3,2,1,0:T(8,128)S(1)}, u32[]{:S(2)}, u32[]{:S(2)}) collective-permute-start(f32[5,2,8,8,128]{4,3,2,1,0:T(8,128)S(1)} %get-tuple-element.25.outer), channel_id=1, source_target_pairs={{0,1},{1,0},{2,3},{3,2},{4,5},{5,4},{6,7},{7,6},{8,9},{9,8},{10,11... | collective-permute-start | bytes 983048 | tf_op jit(solution)/shard_map/ppermute | solution.py:407
  11.6 1.9 %collective-permute-start.2 = (f32[5,2,8,8,128]{4,3,2,1,0:T(8,128)S(1)}, f32[5,2,8,8,128]{4,3,2,1,0:T(8,128)S(1)}, u32[]{:S(2)}, u32[]{:S(2)}) collective-permute-start(f32[5,2,8,8,128]{4,3,2,1,0:T(8,128)S(1)} %get-tuple-element.26.inner), channel_id=1, source_target_pairs={{0,1},{1,0},{2,3},{3,2},{4,5},{5,4},{6,7},{7,6},{8,9},{9,8},{10,11... | collective-permute-start | bytes 983048 | tf_op jit(solution)/shard_map/ppermute | solution.py:407
  13.6 0.0 collective-permute-done.1.near_outer
  13.6 1.6 %collective-permute-done.2.near_inner = f32[5,2,8,8,128]{4,3,2,1,0:T(8,128)S(1)} collective-permute-done((f32[5,2,8,8,128]{4,3,2,1,0:T(8,128)S(1)}, f32[5,2,8,8,128]{4,3,2,1,0:T(8,128)S(1)}, u32[]{:S(2)}, u32[]{:S(2)}) %collective-permute-start.2) | collective-permute-done | bytes 327712 | tf_op jit(solution)/shard_map/ppermute | solution.py:407
  15.2 1.2 %near.2 = (f32[5,2,8,8,128]{4,3,2,1,0:T(8,128)S(1)}, f32[5,2,8,8,128]{4,3,2,1,0:T(8,128)S(1)}, f32[5,2,8,8,128]{4,3,2,1,0:T(8,128)S(1)}, f32[2,8,8,128]{3,2,1,0:T(8,128)S(1)}, f32[5,2,8,8,128]{4,3,2,1,0:T(8,128)S(1)}) custom-call(f32[5,2,8,8,128]{4,3,2,1,0:T(8,128)S(1)} %get-tuple-element.25.outer, f32[5,2,8,8,128]{4,3,2,1,0:T(8,128)S(1)} %get-tuple-element.26.inner, ...), custom_call_target="tpu_custom_call" | custom-call | tf_op jit(solution)/shard_map/near/pallas_call | solution.py:361
  16.4 0.0 collective-permute-done.far
  16.4 0.0 copy-start
  16.4 0.0 copy-start.1
  16.4 1.6 %far.1.own = f32[5,4,64,128]{3,2,1,0:T(8,128)S(1)} custom-call(f32[5,2,8,8,128]{4,3,2,1,0:T(8,128)S(1)} %get-tuple-element.25.outer, f32[5,2,8,8,128]{4,3,2,1,0:T(8,128)S(1)} %get-tuple-element.26.inner, f32[5,4,64,128]{3,2,1,0:T(8,128)S(1)} %collective-permute-done.far, f32[5,4,8,8,128]{4,3,2,1,0:T(8,128)S(1)} %get-tuple-element.27.source, ...), custom_call_target="tpu_custom_call" | custom-call | tf_op jit(solution)/shard_map/far/pallas_call | solution.py:361
  18.0 1.9 %collective-permute-start.3 = (f32[5,4,64,128]{3,2,1,0:T(8,128)S(1)}, f32[5,4,64,128]{3,2,1,0:T(8,128)S(1)}, u32[]{:S(2)}, u32[]{:S(2)}) collective-permute-start(f32[5,4,64,128]{3,2,1,0:T(8,128)S(1)} %far.1.own), channel_id=1, source_target_pairs={{1,2},{2,1},{3,4},{4,3},{5,6},{6,5},{7,8},{8,7},{9,10},{10,9},{11,... | collective-permute-start | bytes 1966088 | tf_op jit(solution)/shard_map/ppermute | solution.py:411
  20.0 3.1 %collective-permute-start.6 = (f32[5,4,64,128]{3,2,1,0:T(8,128)S(1)}, f32[5,4,64,128]{3,2,1,0:T(8,128)S(1)}, u32[]{:S(2)}, u32[]{:S(2)}) collective-permute-start(f32[5,4,64,128]{3,2,1,0:T(8,128)S(1)} %far.1.own), channel_id=1, source_target_pairs={{0,128},{128,256},{256,384},{384,0},{1,129},{129,257},{257,385},{3... | collective-permute-start | bytes 1966088 | tf_op jit(solution)/shard_map/ppermute | solution.py:412
  23.0 0.0 copy-done
  23.1 0.0 copy-done.1
  23.1 0.4 prepare_again.1
  23.5 1.9 %collective-permute-start.4 = (f32[5,2,8,8,128]{4,3,2,1,0:T(8,128)S(1)}, f32[5,2,8,8,128]{4,3,2,1,0:T(8,128)S(1)}, u32[]{:S(2)}, u32[]{:S(2)}) collective-permute-start(f32[5,2,8,8,128]{4,3,2,1,0:T(8,128)S(1)} %get-tuple-element.34.outer), channel_id=1, source_target_pairs={{0,1},{1,0},{2,3},{3,2},{4,5},{5,4},{6,7},{7,6},{8,9},{9,8},{10,11... | collective-permute-start | bytes 983048 | tf_op jit(solution)/shard_map/ppermute | solution.py:417
  25.4 2.4 %collective-permute-start.5 = (f32[5,2,8,8,128]{4,3,2,1,0:T(8,128)S(1)}, f32[5,2,8,8,128]{4,3,2,1,0:T(8,128)S(1)}, u32[]{:S(2)}, u32[]{:S(2)}) collective-permute-start(f32[5,2,8,8,128]{4,3,2,1,0:T(8,128)S(1)} %get-tuple-element.35.inner), channel_id=1, source_target_pairs={{0,1},{1,0},{2,3},{3,2},{4,5},{5,4},{6,7},{7,6},{8,9},{9,8},{10,11... | collective-permute-start | bytes 983048 | tf_op jit(solution)/shard_map/ppermute | solution.py:417
  27.8 0.0 collective-permute-done.4.near_outer
  27.8 1.2 %collective-permute-done.5.near_inner = f32[5,2,8,8,128]{4,3,2,1,0:T(8,128)S(1)} collective-permute-done((f32[5,2,8,8,128]{4,3,2,1,0:T(8,128)S(1)}, f32[5,2,8,8,128]{4,3,2,1,0:T(8,128)S(1)}, u32[]{:S(2)}, u32[]{:S(2)}) %collective-permute-start.5) | collective-permute-done | bytes 327712 | tf_op jit(solution)/shard_map/ppermute | solution.py:417
  29.1 1.3 %near.3 = (f32[5,2,8,8,128]{4,3,2,1,0:T(8,128)S(1)}, f32[5,2,8,8,128]{4,3,2,1,0:T(8,128)S(1)}, f32[5,2,8,8,128]{4,3,2,1,0:T(8,128)S(1)}, f32[2,8,8,128]{3,2,1,0:T(8,128)S(1)}, f32[5,2,8,8,128]{4,3,2,1,0:T(8,128)S(1)}) custom-call(f32[5,2,8,8,128]{4,3,2,1,0:T(8,128)S(1)} %get-tuple-element.34.outer, f32[5,2,8,8,128]{4,3,2,1,0:T(8,128)S(1)} %get-tuple-element.35.inner, ...), custom_call_target="tpu_custom_call" | custom-call | tf_op jit(solution)/shard_map/near/pallas_call | solution.py:361
  30.3 0.0 collective-permute-done.3.far
  30.4 2.4 %far_again.1 = (f32[5,4,64,128]{3,2,1,0:T(8,128)S(1)}, f32[16,8,128]{2,1,0:T(8,128)}) custom-call(f32[5,2,8,8,128]{4,3,2,1,0:T(8,128)S(1)} %get-tuple-element.34.outer, f32[5,2,8,8,128]{4,3,2,1,0:T(8,128)S(1)} %get-tuple-element.35.inner, f32[5,4,64,128]{3,2,1,0:T(8,128)S(1)} %collective-permute-done.3.far, ...), custom_call_target="tpu_custom_call" | custom-call | tf_op jit(solution)/shard_map/far_again/pallas_call | solution.py:361
  32.8 7.9 %all-to-all-start = ((f32[16,8,128]{2,1,0:T(8,128)}), f32[16,8,128]{2,1,0:T(8,128)S(1)}, u32[]{:S(2)}, u32[]{:S(2)}) async-start(f32[16,8,128]{2,1,0:T(8,128)} %get-tuple-element.44), calls=%async_computation | async-start | bytes 131072 | tf_op jit(solution)/shard_map/all_to_all | solution.py:428
  40.7 4.7 %collective-permute-start.7 = (f32[5,4,64,128]{3,2,1,0:T(8,128)S(1)}, f32[5,4,64,128]{3,2,1,0:T(8,128)S(1)}, u32[]{:S(2)}, u32[]{:S(2)}) collective-permute-start(f32[5,4,64,128]{3,2,1,0:T(8,128)S(1)} %get-tuple-element.45), channel_id=1, source_target_pairs={{0,256},{128,384},{256,0},{384,128},{1,257},{129,385},{257,1},{385... | collective-permute-start | bytes 1966088 | tf_op jit(solution)/shard_map/ppermute | solution.py:427
  45.4 0.0 collective-permute-done.6.relaxed
  45.4 3.1 %all-to-all-done.parts = f32[16,8,128]{2,1,0:T(8,128)S(1)} async-done(((f32[16,8,128]{2,1,0:T(8,128)}), f32[16,8,128]{2,1,0:T(8,128)S(1)}, u32[]{:S(2)}, u32[]{:S(2)}) %all-to-all-start) | async-done | bytes 65568 | tf_op jit(solution)/shard_map/all_to_all | solution.py:428
  48.5 0.6 relay.1
  49.1 13.3 %all-to-all-start.1 = ((f32[32,2,128]{2,1,0:T(2,128)}), f32[32,2,128]{2,1,0:T(2,128)S(1)}, u32[]{:S(2)}, u32[]{:S(2)}) async-start(f32[32,2,128]{2,1,0:T(2,128)} %bitcast.1), calls=%async_computation.1 | async-start | bytes 65536 | tf_op jit(solution)/shard_map/all_to_all | solution.py:431
  62.4 0.0 collective-permute-done.7.again
  62.4 0.9 %residual.1 = (f32[1,5,4,64,128]{4,3,2,1,0:T(8,128)}, f32[8,128]{1,0:T(8,128)S(1)}) custom-call(f32[5,4,64,128]{3,2,1,0:T(8,128)S(1)} %collective-permute-done.6.relaxed, f32[5,4,64,128]{3,2,1,0:T(8,128)S(1)} %collective-permute-done.7.again), custom_call_target="tpu_custom_call" | custom-call | tf_op jit(solution)/shard_map/residual/pallas_call | solution.py:361
  63.3 7.8 %all-to-all-done.1 = f32[32,2,128]{2,1,0:T(2,128)S(1)} async-done(((f32[32,2,128]{2,1,0:T(2,128)}), f32[32,2,128]{2,1,0:T(2,128)S(1)}, u32[]{:S(2)}, u32[]{:S(2)}) %all-to-all-start.1) | async-done | bytes 32800 | tf_op jit(solution)/shard_map/all_to_all | solution.py:431
  71.2 1.0 %correct.1 = f32[1,5,4,64,128]{4,3,2,1,0:T(8,128)} custom-call(f32[64,128]{1,0:T(8,128)S(1)} %bitcast.4, f32[5,4,64,128]{3,2,1,0:T(8,128)S(1)} %collective-permute-done.6.relaxed, f32[8,128]{1,0:T(8,128)S(1)} %get-tuple-element.46.written), custom_call_target="tpu_custom_call" | custom-call | tf_op jit(solution)/shard_map/correct/pallas_call | solution.py:361
Async XLA Ops:
  1.8 14.6 %collective-permute-start = (f32[5,4,64,128]{3,2,1,0:T(8,128)S(1)}, f32[5,4,64,128]{3,2,1,0:T(8,128)S(1)}, u32[]{:S(2)}, u32[]{:S(2)}) collective-permute-start(f32[5,4,64,128]{3,2,1,0:T(8,128)S(1)} %bitcast_select_fusion.own), channel_id=1, source_target_pairs={{1,2},{2,1},{3,4},{4,3},{5,6},{6,5},{7,8},{8,7},{9,10},{10,9},{11,... | collective-permute-start | bytes 1966088 | tf_op jit(solution)/shard_map/ppermute | solution.py:405
  6.7 6.8 %collective-permute-start.1 = (f32[5,2,8,8,128]{4,3,2,1,0:T(8,128)S(1)}, f32[5,2,8,8,128]{4,3,2,1,0:T(8,128)S(1)}, u32[]{:S(2)}, u32[]{:S(2)}) collective-permute-start(f32[5,2,8,8,128]{4,3,2,1,0:T(8,128)S(1)} %get-tuple-element.25.outer), channel_id=1, source_target_pairs={{0,1},{1,0},{2,3},{3,2},{4,5},{5,4},{6,7},{7,6},{8,9},{9,8},{10,11... | collective-permute-start | bytes 983048 | tf_op jit(solution)/shard_map/ppermute | solution.py:407
  11.6 3.5 %collective-permute-start.2 = (f32[5,2,8,8,128]{4,3,2,1,0:T(8,128)S(1)}, f32[5,2,8,8,128]{4,3,2,1,0:T(8,128)S(1)}, u32[]{:S(2)}, u32[]{:S(2)}) collective-permute-start(f32[5,2,8,8,128]{4,3,2,1,0:T(8,128)S(1)} %get-tuple-element.26.inner), channel_id=1, source_target_pairs={{0,1},{1,0},{2,3},{3,2},{4,5},{5,4},{6,7},{7,6},{8,9},{9,8},{10,11... | collective-permute-start | bytes 983048 | tf_op jit(solution)/shard_map/ppermute | solution.py:407
  16.4 6.6 %copy-start = (f32[1,5,4,64,128]{4,3,2,1,0:T(8,128)S(1)}, f32[1,5,4,64,128]{4,3,2,1,0:T(8,128)}, u32[]{:S(2)}) copy-start(f32[1,5,4,64,128]{4,3,2,1,0:T(8,128)} %guess.1) | copy-start | bytes 1966084
  16.4 6.6 %copy-start.1 = (f32[4,3,8,128]{3,2,1,0:T(8,128)S(1)}, f32[4,3,8,128]{3,2,1,0:T(8,128)}, u32[]{:S(2)}) copy-start(f32[4,3,8,128]{3,2,1,0:T(8,128)} %constant.10.clone.weights) | copy-start | bytes 147460
  18.0 12.3 %collective-permute-start.3 = (f32[5,4,64,128]{3,2,1,0:T(8,128)S(1)}, f32[5,4,64,128]{3,2,1,0:T(8,128)S(1)}, u32[]{:S(2)}, u32[]{:S(2)}) collective-permute-start(f32[5,4,64,128]{3,2,1,0:T(8,128)S(1)} %far.1.own), channel_id=1, source_target_pairs={{1,2},{2,1},{3,4},{4,3},{5,6},{6,5},{7,8},{8,7},{9,10},{10,9},{11,... | collective-permute-start | bytes 1966088 | tf_op jit(solution)/shard_map/ppermute | solution.py:411
  20.0 25.4 %collective-permute-start.6 = (f32[5,4,64,128]{3,2,1,0:T(8,128)S(1)}, f32[5,4,64,128]{3,2,1,0:T(8,128)S(1)}, u32[]{:S(2)}, u32[]{:S(2)}) collective-permute-start(f32[5,4,64,128]{3,2,1,0:T(8,128)S(1)} %far.1.own), channel_id=1, source_target_pairs={{0,128},{128,256},{256,384},{384,0},{1,129},{129,257},{257,385},{3... | collective-permute-start | bytes 1966088 | tf_op jit(solution)/shard_map/ppermute | solution.py:412
  23.5 4.3 %collective-permute-start.4 = (f32[5,2,8,8,128]{4,3,2,1,0:T(8,128)S(1)}, f32[5,2,8,8,128]{4,3,2,1,0:T(8,128)S(1)}, u32[]{:S(2)}, u32[]{:S(2)}) collective-permute-start(f32[5,2,8,8,128]{4,3,2,1,0:T(8,128)S(1)} %get-tuple-element.34.outer), channel_id=1, source_target_pairs={{0,1},{1,0},{2,3},{3,2},{4,5},{5,4},{6,7},{7,6},{8,9},{9,8},{10,11... | collective-permute-start | bytes 983048 | tf_op jit(solution)/shard_map/ppermute | solution.py:417
  25.4 3.6 %collective-permute-start.5 = (f32[5,2,8,8,128]{4,3,2,1,0:T(8,128)S(1)}, f32[5,2,8,8,128]{4,3,2,1,0:T(8,128)S(1)}, u32[]{:S(2)}, u32[]{:S(2)}) collective-permute-start(f32[5,2,8,8,128]{4,3,2,1,0:T(8,128)S(1)} %get-tuple-element.35.inner), channel_id=1, source_target_pairs={{0,1},{1,0},{2,3},{3,2},{4,5},{5,4},{6,7},{7,6},{8,9},{9,8},{10,11... | collective-permute-start | bytes 983048 | tf_op jit(solution)/shard_map/ppermute | solution.py:417
  32.8 15.7 %all-to-all-start = ((f32[16,8,128]{2,1,0:T(8,128)}), f32[16,8,128]{2,1,0:T(8,128)S(1)}, u32[]{:S(2)}, u32[]{:S(2)}) async-start(f32[16,8,128]{2,1,0:T(8,128)} %get-tuple-element.44), calls=%async_computation | async-start | bytes 131072 | tf_op jit(solution)/shard_map/all_to_all | solution.py:428
  40.7 21.7 %collective-permute-start.7 = (f32[5,4,64,128]{3,2,1,0:T(8,128)S(1)}, f32[5,4,64,128]{3,2,1,0:T(8,128)S(1)}, u32[]{:S(2)}, u32[]{:S(2)}) collective-permute-start(f32[5,4,64,128]{3,2,1,0:T(8,128)S(1)} %get-tuple-element.45), channel_id=1, source_target_pairs={{0,256},{128,384},{256,0},{384,128},{1,257},{129,385},{257,1},{385... | collective-permute-start | bytes 1966088 | tf_op jit(solution)/shard_map/ppermute | solution.py:427
  49.1 22.1 %all-to-all-start.1 = ((f32[32,2,128]{2,1,0:T(2,128)}), f32[32,2,128]{2,1,0:T(2,128)S(1)}, u32[]{:S(2)}, u32[]{:S(2)}) async-start(f32[32,2,128]{2,1,0:T(2,128)} %bitcast.1), calls=%async_computation.1 | async-start | bytes 65536 | tf_op jit(solution)/shard_map/all_to_all | solution.py:431

commit v5 on v4

--- a/solution.py
+++ b/solution.py
@@ -24,6 +24,7 @@
 SPACE = ("outer", "inner")
 LIMIT = pltpu.CompilerParams(vmem_limit_bytes=16 * 1024 * 1024)
 
+SHORT = pl.CostEstimate(flops=0, bytes_accessed=0, transcendentals=0)
 LONG = pl.CostEstimate(flops=40000000000, bytes_accessed=147600000, transcendentals=0)
 
 
@@ -124,13 +125,17 @@
     rest[...] = weights[slab, 1] * relaxed + weights[slab, 2] * old
 
 
-def near_kernel(outer, inner, near_outer, near_inner, source, scale, v1, w2, source2, scale2, v2, near_source, near_scale, v1_more, w2_more):
+def beyond_kernel(*refs):
+    near_kernel(*refs, mirrored=False)
+
+
+def near_kernel(outer, inner, near_outer, near_inner, source, scale, v1, w2, source2, scale2, v2, near_source, near_scale, v1_more, w2_more, mirrored=True):
     count = outer.shape[2]
 
     def w_at(k, r, at=slice(None)):
         if r < 8:
             return (outer if r < 6 else inner)[k, r % 2, at]
-        r = 11 - r
+        r = 11 - r if mirrored else r - 8
         return (near_outer if r < 2 else near_inner)[k, r % 2, at]
 
     for i in range(3):
@@ -205,7 +210,7 @@
     masked = jnp.where(edge, 0.0, cross)
     for j in range(ROWS):
         for k in range(COMP):
-            wf[k, j] = spaced(far, k, row(j))
+            wf[k, j] = jnp.where(edge, 0.0, spaced(far, k, row(j)))
     for r in range(1, 4):
 
         def write_source(k, at, value, r=r):
@@ -381,6 +386,8 @@
     for i in range(1, count - 1, 2):
         far_pairs += [(i, i + 1), (i + 1, i)]
 
+    farther_pairs = [(i - 2, i) for i in range(2, count, 2)] + [(i + 2, i) for i in range(1, count - 2, 2)]
+
     def several(*lead):
         return f32(*lead, *row)
 
@@ -405,17 +412,32 @@
     far = lax.ppermute(start, SPACE, far_pairs)
     outer, inner, source, scale = call(prepare_kernel, "prepare", prepared, (start,))
     near = [lax.ppermute(half, SPACE, near_pairs) for half in (outer, inner)]
-    kept = call(near_kernel, "near", state, (outer, inner, *near, source, scale), near_scratch)
-    relaxed = call(far_kernel, "far", f32(*own.shape), (outer, inner, far, source, scale, *kept), far_scratch)
-
-    far = lax.ppermute(relaxed, SPACE, far_pairs)
+    kept = call(near_kernel, "near", state, (outer, inner, *near, source, scale), near_scratch, SHORT)
+    held, kept = lax.optimization_barrier((start, kept))
+    farther = lax.ppermute(held, SPACE, farther_pairs)
+    relaxed = call(
+        far_kernel, "far", f32(*own.shape), (outer, inner, far, source, scale, *kept), far_scratch, SHORT
+    )
+
+    beyond = call(prepare_kernel, "prepare_far", prepared, (far,), (), SHORT)
+    kept = call(
+        beyond_kernel, "beyond", state, (*beyond[:2], outer, inner, *beyond[2:]), near_scratch, SHORT
+    )
+    far = call(
+        far_kernel,
+        "far_relaxed",
+        f32(*own.shape),
+        (*beyond[:2], farther, *beyond[2:], *kept),
+        far_scratch,
+        SHORT,
+    )
     my_relaxed = lax.ppermute(relaxed, "tm", [(i, (i + 1) % slabs) for i in range(slabs)])
     weights = slot_weights(slabs, nz, count * rows * ny * BLK)
     outer, inner, source, scale, rest = call(
-        prepare_again_kernel, "prepare_again", (*prepared, f32(SUB, nz)), (relaxed, guess, weights)
+        prepare_again_kernel, "prepare_again", (*prepared, f32(SUB, nz)), (relaxed, guess, weights), (), SHORT
     )
     near = [lax.ppermute(half, SPACE, near_pairs) for half in (outer, inner)]
-    kept = call(near_kernel, "near", state, (outer, inner, *near, source, scale), near_scratch)
+    kept = call(near_kernel, "near", state, (outer, inner, *near, source, scale), near_scratch, SHORT)
     again, share = call(
         far_again_kernel,
         "far_again",

time: 72.6 us -> 72 us (level)
  Pallas kernels: 9.76 us -> 12.8 us
  starting transfers between devices: 46.6 us -> 44 us
  waiting for transfers between devices: 13.8 us -> 12.7 us
    pallas_call x9 -> x12, Pallas kernels: 9.76 us -> 12.8 us  [call(): pl.pallas_call(kernel, out_shape=out, in_specs=[vmem] * len(inputs), out_...]
    ppermute x4, waiting for transfers between devices: 2.81 us -> 1.63 us  [per_device(): near = [lax.ppermute(half, SPACE, near_pairs) for half in (outer, inner)]]
    ppermute x1, starting transfers between devices: 3.07 us -> 1.92 us  [per_device(): lax.ppermute(relaxed, 'tm', [(i, (i + 1) % slabs) for i in range(slabs)])]
    all_to_all x1, starting transfers between devices: 7.88 us -> 6.81 us  [per_device(): parts = lax.all_to_all(share, 'inner', 0, 0)]
    ppermute x4, starting transfers between devices: 11.1 us -> 11.9 us  [per_device(): near = [lax.ppermute(half, SPACE, near_pairs) for half in (outer, inner)]]
  transfers between devices with their start and end apart: 10 -> 10, of which waited for: 4 -> 3; matrix products, arithmetic and copies ran while one was open for 0% -> 0% of each run, Pallas kernels for 10% -> 17%
where the time goes in v5:
time: 72 us; the launch traced here: 71.5 us
  starting transfers between devices  44 us (61%)
  Pallas kernels  12.8 us (18%)
  waiting for transfers between devices  12.7 us (18%)
  other arithmetic  1.18 us (2%)
  between operations  0.84 us (1%)
    all_to_all x1, starting transfers between devices, per_device(): lax.all_to_all(share.reshape(wide, 2, nz), ('tm', 'outer'), 0, 0)  12.8 us
    pallas_call x12, Pallas kernels, call(): pl.pallas_call(kernel, out_shape=out, in_specs=[vmem] * len(inputs), out_...  12.8 us
    ppermute x4, starting transfers between devices, per_device(): near = [lax.ppermute(half, SPACE, near_pairs) for half in (outer, inner)]  11.9 us
    all_to_all x1, waiting for transfers between devices, per_device(): lax.all_to_all(share.reshape(wide, 2, nz), ('tm', 'outer'), 0, 0)  7.85 us
    all_to_all x1, starting transfers between devices, per_device(): parts = lax.all_to_all(share, 'inner', 0, 0)  6.81 us
    ppermute x1, starting transfers between devices, per_device(): far = lax.ppermute(start, SPACE, far_pairs)  4.59 us
    ppermute x1, starting transfers between devices, per_device(): lax.ppermute(again, 'tm', [(i, (i + 2) % slabs) for i in range(slabs)])  4.57 us
    all_to_all x1, waiting for transfers between devices, per_device(): parts = lax.all_to_all(share, 'inner', 0, 0)  3.23 us
  transfers between devices with their start and end apart: 10, of which 3 were waited for; matrix products, arithmetic and copies ran while one was open for 0% of the time, Pallas kernels for 17%

profile of v5, /device:TPU:1, one launch (start us, length us, event | category | flops | bytes accessed | tf_op | source)
XLA Modules:
  0.0 71.5 jit_solution(14715409967855608678)
XLA Ops:
  0.6 1.2 %bitcast_select_fusion.own = f32[5,4,64,128]{3,2,1,0:T(8,128)S(1)} fusion(f32[5,4,64,128]{3,2,1,0:T(8,128)} %param.3, f32[1,5,4,64,128]{4,3,2,1,0:T(8,128)} %guess.1, pred[]{:T(512)S(6)} %eq.3), kind=kLoop, calls=%fused_computation | loop fusion | flops 163840 | bytes 1966081 | tf_op jit(solution)/shard_map/jit(_where)/select_n | solution.py:411
  1.8 4.6 %collective-permute-start = (f32[5,4,64,128]{3,2,1,0:T(8,128)S(1)}, f32[5,4,64,128]{3,2,1,0:T(8,128)S(1)}, u32[]{:S(2)}, u32[]{:S(2)}) collective-permute-start(f32[5,4,64,128]{3,2,1,0:T(8,128)S(1)} %bitcast_select_fusion.own), channel_id=1, source_target_pairs={{1,2},{2,1},{3,4},{4,3},{5,6},{6,5},{7,8},{8,7},{9,10},{10,9},{11,... | collective-permute-start | bytes 1966088 | tf_op jit(solution)/shard_map/ppermute | solution.py:412
  6.4 0.3 prepare.1
  6.7 4.9 %collective-permute-start.1 = (f32[5,2,8,8,128]{4,3,2,1,0:T(8,128)S(1)}, f32[5,2,8,8,128]{4,3,2,1,0:T(8,128)S(1)}, u32[]{:S(2)}, u32[]{:S(2)}) collective-permute-start(f32[5,2,8,8,128]{4,3,2,1,0:T(8,128)S(1)} %get-tuple-element.40.outer.refs_2_), channel_id=1, source_target_pairs={{0,1},{1,0},{2,3},{3,2},{4,5},{5,4},{6,7},{7,6},{8,9},{9,8},{10,11... | collective-permute-start | bytes 983048 | tf_op jit(solution)/shard_map/ppermute | solution.py:414
  11.6 1.9 %collective-permute-start.2 = (f32[5,2,8,8,128]{4,3,2,1,0:T(8,128)S(1)}, f32[5,2,8,8,128]{4,3,2,1,0:T(8,128)S(1)}, u32[]{:S(2)}, u32[]{:S(2)}) collective-permute-start(f32[5,2,8,8,128]{4,3,2,1,0:T(8,128)S(1)} %get-tuple-element.41.inner.refs_3_), channel_id=1, source_target_pairs={{0,1},{1,0},{2,3},{3,2},{4,5},{5,4},{6,7},{7,6},{8,9},{9,8},{10,11... | collective-permute-start | bytes 983048 | tf_op jit(solution)/shard_map/ppermute | solution.py:414
  13.6 0.0 collective-permute-done.1.near_outer
  13.6 1.6 %collective-permute-done.2.near_inner = f32[5,2,8,8,128]{4,3,2,1,0:T(8,128)S(1)} collective-permute-done((f32[5,2,8,8,128]{4,3,2,1,0:T(8,128)S(1)}, f32[5,2,8,8,128]{4,3,2,1,0:T(8,128)S(1)}, u32[]{:S(2)}, u32[]{:S(2)}) %collective-permute-start.2) | collective-permute-done | bytes 327712 | tf_op jit(solution)/shard_map/ppermute | solution.py:414
  15.2 1.2 %near.2 = (f32[5,2,8,8,128]{4,3,2,1,0:T(8,128)S(1)}, f32[5,2,8,8,128]{4,3,2,1,0:T(8,128)S(1)}, f32[5,2,8,8,128]{4,3,2,1,0:T(8,128)S(1)}, f32[2,8,8,128]{3,2,1,0:T(8,128)S(1)}, f32[5,2,8,8,128]{4,3,2,1,0:T(8,128)S(1)}) custom-call(f32[5,2,8,8,128]{4,3,2,1,0:T(8,128)S(1)} %get-tuple-element.40.outer.refs_2_, ...), custom_call_target="tpu_custom_call" | custom-call | tf_op jit(solution)/shard_map/near/pallas_call | solution.py:366
  16.4 0.0 copy-start
  16.4 0.0 copy-start.1
  16.4 1.4 %collective-permute-start.3 = (f32[5,4,64,128]{3,2,1,0:T(8,128)S(1)}, f32[5,4,64,128]{3,2,1,0:T(8,128)S(1)}, u32[]{:S(2)}, u32[]{:S(2)}) collective-permute-start(f32[5,4,64,128]{3,2,1,0:T(8,128)S(1)} %bitcast_select_fusion.own), channel_id=1, source_target_pairs={{0,2},{2,4},{4,6},{6,8},{8,10},{10,12},{12,14},{14,16},{16,18},{18... | collective-permute-start | bytes 1966088 | tf_op jit(solution)/shard_map/ppermute | solution.py:417
  17.9 0.0 collective-permute-done.far.own
  17.9 1.6 %far.1.own = f32[5,4,64,128]{3,2,1,0:T(8,128)S(1)} custom-call(f32[5,2,8,8,128]{4,3,2,1,0:T(8,128)S(1)} %get-tuple-element.40.outer.refs_2_, f32[5,2,8,8,128]{4,3,2,1,0:T(8,128)S(1)} %get-tuple-element.41.inner.refs_3_, f32[5,4,64,128]{3,2,1,0:T(8,128)S(1)} %collective-permute-done.far.own, f32[5,4,8,8,128]{4,3,2,1,0:T(8,128)S(1)} %get-tuple-element.42.source, ...), custom_call_target="tpu_custom_call" | custom-call | tf_op jit(solution)/shard_map/far/pallas_call | solution.py:366
  19.4 1.9 %collective-permute-start.6 = (f32[5,4,64,128]{3,2,1,0:T(8,128)S(1)}, f32[5,4,64,128]{3,2,1,0:T(8,128)S(1)}, u32[]{:S(2)}, u32[]{:S(2)}) collective-permute-start(f32[5,4,64,128]{3,2,1,0:T(8,128)S(1)} %far.1.own), channel_id=1, source_target_pairs={{0,128},{128,256},{256,384},{384,0},{1,129},{129,257},{257,385},{3... | collective-permute-start | bytes 1966088 | tf_op jit(solution)/shard_map/ppermute | solution.py:434
  21.4 0.0 copy-done
  21.4 0.0 copy-done.1
  21.4 0.4 prepare_again.1
  21.8 3.1 %collective-permute-start.4 = (f32[5,2,8,8,128]{4,3,2,1,0:T(8,128)S(1)}, f32[5,2,8,8,128]{4,3,2,1,0:T(8,128)S(1)}, u32[]{:S(2)}, u32[]{:S(2)}) collective-permute-start(f32[5,2,8,8,128]{4,3,2,1,0:T(8,128)S(1)} %get-tuple-element.54.outer), channel_id=1, source_target_pairs={{0,1},{1,0},{2,3},{3,2},{4,5},{5,4},{6,7},{7,6},{8,9},{9,8},{10,11... | collective-permute-start | bytes 983048 | tf_op jit(solution)/shard_map/ppermute | solution.py:439
  24.9 1.9 %collective-permute-start.5 = (f32[5,2,8,8,128]{4,3,2,1,0:T(8,128)S(1)}, f32[5,2,8,8,128]{4,3,2,1,0:T(8,128)S(1)}, u32[]{:S(2)}, u32[]{:S(2)}) collective-permute-start(f32[5,2,8,8,128]{4,3,2,1,0:T(8,128)S(1)} %get-tuple-element.55.inner), channel_id=1, source_target_pairs={{0,1},{1,0},{2,3},{3,2},{4,5},{5,4},{6,7},{7,6},{8,9},{9,8},{10,11... | collective-permute-start | bytes 983048 | tf_op jit(solution)/shard_map/ppermute | solution.py:439
  26.9 0.3 prepare_far.1
  27.2 1.2 %beyond.1 = (f32[5,2,8,8,128]{4,3,2,1,0:T(8,128)S(1)}, f32[5,2,8,8,128]{4,3,2,1,0:T(8,128)S(1)}, f32[5,2,8,8,128]{4,3,2,1,0:T(8,128)S(1)}, f32[2,8,8,128]{3,2,1,0:T(8,128)S(1)}, f32[5,2,8,8,128]{4,3,2,1,0:T(8,128)S(1)}) custom-call(f32[5,2,8,8,128]{4,3,2,1,0:T(8,128)S(1)} %get-tuple-element.56.refs_0_.outer, ...), custom_call_target="tpu_custom_call" | custom-call | tf_op jit(solution)/shard_map/beyond/pallas_call | solution.py:366
  28.4 0.0 collective-permute-done.4.near_outer
  28.4 0.0 collective-permute-done.5.near_inner
  28.5 1.3 %near.3 = (f32[5,2,8,8,128]{4,3,2,1,0:T(8,128)S(1)}, f32[5,2,8,8,128]{4,3,2,1,0:T(8,128)S(1)}, f32[5,2,8,8,128]{4,3,2,1,0:T(8,128)S(1)}, f32[2,8,8,128]{3,2,1,0:T(8,128)S(1)}, f32[5,2,8,8,128]{4,3,2,1,0:T(8,128)S(1)}) custom-call(f32[5,2,8,8,128]{4,3,2,1,0:T(8,128)S(1)} %get-tuple-element.54.outer, f32[5,2,8,8,128]{4,3,2,1,0:T(8,128)S(1)} %get-tuple-element.55.inner, ...), custom_call_target="tpu_custom_call" | custom-call | tf_op jit(solution)/shard_map/near/pallas_call | solution.py:366
  29.7 0.0 collective-permute-done.3.far
  29.8 1.6 %far_relaxed.1.far = f32[5,4,64,128]{3,2,1,0:T(8,128)S(1)} custom-call(f32[5,2,8,8,128]{4,3,2,1,0:T(8,128)S(1)} %get-tuple-element.56.refs_0_.outer, f32[5,2,8,8,128]{4,3,2,1,0:T(8,128)S(1)} %get-tuple-element.57.refs_1_.inner, f32[5,4,64,128]{3,2,1,0:T(8,128)S(1)} %collective-permute-done.3.far, f32[5,4,8,8,128]{4,3,2,1,0:T(8,128)S(1)} %get-tuple-element.59.refs_4_.source, ...), custom_call_target="tpu_custom_call" | custom-call | tf_op jit(solution)/shard_map/far_relaxed/pallas_call | solution.py:366
  31.3 2.4 %far_again.1 = (f32[5,4,64,128]{3,2,1,0:T(8,128)S(1)}, f32[16,8,128]{2,1,0:T(8,128)}) custom-call(f32[5,2,8,8,128]{4,3,2,1,0:T(8,128)S(1)} %get-tuple-element.54.outer, f32[5,2,8,8,128]{4,3,2,1,0:T(8,128)S(1)} %get-tuple-element.55.inner, f32[5,4,64,128]{3,2,1,0:T(8,128)S(1)} %far_relaxed.1.far, f32[5,4,8,8,128]{4,3,2,1,0:T(8,128)S(1)} %get-tuple-element.66.source, ...), custom_call_target="tpu_custom_call" | custom-call | tf_op jit(solution)/shard_map/far_again/pallas_call | solution.py:366
  33.7 6.8 %all-to-all-start = ((f32[16,8,128]{2,1,0:T(8,128)}), f32[16,8,128]{2,1,0:T(8,128)S(1)}, u32[]{:S(2)}, u32[]{:S(2)}) async-start(f32[16,8,128]{2,1,0:T(8,128)} %get-tuple-element.74), calls=%async_computation | async-start | bytes 131072 | tf_op jit(solution)/shard_map/all_to_all | solution.py:450
  40.5 4.6 %collective-permute-start.7 = (f32[5,4,64,128]{3,2,1,0:T(8,128)S(1)}, f32[5,4,64,128]{3,2,1,0:T(8,128)S(1)}, u32[]{:S(2)}, u32[]{:S(2)}) collective-permute-start(f32[5,4,64,128]{3,2,1,0:T(8,128)S(1)} %get-tuple-element.75), channel_id=1, source_target_pairs={{0,256},{128,384},{256,0},{384,128},{1,257},{129,385},{257,1},{385... | collective-permute-start | bytes 1966088 | tf_op jit(solution)/shard_map/ppermute | solution.py:449
  45.1 3.2 %all-to-all-done.parts = f32[16,8,128]{2,1,0:T(8,128)S(1)} async-done(((f32[16,8,128]{2,1,0:T(8,128)}), f32[16,8,128]{2,1,0:T(8,128)S(1)}, u32[]{:S(2)}, u32[]{:S(2)}) %all-to-all-start) | async-done | bytes 65568 | tf_op jit(solution)/shard_map/all_to_all | solution.py:450
  48.3 0.0 collective-permute-done.6.relaxed
  48.3 0.6 relay.1
  49.0 12.8 %all-to-all-start.1 = ((f32[32,2,128]{2,1,0:T(2,128)}), f32[32,2,128]{2,1,0:T(2,128)S(1)}, u32[]{:S(2)}, u32[]{:S(2)}) async-start(f32[32,2,128]{2,1,0:T(2,128)} %bitcast.1), calls=%async_computation.1 | async-start | bytes 65536 | tf_op jit(solution)/shard_map/all_to_all | solution.py:453
  61.8 0.0 collective-permute-done.7.again
  61.8 0.9 %residual.1 = (f32[1,5,4,64,128]{4,3,2,1,0:T(8,128)}, f32[8,128]{1,0:T(8,128)S(1)}) custom-call(f32[5,4,64,128]{3,2,1,0:T(8,128)S(1)} %collective-permute-done.6.relaxed, f32[5,4,64,128]{3,2,1,0:T(8,128)S(1)} %collective-permute-done.7.again), custom_call_target="tpu_custom_call" | custom-call | tf_op jit(solution)/shard_map/residual/pallas_call | solution.py:366
  62.7 7.8 %all-to-all-done.1 = f32[32,2,128]{2,1,0:T(2,128)S(1)} async-done(((f32[32,2,128]{2,1,0:T(2,128)}), f32[32,2,128]{2,1,0:T(2,128)S(1)}, u32[]{:S(2)}, u32[]{:S(2)}) %all-to-all-start.1) | async-done | bytes 32800 | tf_op jit(solution)/shard_map/all_to_all | solution.py:453
  70.5 1.0 %correct.1 = f32[1,5,4,64,128]{4,3,2,1,0:T(8,128)} custom-call(f32[64,128]{1,0:T(8,128)S(1)} %bitcast.4, f32[5,4,64,128]{3,2,1,0:T(8,128)S(1)} %collective-permute-done.6.relaxed, f32[8,128]{1,0:T(8,128)S(1)} %get-tuple-element.76.written), custom_call_target="tpu_custom_call" | custom-call | tf_op jit(solution)/shard_map/correct/pallas_call | solution.py:366
Async XLA Ops:
  1.8 16.0 %collective-permute-start = (f32[5,4,64,128]{3,2,1,0:T(8,128)S(1)}, f32[5,4,64,128]{3,2,1,0:T(8,128)S(1)}, u32[]{:S(2)}, u32[]{:S(2)}) collective-permute-start(f32[5,4,64,128]{3,2,1,0:T(8,128)S(1)} %bitcast_select_fusion.own), channel_id=1, source_target_pairs={{1,2},{2,1},{3,4},{4,3},{5,6},{6,5},{7,8},{8,7},{9,10},{10,9},{11,... | collective-permute-start | bytes 1966088 | tf_op jit(solution)/shard_map/ppermute | solution.py:412
  6.7 6.8 %collective-permute-start.1 = (f32[5,2,8,8,128]{4,3,2,1,0:T(8,128)S(1)}, f32[5,2,8,8,128]{4,3,2,1,0:T(8,128)S(1)}, u32[]{:S(2)}, u32[]{:S(2)}) collective-permute-start(f32[5,2,8,8,128]{4,3,2,1,0:T(8,128)S(1)} %get-tuple-element.40.outer.refs_2_), channel_id=1, source_target_pairs={{0,1},{1,0},{2,3},{3,2},{4,5},{5,4},{6,7},{7,6},{8,9},{9,8},{10,11... | collective-permute-start | bytes 983048 | tf_op jit(solution)/shard_map/ppermute | solution.py:414
  11.6 3.5 %collective-permute-start.2 = (f32[5,2,8,8,128]{4,3,2,1,0:T(8,128)S(1)}, f32[5,2,8,8,128]{4,3,2,1,0:T(8,128)S(1)}, u32[]{:S(2)}, u32[]{:S(2)}) collective-permute-start(f32[5,2,8,8,128]{4,3,2,1,0:T(8,128)S(1)} %get-tuple-element.41.inner.refs_3_), channel_id=1, source_target_pairs={{0,1},{1,0},{2,3},{3,2},{4,5},{5,4},{6,7},{7,6},{8,9},{9,8},{10,11... | collective-permute-start | bytes 983048 | tf_op jit(solution)/shard_map/ppermute | solution.py:414
  16.4 5.0 %copy-start = (f32[1,5,4,64,128]{4,3,2,1,0:T(8,128)S(1)}, f32[1,5,4,64,128]{4,3,2,1,0:T(8,128)}, u32[]{:S(2)}) copy-start(f32[1,5,4,64,128]{4,3,2,1,0:T(8,128)} %guess.1) | copy-start | bytes 1966084
  16.4 5.0 %copy-start.1 = (f32[4,3,8,128]{3,2,1,0:T(8,128)S(1)}, f32[4,3,8,128]{3,2,1,0:T(8,128)}, u32[]{:S(2)}) copy-start(f32[4,3,8,128]{3,2,1,0:T(8,128)} %constant.10.clone.weights) | copy-start | bytes 147460
  16.4 13.3 %collective-permute-start.3 = (f32[5,4,64,128]{3,2,1,0:T(8,128)S(1)}, f32[5,4,64,128]{3,2,1,0:T(8,128)S(1)}, u32[]{:S(2)}, u32[]{:S(2)}) collective-permute-start(f32[5,4,64,128]{3,2,1,0:T(8,128)S(1)} %bitcast_select_fusion.own), channel_id=1, source_target_pairs={{0,2},{2,4},{4,6},{6,8},{8,10},{10,12},{12,14},{14,16},{16,18},{18... | collective-permute-start | bytes 1966088 | tf_op jit(solution)/shard_map/ppermute | solution.py:417
  19.4 28.9 %collective-permute-start.6 = (f32[5,4,64,128]{3,2,1,0:T(8,128)S(1)}, f32[5,4,64,128]{3,2,1,0:T(8,128)S(1)}, u32[]{:S(2)}, u32[]{:S(2)}) collective-permute-start(f32[5,4,64,128]{3,2,1,0:T(8,128)S(1)} %far.1.own), channel_id=1, source_target_pairs={{0,128},{128,256},{256,384},{384,0},{1,129},{129,257},{257,385},{3... | collective-permute-start | bytes 1966088 | tf_op jit(solution)/shard_map/ppermute | solution.py:434
  21.8 6.6 %collective-permute-start.4 = (f32[5,2,8,8,128]{4,3,2,1,0:T(8,128)S(1)}, f32[5,2,8,8,128]{4,3,2,1,0:T(8,128)S(1)}, u32[]{:S(2)}, u32[]{:S(2)}) collective-permute-start(f32[5,2,8,8,128]{4,3,2,1,0:T(8,128)S(1)} %get-tuple-element.54.outer), channel_id=1, source_target_pairs={{0,1},{1,0},{2,3},{3,2},{4,5},{5,4},{6,7},{7,6},{8,9},{9,8},{10,11... | collective-permute-start | bytes 983048 | tf_op jit(solution)/shard_map/ppermute | solution.py:439
  24.9 3.5 %collective-permute-start.5 = (f32[5,2,8,8,128]{4,3,2,1,0:T(8,128)S(1)}, f32[5,2,8,8,128]{4,3,2,1,0:T(8,128)S(1)}, u32[]{:S(2)}, u32[]{:S(2)}) collective-permute-start(f32[5,2,8,8,128]{4,3,2,1,0:T(8,128)S(1)} %get-tuple-element.55.inner), channel_id=1, source_target_pairs={{0,1},{1,0},{2,3},{3,2},{4,5},{5,4},{6,7},{7,6},{8,9},{9,8},{10,11... | collective-permute-start | bytes 983048 | tf_op jit(solution)/shard_map/ppermute | solution.py:439
  33.7 14.6 %all-to-all-start = ((f32[16,8,128]{2,1,0:T(8,128)}), f32[16,8,128]{2,1,0:T(8,128)S(1)}, u32[]{:S(2)}, u32[]{:S(2)}) async-start(f32[16,8,128]{2,1,0:T(8,128)} %get-tuple-element.74), calls=%async_computation | async-start | bytes 131072 | tf_op jit(solution)/shard_map/all_to_all | solution.py:450
  40.5 21.2 %collective-permute-start.7 = (f32[5,4,64,128]{3,2,1,0:T(8,128)S(1)}, f32[5,4,64,128]{3,2,1,0:T(8,128)S(1)}, u32[]{:S(2)}, u32[]{:S(2)}) collective-permute-start(f32[5,4,64,128]{3,2,1,0:T(8,128)S(1)} %get-tuple-element.75), channel_id=1, source_target_pairs={{0,256},{128,384},{256,0},{384,128},{1,257},{129,385},{257,1},{385... | collective-permute-start | bytes 1966088 | tf_op jit(solution)/shard_map/ppermute | solution.py:449
  49.0 21.6 %all-to-all-start.1 = ((f32[32,2,128]{2,1,0:T(2,128)}), f32[32,2,128]{2,1,0:T(2,128)S(1)}, u32[]{:S(2)}, u32[]{:S(2)}) async-start(f32[32,2,128]{2,1,0:T(2,128)} %bitcast.1), calls=%async_computation.1 | async-start | bytes 65536 | tf_op jit(solution)/shard_map/all_to_all | solution.py:453

commit v6 on v5

--- a/solution.py
+++ b/solution.py
@@ -117,8 +117,12 @@
     return [jnp.sum(jnp.sum(field(k), axis=0), axis=0, keepdims=True) for k in range(COMP)]
 
 
-def prepare_again_kernel(own, guess, weights, outer, inner, source, scale, rest):
-    prepare_rows(own, (outer, inner), source, scale)
+def halves(packed):
+    return packed.at[:, pl.ds(0, 2)], packed.at[:, pl.ds(2, 2)]
+
+
+def prepare_again_kernel(own, guess, weights, packed, source, scale, rest):
+    prepare_rows(own, halves(packed), source, scale)
     slab = lax.axis_index("tm")
     relaxed = packed_sums(field_sums(lambda k: own[k]))
     old = packed_sums(field_sums(lambda k: guess[0, k]))
@@ -127,6 +131,10 @@
 
 def beyond_kernel(*refs):
     near_kernel(*refs, mirrored=False)
+
+
+def near_again_kernel(packed, near, *refs):
+    near_kernel(*halves(packed), *halves(near), *refs)
 
 
 def near_kernel(outer, inner, near_outer, near_inner, source, scale, v1, w2, source2, scale2, v2, near_source, near_scale, v1_more, w2_more, mirrored=True):
@@ -289,7 +297,7 @@
     far_rows(outer, inner, far, source, scale, v1, w2, source2, scale2, v2, work, emit)
 
 
-def far_again_kernel(outer, inner, far, source, scale, v1, w2, source2, scale2, v2, rest, weights, out, share, *work):
+def far_again_kernel(packed, far, source, scale, v1, w2, source2, scale2, v2, rest, weights, out, share, *work):
     nz = out.shape[3]
     total = [jnp.zeros((SUB, nz), jnp.float32) for _ in range(COMP)]
 
@@ -297,7 +305,7 @@
         store_spaced(out, k, row, value)
         total[k] = total[k] + jnp.sum(value, axis=0)
 
-    far_rows(outer, inner, far, source, scale, v1, w2, source2, scale2, v2, work, emit)
+    far_rows(*halves(packed), far, source, scale, v1, w2, source2, scale2, v2, work, emit)
     again = packed_sums([jnp.sum(t, axis=0, keepdims=True) for t in total])
     value = weights[lax.axis_index("tm"), 0] * again + rest[...]
     for i in range(share.shape[0]):
@@ -433,16 +441,23 @@
     )
     my_relaxed = lax.ppermute(relaxed, "tm", [(i, (i + 1) % slabs) for i in range(slabs)])
     weights = slot_weights(slabs, nz, count * rows * ny * BLK)
-    outer, inner, source, scale, rest = call(
-        prepare_again_kernel, "prepare_again", (*prepared, f32(SUB, nz)), (relaxed, guess, weights), (), SHORT
-    )
-    near = [lax.ppermute(half, SPACE, near_pairs) for half in (outer, inner)]
-    kept = call(near_kernel, "near", state, (outer, inner, *near, source, scale), near_scratch, SHORT)
+    packed, source, scale, rest = call(
+        prepare_again_kernel,
+        "prepare_again",
+        (several(COMP, ROWS), *prepared[2:], f32(SUB, nz)),
+        (relaxed, guess, weights),
+        (),
+        SHORT,
+    )
+    near = lax.ppermute(packed, SPACE, near_pairs)
+    kept = call(
+        near_again_kernel, "near_again", state, (packed, near, source, scale), near_scratch, SHORT
+    )
     again, share = call(
         far_again_kernel,
         "far_again",
         (f32(*own.shape), f32(GROUP, SUB, nz)),
-        (outer, inner, far, source, scale, *kept, rest, weights),
+        (packed, far, source, scale, *kept, rest, weights),
         far_scratch,
     )
 

time: 72 us -> 70.6 us (0.981)
  starting transfers between devices: 44 us -> 41.3 us
  waiting for transfers between devices: 12.7 us -> 14.2 us
    ppermute x4 -> x2, starting transfers between devices: 11.9 us -> 6.82 us  [per_device(): near = [lax.ppermute(half, SPACE, near_pairs) for half in (outer, inner)]]
    ppermute x0 -> x1, starting transfers between devices: none -> 2.08 us  [per_device(): near = lax.ppermute(packed, SPACE, near_pairs)]
    ppermute x1, waiting for transfers between devices: 0.01 us -> 1.67 us  [per_device(): farther = lax.ppermute(held, SPACE, farther_pairs)]
    ppermute x1, starting transfers between devices: 1.92 us -> 2.7 us  [per_device(): lax.ppermute(relaxed, 'tm', [(i, (i + 1) % slabs) for i in range(slabs)])]
    ppermute x4 -> x2, waiting for transfers between devices: 1.63 us -> 1.59 us  [per_device(): near = [lax.ppermute(half, SPACE, near_pairs) for half in (outer, inner)]]
  transfers between devices with their start and end apart: 10 -> 9, of which waited for: 3 -> 4; matrix products, arithmetic and copies ran while one was open for 0% -> 0% of each run, Pallas kernels for 17% -> 17%
where the time goes in v6:
time: 70.6 us; the launch traced here: 70.2 us
  starting transfers between devices  41.3 us (58%)
  waiting for transfers between devices  14.2 us (20%)
  Pallas kernels  12.7 us (18%)
  other arithmetic  1.18 us (2%)
  between operations  0.84 us (1%)
    all_to_all x1, starting transfers between devices, per_device(): lax.all_to_all(share.reshape(wide, 2, nz), ('tm', 'outer'), 0, 0)  12.9 us
    pallas_call x12, Pallas kernels, call(): pl.pallas_call(kernel, out_shape=out, in_specs=[vmem] * len(inputs), out_...  12.7 us
    all_to_all x1, waiting for transfers between devices, per_device(): lax.all_to_all(share.reshape(wide, 2, nz), ('tm', 'outer'), 0, 0)  7.85 us
    ppermute x2, starting transfers between devices, per_device(): near = [lax.ppermute(half, SPACE, near_pairs) for half in (outer, inner)]  6.82 us
    all_to_all x1, starting transfers between devices, per_device(): parts = lax.all_to_all(share, 'inner', 0, 0)  6.1 us
    ppermute x1, starting transfers between devices, per_device(): lax.ppermute(again, 'tm', [(i, (i + 2) % slabs) for i in range(slabs)])  4.67 us
    ppermute x1, starting transfers between devices, per_device(): far = lax.ppermute(start, SPACE, far_pairs)  4.59 us
    all_to_all x1, waiting for transfers between devices, per_device(): parts = lax.all_to_all(share, 'inner', 0, 0)  3.12 us
  transfers between devices with their start and end apart: 9, of which 4 were waited for; matrix products, arithmetic and copies ran while one was open for 0% of the time, Pallas kernels for 17%

profile of v6, /device:TPU:1, one launch (start us, length us, event | category | flops | bytes accessed | tf_op | source)
XLA Modules:
  0.0 70.2 jit_solution(8645175471588290883)
XLA Ops:
  0.6 1.2 %bitcast_select_fusion.own = f32[5,4,64,128]{3,2,1,0:T(8,128)S(1)} fusion(f32[5,4,64,128]{3,2,1,0:T(8,128)} %param.3, f32[1,5,4,64,128]{4,3,2,1,0:T(8,128)} %guess.1, pred[]{:T(512)S(6)} %eq.3), kind=kLoop, calls=%fused_computation | loop fusion | flops 163840 | bytes 1966081 | tf_op jit(solution)/shard_map/jit(_where)/select_n | solution.py:419
  1.8 4.6 %collective-permute-start = (f32[5,4,64,128]{3,2,1,0:T(8,128)S(1)}, f32[5,4,64,128]{3,2,1,0:T(8,128)S(1)}, u32[]{:S(2)}, u32[]{:S(2)}) collective-permute-start(f32[5,4,64,128]{3,2,1,0:T(8,128)S(1)} %bitcast_select_fusion.own), channel_id=1, source_target_pairs={{1,2},{2,1},{3,4},{4,3},{5,6},{6,5},{7,8},{8,7},{9,10},{10,9},{11,... | collective-permute-start | bytes 1966088 | tf_op jit(solution)/shard_map/ppermute | solution.py:420
  6.4 0.3 prepare.1
  6.7 4.9 %collective-permute-start.1 = (f32[5,2,8,8,128]{4,3,2,1,0:T(8,128)S(1)}, f32[5,2,8,8,128]{4,3,2,1,0:T(8,128)S(1)}, u32[]{:S(2)}, u32[]{:S(2)}) collective-permute-start(f32[5,2,8,8,128]{4,3,2,1,0:T(8,128)S(1)} %get-tuple-element.39.outer.refs_2_), channel_id=1, source_target_pairs={{0,1},{1,0},{2,3},{3,2},{4,5},{5,4},{6,7},{7,6},{8,9},{9,8},{10,11... | collective-permute-start | bytes 983048 | tf_op jit(solution)/shard_map/ppermute | solution.py:422
  11.6 1.9 %collective-permute-start.2 = (f32[5,2,8,8,128]{4,3,2,1,0:T(8,128)S(1)}, f32[5,2,8,8,128]{4,3,2,1,0:T(8,128)S(1)}, u32[]{:S(2)}, u32[]{:S(2)}) collective-permute-start(f32[5,2,8,8,128]{4,3,2,1,0:T(8,128)S(1)} %get-tuple-element.40.inner.refs_3_), channel_id=1, source_target_pairs={{0,1},{1,0},{2,3},{3,2},{4,5},{5,4},{6,7},{7,6},{8,9},{9,8},{10,11... | collective-permute-start | bytes 983048 | tf_op jit(solution)/shard_map/ppermute | solution.py:422
  13.6 0.0 collective-permute-done.1.near_outer
  13.6 1.6 %collective-permute-done.2.near_inner = f32[5,2,8,8,128]{4,3,2,1,0:T(8,128)S(1)} collective-permute-done((f32[5,2,8,8,128]{4,3,2,1,0:T(8,128)S(1)}, f32[5,2,8,8,128]{4,3,2,1,0:T(8,128)S(1)}, u32[]{:S(2)}, u32[]{:S(2)}) %collective-permute-start.2) | collective-permute-done | bytes 327712 | tf_op jit(solution)/shard_map/ppermute | solution.py:422
  15.2 1.2 %near.1 = (f32[5,2,8,8,128]{4,3,2,1,0:T(8,128)S(1)}, f32[5,2,8,8,128]{4,3,2,1,0:T(8,128)S(1)}, f32[5,2,8,8,128]{4,3,2,1,0:T(8,128)S(1)}, f32[2,8,8,128]{3,2,1,0:T(8,128)S(1)}, f32[5,2,8,8,128]{4,3,2,1,0:T(8,128)S(1)}) custom-call(f32[5,2,8,8,128]{4,3,2,1,0:T(8,128)S(1)} %get-tuple-element.39.outer.refs_2_, ...), custom_call_target="tpu_custom_call" | custom-call | tf_op jit(solution)/shard_map/near/pallas_call | solution.py:374
  16.4 0.0 copy-start
  16.4 0.0 copy-start.1
  16.4 1.4 %collective-permute-start.3 = (f32[5,4,64,128]{3,2,1,0:T(8,128)S(1)}, f32[5,4,64,128]{3,2,1,0:T(8,128)S(1)}, u32[]{:S(2)}, u32[]{:S(2)}) collective-permute-start(f32[5,4,64,128]{3,2,1,0:T(8,128)S(1)} %bitcast_select_fusion.own), channel_id=1, source_target_pairs={{0,2},{2,4},{4,6},{6,8},{8,10},{10,12},{12,14},{14,16},{16,18},{18... | collective-permute-start | bytes 1966088 | tf_op jit(solution)/shard_map/ppermute | solution.py:425
  17.9 0.0 collective-permute-done.far.own
  17.9 1.6 %far.1.own = f32[5,4,64,128]{3,2,1,0:T(8,128)S(1)} custom-call(f32[5,2,8,8,128]{4,3,2,1,0:T(8,128)S(1)} %get-tuple-element.39.outer.refs_2_, f32[5,2,8,8,128]{4,3,2,1,0:T(8,128)S(1)} %get-tuple-element.40.inner.refs_3_, f32[5,4,64,128]{3,2,1,0:T(8,128)S(1)} %collective-permute-done.far.own, f32[5,4,8,8,128]{4,3,2,1,0:T(8,128)S(1)} %get-tuple-element.41.source, ...), custom_call_target="tpu_custom_call" | custom-call | tf_op jit(solution)/shard_map/far/pallas_call | solution.py:374
  19.4 0.0 copy-done
  19.4 0.0 copy-done.1
  19.4 0.4 prepare_again.1
  19.9 2.1 %collective-permute-start.4 = (f32[5,4,8,8,128]{4,3,2,1,0:T(8,128)S(1)}, f32[5,4,8,8,128]{4,3,2,1,0:T(8,128)S(1)}, u32[]{:S(2)}, u32[]{:S(2)}) collective-permute-start(f32[5,4,8,8,128]{4,3,2,1,0:T(8,128)S(1)} %get-tuple-element.53.packed), channel_id=1, source_target_pairs={{0,1},{1,0},{2,3},{3,2},{4,5},{5,4},{6,7},{7,6},{8,9},{9,8},{10,11... | collective-permute-start | bytes 1966088 | tf_op jit(solution)/shard_map/ppermute | solution.py:452
  22.0 2.7 %collective-permute-start.5 = (f32[5,4,64,128]{3,2,1,0:T(8,128)S(1)}, f32[5,4,64,128]{3,2,1,0:T(8,128)S(1)}, u32[]{:S(2)}, u32[]{:S(2)}) collective-permute-start(f32[5,4,64,128]{3,2,1,0:T(8,128)S(1)} %far.1.own), channel_id=1, source_target_pairs={{0,128},{128,256},{256,384},{384,0},{1,129},{129,257},{257,385},{3... | collective-permute-start | bytes 1966088 | tf_op jit(solution)/shard_map/ppermute | solution.py:442
  24.7 0.3 prepare_far.1
  25.0 1.2 %beyond.1 = (f32[5,2,8,8,128]{4,3,2,1,0:T(8,128)S(1)}, f32[5,2,8,8,128]{4,3,2,1,0:T(8,128)S(1)}, f32[5,2,8,8,128]{4,3,2,1,0:T(8,128)S(1)}, f32[2,8,8,128]{3,2,1,0:T(8,128)S(1)}, f32[5,2,8,8,128]{4,3,2,1,0:T(8,128)S(1)}) custom-call(f32[5,2,8,8,128]{4,3,2,1,0:T(8,128)S(1)} %get-tuple-element.54.refs_0_.outer, ...), custom_call_target="tpu_custom_call" | custom-call | tf_op jit(solution)/shard_map/beyond/pallas_call | solution.py:374
  26.2 1.7 %collective-permute-done.3.far = f32[5,4,64,128]{3,2,1,0:T(8,128)S(1)} collective-permute-done((f32[5,4,64,128]{3,2,1,0:T(8,128)S(1)}, f32[5,4,64,128]{3,2,1,0:T(8,128)S(1)}, u32[]{:S(2)}, u32[]{:S(2)}) %collective-permute-start.3) | collective-permute-done | bytes 655392 | tf_op jit(solution)/shard_map/ppermute | solution.py:425
  27.9 1.5 %far_relaxed.1.far = f32[5,4,64,128]{3,2,1,0:T(8,128)S(1)} custom-call(f32[5,2,8,8,128]{4,3,2,1,0:T(8,128)S(1)} %get-tuple-element.54.refs_0_.outer, f32[5,2,8,8,128]{4,3,2,1,0:T(8,128)S(1)} %get-tuple-element.55.refs_1_.inner, f32[5,4,64,128]{3,2,1,0:T(8,128)S(1)} %collective-permute-done.3.far, f32[5,4,8,8,128]{4,3,2,1,0:T(8,128)S(1)} %get-tuple-element.57.refs_4_.source, ...), custom_call_target="tpu_custom_call" | custom-call | tf_op jit(solution)/shard_map/far_relaxed/pallas_call | solution.py:374
  29.4 0.0 collective-permute-done.4.near
  29.4 1.2 %near_again.1 = (f32[5,2,8,8,128]{4,3,2,1,0:T(8,128)S(1)}, f32[5,2,8,8,128]{4,3,2,1,0:T(8,128)S(1)}, f32[5,2,8,8,128]{4,3,2,1,0:T(8,128)S(1)}, f32[2,8,8,128]{3,2,1,0:T(8,128)S(1)}, f32[5,2,8,8,128]{4,3,2,1,0:T(8,128)S(1)}) custom-call(f32[5,4,8,8,128]{4,3,2,1,0:T(8,128)S(1)} %get-tuple-element.53.packed, ...), custom_call_target="tpu_custom_call" | custom-call | tf_op jit(solution)/shard_map/near_again/pallas_call | solution.py:374
  30.7 2.4 %far_again.1 = (f32[5,4,64,128]{3,2,1,0:T(8,128)S(1)}, f32[16,8,128]{2,1,0:T(8,128)}) custom-call(f32[5,4,8,8,128]{4,3,2,1,0:T(8,128)S(1)} %get-tuple-element.53.packed, f32[5,4,64,128]{3,2,1,0:T(8,128)S(1)} %far_relaxed.1.far, f32[5,4,8,8,128]{4,3,2,1,0:T(8,128)S(1)} %get-tuple-element.64.refs_0_.source, ...), custom_call_target="tpu_custom_call" | custom-call | tf_op jit(solution)/shard_map/far_again/pallas_call | solution.py:374
  33.0 6.1 %all-to-all-start = ((f32[16,8,128]{2,1,0:T(8,128)}), f32[16,8,128]{2,1,0:T(8,128)S(1)}, u32[]{:S(2)}, u32[]{:S(2)}) async-start(f32[16,8,128]{2,1,0:T(8,128)} %get-tuple-element.72), calls=%async_computation | async-start | bytes 131072 | tf_op jit(solution)/shard_map/all_to_all | solution.py:465
  39.1 4.7 %collective-permute-start.6 = (f32[5,4,64,128]{3,2,1,0:T(8,128)S(1)}, f32[5,4,64,128]{3,2,1,0:T(8,128)S(1)}, u32[]{:S(2)}, u32[]{:S(2)}) collective-permute-start(f32[5,4,64,128]{3,2,1,0:T(8,128)S(1)} %get-tuple-element.73), channel_id=1, source_target_pairs={{0,256},{128,384},{256,0},{384,128},{1,257},{129,385},{257,1},{385... | collective-permute-start | bytes 1966088 | tf_op jit(solution)/shard_map/ppermute | solution.py:464
  43.8 0.0 collective-permute-done.5.relaxed
  43.8 3.1 %all-to-all-done.parts = f32[16,8,128]{2,1,0:T(8,128)S(1)} async-done(((f32[16,8,128]{2,1,0:T(8,128)}), f32[16,8,128]{2,1,0:T(8,128)S(1)}, u32[]{:S(2)}, u32[]{:S(2)}) %all-to-all-start) | async-done | bytes 65568 | tf_op jit(solution)/shard_map/all_to_all | solution.py:465
  47.0 0.6 relay.1
  47.6 12.9 %all-to-all-start.1 = ((f32[32,2,128]{2,1,0:T(2,128)}), f32[32,2,128]{2,1,0:T(2,128)S(1)}, u32[]{:S(2)}, u32[]{:S(2)}) async-start(f32[32,2,128]{2,1,0:T(2,128)} %bitcast.1), calls=%async_computation.1 | async-start | bytes 65536 | tf_op jit(solution)/shard_map/all_to_all | solution.py:468
  60.5 0.0 collective-permute-done.6.again
  60.5 0.9 %residual.1 = (f32[1,5,4,64,128]{4,3,2,1,0:T(8,128)}, f32[8,128]{1,0:T(8,128)S(1)}) custom-call(f32[5,4,64,128]{3,2,1,0:T(8,128)S(1)} %collective-permute-done.5.relaxed, f32[5,4,64,128]{3,2,1,0:T(8,128)S(1)} %collective-permute-done.6.again), custom_call_target="tpu_custom_call" | custom-call | tf_op jit(solution)/shard_map/residual/pallas_call | solution.py:374
  61.4 7.8 %all-to-all-done.1 = f32[32,2,128]{2,1,0:T(2,128)S(1)} async-done(((f32[32,2,128]{2,1,0:T(2,128)}), f32[32,2,128]{2,1,0:T(2,128)S(1)}, u32[]{:S(2)}, u32[]{:S(2)}) %all-to-all-start.1) | async-done | bytes 32800 | tf_op jit(solution)/shard_map/all_to_all | solution.py:468
  69.2 1.0 %correct.1 = f32[1,5,4,64,128]{4,3,2,1,0:T(8,128)} custom-call(f32[64,128]{1,0:T(8,128)S(1)} %bitcast.4, f32[5,4,64,128]{3,2,1,0:T(8,128)S(1)} %collective-permute-done.5.relaxed, f32[8,128]{1,0:T(8,128)S(1)} %get-tuple-element.74.written), custom_call_target="tpu_custom_call" | custom-call | tf_op jit(solution)/shard_map/correct/pallas_call | solution.py:374
Async XLA Ops:
  1.8 16.0 %collective-permute-start = (f32[5,4,64,128]{3,2,1,0:T(8,128)S(1)}, f32[5,4,64,128]{3,2,1,0:T(8,128)S(1)}, u32[]{:S(2)}, u32[]{:S(2)}) collective-permute-start(f32[5,4,64,128]{3,2,1,0:T(8,128)S(1)} %bitcast_select_fusion.own), channel_id=1, source_target_pairs={{1,2},{2,1},{3,4},{4,3},{5,6},{6,5},{7,8},{8,7},{9,10},{10,9},{11,... | collective-permute-start | bytes 1966088 | tf_op jit(solution)/shard_map/ppermute | solution.py:420
  6.7 6.8 %collective-permute-start.1 = (f32[5,2,8,8,128]{4,3,2,1,0:T(8,128)S(1)}, f32[5,2,8,8,128]{4,3,2,1,0:T(8,128)S(1)}, u32[]{:S(2)}, u32[]{:S(2)}) collective-permute-start(f32[5,2,8,8,128]{4,3,2,1,0:T(8,128)S(1)} %get-tuple-element.39.outer.refs_2_), channel_id=1, source_target_pairs={{0,1},{1,0},{2,3},{3,2},{4,5},{5,4},{6,7},{7,6},{8,9},{9,8},{10,11... | collective-permute-start | bytes 983048 | tf_op jit(solution)/shard_map/ppermute | solution.py:422
  11.6 3.5 %collective-permute-start.2 = (f32[5,2,8,8,128]{4,3,2,1,0:T(8,128)S(1)}, f32[5,2,8,8,128]{4,3,2,1,0:T(8,128)S(1)}, u32[]{:S(2)}, u32[]{:S(2)}) collective-permute-start(f32[5,2,8,8,128]{4,3,2,1,0:T(8,128)S(1)} %get-tuple-element.40.inner.refs_3_), channel_id=1, source_target_pairs={{0,1},{1,0},{2,3},{3,2},{4,5},{5,4},{6,7},{7,6},{8,9},{9,8},{10,11... | collective-permute-start | bytes 983048 | tf_op jit(solution)/shard_map/ppermute | solution.py:422
  16.4 3.0 %copy-start = (f32[1,5,4,64,128]{4,3,2,1,0:T(8,128)S(1)}, f32[1,5,4,64,128]{4,3,2,1,0:T(8,128)}, u32[]{:S(2)}) copy-start(f32[1,5,4,64,128]{4,3,2,1,0:T(8,128)} %guess.1) | copy-start | bytes 1966084
  16.4 3.0 %copy-start.1 = (f32[4,3,8,128]{3,2,1,0:T(8,128)S(1)}, f32[4,3,8,128]{3,2,1,0:T(8,128)}, u32[]{:S(2)}) copy-start(f32[4,3,8,128]{3,2,1,0:T(8,128)} %constant.10.clone.weights) | copy-start | bytes 147460
  16.4 11.5 %collective-permute-start.3 = (f32[5,4,64,128]{3,2,1,0:T(8,128)S(1)}, f32[5,4,64,128]{3,2,1,0:T(8,128)S(1)}, u32[]{:S(2)}, u32[]{:S(2)}) collective-permute-start(f32[5,4,64,128]{3,2,1,0:T(8,128)S(1)} %bitcast_select_fusion.own), channel_id=1, source_target_pairs={{0,2},{2,4},{4,6},{6,8},{8,10},{10,12},{12,14},{14,16},{16,18},{18... | collective-permute-start | bytes 1966088 | tf_op jit(solution)/shard_map/ppermute | solution.py:425
  19.9 9.6 %collective-permute-start.4 = (f32[5,4,8,8,128]{4,3,2,1,0:T(8,128)S(1)}, f32[5,4,8,8,128]{4,3,2,1,0:T(8,128)S(1)}, u32[]{:S(2)}, u32[]{:S(2)}) collective-permute-start(f32[5,4,8,8,128]{4,3,2,1,0:T(8,128)S(1)} %get-tuple-element.53.packed), channel_id=1, source_target_pairs={{0,1},{1,0},{2,3},{3,2},{4,5},{5,4},{6,7},{7,6},{8,9},{9,8},{10,11... | collective-permute-start | bytes 1966088 | tf_op jit(solution)/shard_map/ppermute | solution.py:452
  22.0 21.9 %collective-permute-start.5 = (f32[5,4,64,128]{3,2,1,0:T(8,128)S(1)}, f32[5,4,64,128]{3,2,1,0:T(8,128)S(1)}, u32[]{:S(2)}, u32[]{:S(2)}) collective-permute-start(f32[5,4,64,128]{3,2,1,0:T(8,128)S(1)} %far.1.own), channel_id=1, source_target_pairs={{0,128},{128,256},{256,384},{384,0},{1,129},{129,257},{257,385},{3... | collective-permute-start | bytes 1966088 | tf_op jit(solution)/shard_map/ppermute | solution.py:442
  33.0 13.9 %all-to-all-start = ((f32[16,8,128]{2,1,0:T(8,128)}), f32[16,8,128]{2,1,0:T(8,128)S(1)}, u32[]{:S(2)}, u32[]{:S(2)}) async-start(f32[16,8,128]{2,1,0:T(8,128)} %get-tuple-element.72), calls=%async_computation | async-start | bytes 131072 | tf_op jit(solution)/shard_map/all_to_all | solution.py:465
  39.1 21.3 %collective-permute-start.6 = (f32[5,4,64,128]{3,2,1,0:T(8,128)S(1)}, f32[5,4,64,128]{3,2,1,0:T(8,128)S(1)}, u32[]{:S(2)}, u32[]{:S(2)}) collective-permute-start(f32[5,4,64,128]{3,2,1,0:T(8,128)S(1)} %get-tuple-element.73), channel_id=1, source_target_pairs={{0,256},{128,384},{256,0},{384,128},{1,257},{129,385},{257,1},{385... | collective-permute-start | bytes 1966088 | tf_op jit(solution)/shard_map/ppermute | solution.py:464
  47.6 21.7 %all-to-all-start.1 = ((f32[32,2,128]{2,1,0:T(2,128)}), f32[32,2,128]{2,1,0:T(2,128)S(1)}, u32[]{:S(2)}, u32[]{:S(2)}) async-start(f32[32,2,128]{2,1,0:T(2,128)} %bitcast.1), calls=%async_computation.1 | async-start | bytes 65536 | tf_op jit(solution)/shard_map/all_to_all | solution.py:468

commit v7 on v6

--- a/solution.py
+++ b/solution.py
@@ -420,8 +420,8 @@
     far = lax.ppermute(start, SPACE, far_pairs)
     outer, inner, source, scale = call(prepare_kernel, "prepare", prepared, (start,))
     near = [lax.ppermute(half, SPACE, near_pairs) for half in (outer, inner)]
+    held, near = lax.optimization_barrier((start, near))
     kept = call(near_kernel, "near", state, (outer, inner, *near, source, scale), near_scratch, SHORT)
-    held, kept = lax.optimization_barrier((start, kept))
     farther = lax.ppermute(held, SPACE, farther_pairs)
     relaxed = call(
         far_kernel, "far", f32(*own.shape), (outer, inner, far, source, scale, *kept), far_scratch, SHORT

time: 70.6 us -> 70 us (level)
  waiting for transfers between devices: 14.2 us -> 13.1 us
    ppermute x1, waiting for transfers between devices: 1.67 us -> 0.41 us  [per_device(): farther = lax.ppermute(held, SPACE, farther_pairs)]
    all_to_all x1, starting transfers between devices: 6.1 us -> 6.91 us  [per_device(): parts = lax.all_to_all(share, 'inner', 0, 0)]
where the time goes in v7:
time: 70 us; the launch traced here: 69.5 us
  starting transfers between devices  41.7 us (60%)
  waiting for transfers between devices  13.1 us (19%)
  Pallas kernels  12.7 us (18%)
  other arithmetic  1.18 us (2%)
  between operations  0.84 us (1%)
    all_to_all x1, starting transfers between devices, per_device(): lax.all_to_all(share.reshape(wide, 2, nz), ('tm', 'outer'), 0, 0)  12.8 us
    pallas_call x12, Pallas kernels, call(): pl.pallas_call(kernel, out_shape=out, in_specs=[vmem] * len(inputs), out_...  12.7 us
    all_to_all x1, waiting for transfers between devices, per_device(): lax.all_to_all(share.reshape(wide, 2, nz), ('tm', 'outer'), 0, 0)  7.85 us
    all_to_all x1, starting transfers between devices, per_device(): parts = lax.all_to_all(share, 'inner', 0, 0)  6.91 us
    ppermute x2, starting transfers between devices, per_device(): near = [lax.ppermute(half, SPACE, near_pairs) for half in (outer, inner)]  6.82 us
    ppermute x1, starting transfers between devices, per_device(): far = lax.ppermute(start, SPACE, far_pairs)  4.59 us
    ppermute x1, starting transfers between devices, per_device(): lax.ppermute(again, 'tm', [(i, (i + 2) % slabs) for i in range(slabs)])  4.57 us
    all_to_all x1, waiting for transfers between devices, per_device(): parts = lax.all_to_all(share, 'inner', 0, 0)  3.22 us
  transfers between devices with their start and end apart: 9, of which 4 were waited for; matrix products, arithmetic and copies ran while one was open for 0% of the time, Pallas kernels for 17%

profile of v7, /device:TPU:1, one launch (start us, length us, event | category | flops | bytes accessed | tf_op | source)
XLA Modules:
  0.0 69.5 jit_solution(15648331325809616678)
XLA Ops:
  0.6 1.2 %bitcast_select_fusion.own = f32[5,4,64,128]{3,2,1,0:T(8,128)S(1)} fusion(f32[5,4,64,128]{3,2,1,0:T(8,128)} %param.3, f32[1,5,4,64,128]{4,3,2,1,0:T(8,128)} %guess.1, pred[]{:T(512)S(6)} %eq.3), kind=kLoop, calls=%fused_computation | loop fusion | flops 163840 | bytes 1966081 | tf_op jit(solution)/shard_map/jit(_where)/select_n | solution.py:419
  1.8 4.6 %collective-permute-start = (f32[5,4,64,128]{3,2,1,0:T(8,128)S(1)}, f32[5,4,64,128]{3,2,1,0:T(8,128)S(1)}, u32[]{:S(2)}, u32[]{:S(2)}) collective-permute-start(f32[5,4,64,128]{3,2,1,0:T(8,128)S(1)} %bitcast_select_fusion.own), channel_id=1, source_target_pairs={{1,2},{2,1},{3,4},{4,3},{5,6},{6,5},{7,8},{8,7},{9,10},{10,9},{11,... | collective-permute-start | bytes 1966088 | tf_op jit(solution)/shard_map/ppermute | solution.py:420
  6.4 0.3 prepare.1
  6.7 4.9 %collective-permute-start.1 = (f32[5,2,8,8,128]{4,3,2,1,0:T(8,128)S(1)}, f32[5,2,8,8,128]{4,3,2,1,0:T(8,128)S(1)}, u32[]{:S(2)}, u32[]{:S(2)}) collective-permute-start(f32[5,2,8,8,128]{4,3,2,1,0:T(8,128)S(1)} %get-tuple-element.36.outer.refs_2_), channel_id=1, source_target_pairs={{0,1},{1,0},{2,3},{3,2},{4,5},{5,4},{6,7},{7,6},{8,9},{9,8},{10,11... | collective-permute-start | bytes 983048 | tf_op jit(solution)/shard_map/ppermute | solution.py:422
  11.6 1.9 %collective-permute-start.2 = (f32[5,2,8,8,128]{4,3,2,1,0:T(8,128)S(1)}, f32[5,2,8,8,128]{4,3,2,1,0:T(8,128)S(1)}, u32[]{:S(2)}, u32[]{:S(2)}) collective-permute-start(f32[5,2,8,8,128]{4,3,2,1,0:T(8,128)S(1)} %get-tuple-element.37.inner.refs_3_), channel_id=1, source_target_pairs={{0,1},{1,0},{2,3},{3,2},{4,5},{5,4},{6,7},{7,6},{8,9},{9,8},{10,11... | collective-permute-start | bytes 983048 | tf_op jit(solution)/shard_map/ppermute | solution.py:422
  13.6 0.0 collective-permute-done.1.near_outer
  13.6 1.6 %collective-permute-done.2.near_inner = f32[5,2,8,8,128]{4,3,2,1,0:T(8,128)S(1)} collective-permute-done((f32[5,2,8,8,128]{4,3,2,1,0:T(8,128)S(1)}, f32[5,2,8,8,128]{4,3,2,1,0:T(8,128)S(1)}, u32[]{:S(2)}, u32[]{:S(2)}) %collective-permute-start.2) | collective-permute-done | bytes 327712 | tf_op jit(solution)/shard_map/ppermute | solution.py:422
  15.2 1.3 %collective-permute-start.3 = (f32[5,4,64,128]{3,2,1,0:T(8,128)S(1)}, f32[5,4,64,128]{3,2,1,0:T(8,128)S(1)}, u32[]{:S(2)}, u32[]{:S(2)}) collective-permute-start(f32[5,4,64,128]{3,2,1,0:T(8,128)S(1)} %bitcast_select_fusion.own), channel_id=1, source_target_pairs={{0,2},{2,4},{4,6},{6,8},{8,10},{10,12},{12,14},{14,16},{16,18},{18... | collective-permute-start | bytes 1966088 | tf_op jit(solution)/shard_map/ppermute | solution.py:425
  16.5 1.2 %near.1 = (f32[5,2,8,8,128]{4,3,2,1,0:T(8,128)S(1)}, f32[5,2,8,8,128]{4,3,2,1,0:T(8,128)S(1)}, f32[5,2,8,8,128]{4,3,2,1,0:T(8,128)S(1)}, f32[2,8,8,128]{3,2,1,0:T(8,128)S(1)}, f32[5,2,8,8,128]{4,3,2,1,0:T(8,128)S(1)}) custom-call(f32[5,2,8,8,128]{4,3,2,1,0:T(8,128)S(1)} %get-tuple-element.36.outer.refs_2_, ...), custom_call_target="tpu_custom_call" | custom-call | tf_op jit(solution)/shard_map/near/pallas_call | solution.py:374
  17.7 0.0 collective-permute-done.far.own
  17.7 0.0 copy-start
  17.7 0.0 copy-start.1
  17.7 1.6 %far.1.own = f32[5,4,64,128]{3,2,1,0:T(8,128)S(1)} custom-call(f32[5,2,8,8,128]{4,3,2,1,0:T(8,128)S(1)} %get-tuple-element.36.outer.refs_2_, f32[5,2,8,8,128]{4,3,2,1,0:T(8,128)S(1)} %get-tuple-element.37.inner.refs_3_, f32[5,4,64,128]{3,2,1,0:T(8,128)S(1)} %collective-permute-done.far.own, f32[5,4,8,8,128]{4,3,2,1,0:T(8,128)S(1)} %get-tuple-element.38.source, ...), custom_call_target="tpu_custom_call" | custom-call | tf_op jit(solution)/shard_map/far/pallas_call | solution.py:374
  19.3 0.0 copy-done
  19.3 0.0 copy-done.1
  19.3 0.4 prepare_again.1
  19.7 2.1 %collective-permute-start.4 = (f32[5,4,8,8,128]{4,3,2,1,0:T(8,128)S(1)}, f32[5,4,8,8,128]{4,3,2,1,0:T(8,128)S(1)}, u32[]{:S(2)}, u32[]{:S(2)}) collective-permute-start(f32[5,4,8,8,128]{4,3,2,1,0:T(8,128)S(1)} %get-tuple-element.47.packed), channel_id=1, source_target_pairs={{0,1},{1,0},{2,3},{3,2},{4,5},{5,4},{6,7},{7,6},{8,9},{9,8},{10,11... | collective-permute-start | bytes 1966088 | tf_op jit(solution)/shard_map/ppermute | solution.py:452
  21.8 2.7 %collective-permute-start.5 = (f32[5,4,64,128]{3,2,1,0:T(8,128)S(1)}, f32[5,4,64,128]{3,2,1,0:T(8,128)S(1)}, u32[]{:S(2)}, u32[]{:S(2)}) collective-permute-start(f32[5,4,64,128]{3,2,1,0:T(8,128)S(1)} %far.1.own), channel_id=1, source_target_pairs={{0,128},{128,256},{256,384},{384,0},{1,129},{129,257},{257,385},{3... | collective-permute-start | bytes 1966088 | tf_op jit(solution)/shard_map/ppermute | solution.py:442
  24.5 0.3 prepare_far.1
  24.8 1.2 %beyond.1 = (f32[5,2,8,8,128]{4,3,2,1,0:T(8,128)S(1)}, f32[5,2,8,8,128]{4,3,2,1,0:T(8,128)S(1)}, f32[5,2,8,8,128]{4,3,2,1,0:T(8,128)S(1)}, f32[2,8,8,128]{3,2,1,0:T(8,128)S(1)}, f32[5,2,8,8,128]{4,3,2,1,0:T(8,128)S(1)}) custom-call(f32[5,2,8,8,128]{4,3,2,1,0:T(8,128)S(1)} %get-tuple-element.48.refs_0_.outer, ...), custom_call_target="tpu_custom_call" | custom-call | tf_op jit(solution)/shard_map/beyond/pallas_call | solution.py:374
  26.1 0.4 collective-permute-done.3.far
  26.5 1.5 %far_relaxed.1.far = f32[5,4,64,128]{3,2,1,0:T(8,128)S(1)} custom-call(f32[5,2,8,8,128]{4,3,2,1,0:T(8,128)S(1)} %get-tuple-element.48.refs_0_.outer, f32[5,2,8,8,128]{4,3,2,1,0:T(8,128)S(1)} %get-tuple-element.49.refs_1_.inner, f32[5,4,64,128]{3,2,1,0:T(8,128)S(1)} %collective-permute-done.3.far, f32[5,4,8,8,128]{4,3,2,1,0:T(8,128)S(1)} %get-tuple-element.51.refs_4_.source, ...), custom_call_target="tpu_custom_call" | custom-call | tf_op jit(solution)/shard_map/far_relaxed/pallas_call | solution.py:374
  28.0 0.0 collective-permute-done.4.near
  28.0 1.2 %near_again.1 = (f32[5,2,8,8,128]{4,3,2,1,0:T(8,128)S(1)}, f32[5,2,8,8,128]{4,3,2,1,0:T(8,128)S(1)}, f32[5,2,8,8,128]{4,3,2,1,0:T(8,128)S(1)}, f32[2,8,8,128]{3,2,1,0:T(8,128)S(1)}, f32[5,2,8,8,128]{4,3,2,1,0:T(8,128)S(1)}) custom-call(f32[5,4,8,8,128]{4,3,2,1,0:T(8,128)S(1)} %get-tuple-element.47.packed, ...), custom_call_target="tpu_custom_call" | custom-call | tf_op jit(solution)/shard_map/near_again/pallas_call | solution.py:374
  29.3 2.4 %far_again.1 = (f32[5,4,64,128]{3,2,1,0:T(8,128)S(1)}, f32[16,8,128]{2,1,0:T(8,128)}) custom-call(f32[5,4,8,8,128]{4,3,2,1,0:T(8,128)S(1)} %get-tuple-element.47.packed, f32[5,4,64,128]{3,2,1,0:T(8,128)S(1)} %far_relaxed.1.far, f32[5,4,8,8,128]{4,3,2,1,0:T(8,128)S(1)} %get-tuple-element.58.refs_0_.source, ...), custom_call_target="tpu_custom_call" | custom-call | tf_op jit(solution)/shard_map/far_again/pallas_call | solution.py:374
  31.7 6.9 %all-to-all-start = ((f32[16,8,128]{2,1,0:T(8,128)}), f32[16,8,128]{2,1,0:T(8,128)S(1)}, u32[]{:S(2)}, u32[]{:S(2)}) async-start(f32[16,8,128]{2,1,0:T(8,128)} %get-tuple-element.66), calls=%async_computation | async-start | bytes 131072 | tf_op jit(solution)/shard_map/all_to_all | solution.py:465
  38.6 4.6 %collective-permute-start.6 = (f32[5,4,64,128]{3,2,1,0:T(8,128)S(1)}, f32[5,4,64,128]{3,2,1,0:T(8,128)S(1)}, u32[]{:S(2)}, u32[]{:S(2)}) collective-permute-start(f32[5,4,64,128]{3,2,1,0:T(8,128)S(1)} %get-tuple-element.67), channel_id=1, source_target_pairs={{0,256},{128,384},{256,0},{384,128},{1,257},{129,385},{257,1},{385... | collective-permute-start | bytes 1966088 | tf_op jit(solution)/shard_map/ppermute | solution.py:464
  43.1 0.0 collective-permute-done.5.relaxed
  43.2 3.2 %all-to-all-done.parts = f32[16,8,128]{2,1,0:T(8,128)S(1)} async-done(((f32[16,8,128]{2,1,0:T(8,128)}), f32[16,8,128]{2,1,0:T(8,128)S(1)}, u32[]{:S(2)}, u32[]{:S(2)}) %all-to-all-start) | async-done | bytes 65568 | tf_op jit(solution)/shard_map/all_to_all | solution.py:465
  46.4 0.6 relay.1
  47.0 12.8 %all-to-all-start.1 = ((f32[32,2,128]{2,1,0:T(2,128)}), f32[32,2,128]{2,1,0:T(2,128)S(1)}, u32[]{:S(2)}, u32[]{:S(2)}) async-start(f32[32,2,128]{2,1,0:T(2,128)} %bitcast.1), calls=%async_computation.1 | async-start | bytes 65536 | tf_op jit(solution)/shard_map/all_to_all | solution.py:468
  59.8 0.0 collective-permute-done.6.again
  59.8 0.9 %residual.1 = (f32[1,5,4,64,128]{4,3,2,1,0:T(8,128)}, f32[8,128]{1,0:T(8,128)S(1)}) custom-call(f32[5,4,64,128]{3,2,1,0:T(8,128)S(1)} %collective-permute-done.5.relaxed, f32[5,4,64,128]{3,2,1,0:T(8,128)S(1)} %collective-permute-done.6.again), custom_call_target="tpu_custom_call" | custom-call | tf_op jit(solution)/shard_map/residual/pallas_call | solution.py:374
  60.7 7.8 %all-to-all-done.1 = f32[32,2,128]{2,1,0:T(2,128)S(1)} async-done(((f32[32,2,128]{2,1,0:T(2,128)}), f32[32,2,128]{2,1,0:T(2,128)S(1)}, u32[]{:S(2)}, u32[]{:S(2)}) %all-to-all-start.1) | async-done | bytes 32800 | tf_op jit(solution)/shard_map/all_to_all | solution.py:468
  68.6 1.0 %correct.1 = f32[1,5,4,64,128]{4,3,2,1,0:T(8,128)} custom-call(f32[64,128]{1,0:T(8,128)S(1)} %bitcast.4, f32[5,4,64,128]{3,2,1,0:T(8,128)S(1)} %collective-permute-done.5.relaxed, f32[8,128]{1,0:T(8,128)S(1)} %get-tuple-element.68.written), custom_call_target="tpu_custom_call" | custom-call | tf_op jit(solution)/shard_map/correct/pallas_call | solution.py:374
Async XLA Ops:
  1.8 15.9 %collective-permute-start = (f32[5,4,64,128]{3,2,1,0:T(8,128)S(1)}, f32[5,4,64,128]{3,2,1,0:T(8,128)S(1)}, u32[]{:S(2)}, u32[]{:S(2)}) collective-permute-start(f32[5,4,64,128]{3,2,1,0:T(8,128)S(1)} %bitcast_select_fusion.own), channel_id=1, source_target_pairs={{1,2},{2,1},{3,4},{4,3},{5,6},{6,5},{7,8},{8,7},{9,10},{10,9},{11,... | collective-permute-start | bytes 1966088 | tf_op jit(solution)/shard_map/ppermute | solution.py:420
  6.7 6.8 %collective-permute-start.1 = (f32[5,2,8,8,128]{4,3,2,1,0:T(8,128)S(1)}, f32[5,2,8,8,128]{4,3,2,1,0:T(8,128)S(1)}, u32[]{:S(2)}, u32[]{:S(2)}) collective-permute-start(f32[5,2,8,8,128]{4,3,2,1,0:T(8,128)S(1)} %get-tuple-element.36.outer.refs_2_), channel_id=1, source_target_pairs={{0,1},{1,0},{2,3},{3,2},{4,5},{5,4},{6,7},{7,6},{8,9},{9,8},{10,11... | collective-permute-start | bytes 983048 | tf_op jit(solution)/shard_map/ppermute | solution.py:422
  11.6 3.5 %collective-permute-start.2 = (f32[5,2,8,8,128]{4,3,2,1,0:T(8,128)S(1)}, f32[5,2,8,8,128]{4,3,2,1,0:T(8,128)S(1)}, u32[]{:S(2)}, u32[]{:S(2)}) collective-permute-start(f32[5,2,8,8,128]{4,3,2,1,0:T(8,128)S(1)} %get-tuple-element.37.inner.refs_3_), channel_id=1, source_target_pairs={{0,1},{1,0},{2,3},{3,2},{4,5},{5,4},{6,7},{7,6},{8,9},{9,8},{10,11... | collective-permute-start | bytes 983048 | tf_op jit(solution)/shard_map/ppermute | solution.py:422
  15.2 11.3 %collective-permute-start.3 = (f32[5,4,64,128]{3,2,1,0:T(8,128)S(1)}, f32[5,4,64,128]{3,2,1,0:T(8,128)S(1)}, u32[]{:S(2)}, u32[]{:S(2)}) collective-permute-start(f32[5,4,64,128]{3,2,1,0:T(8,128)S(1)} %bitcast_select_fusion.own), channel_id=1, source_target_pairs={{0,2},{2,4},{4,6},{6,8},{8,10},{10,12},{12,14},{14,16},{16,18},{18... | collective-permute-start | bytes 1966088 | tf_op jit(solution)/shard_map/ppermute | solution.py:425
  17.7 1.6 %copy-start = (f32[1,5,4,64,128]{4,3,2,1,0:T(8,128)S(1)}, f32[1,5,4,64,128]{4,3,2,1,0:T(8,128)}, u32[]{:S(2)}) copy-start(f32[1,5,4,64,128]{4,3,2,1,0:T(8,128)} %guess.1) | copy-start | bytes 1966084
  17.7 1.6 %copy-start.1 = (f32[4,3,8,128]{3,2,1,0:T(8,128)S(1)}, f32[4,3,8,128]{3,2,1,0:T(8,128)}, u32[]{:S(2)}) copy-start(f32[4,3,8,128]{3,2,1,0:T(8,128)} %constant.10.clone.weights) | copy-start | bytes 147460
  19.7 8.3 %collective-permute-start.4 = (f32[5,4,8,8,128]{4,3,2,1,0:T(8,128)S(1)}, f32[5,4,8,8,128]{4,3,2,1,0:T(8,128)S(1)}, u32[]{:S(2)}, u32[]{:S(2)}) collective-permute-start(f32[5,4,8,8,128]{4,3,2,1,0:T(8,128)S(1)} %get-tuple-element.47.packed), channel_id=1, source_target_pairs={{0,1},{1,0},{2,3},{3,2},{4,5},{5,4},{6,7},{7,6},{8,9},{9,8},{10,11... | collective-permute-start | bytes 1966088 | tf_op jit(solution)/shard_map/ppermute | solution.py:452
  21.8 21.3 %collective-permute-start.5 = (f32[5,4,64,128]{3,2,1,0:T(8,128)S(1)}, f32[5,4,64,128]{3,2,1,0:T(8,128)S(1)}, u32[]{:S(2)}, u32[]{:S(2)}) collective-permute-start(f32[5,4,64,128]{3,2,1,0:T(8,128)S(1)} %far.1.own), channel_id=1, source_target_pairs={{0,128},{128,256},{256,384},{384,0},{1,129},{129,257},{257,385},{3... | collective-permute-start | bytes 1966088 | tf_op jit(solution)/shard_map/ppermute | solution.py:442
  31.7 14.7 %all-to-all-start = ((f32[16,8,128]{2,1,0:T(8,128)}), f32[16,8,128]{2,1,0:T(8,128)S(1)}, u32[]{:S(2)}, u32[]{:S(2)}) async-start(f32[16,8,128]{2,1,0:T(8,128)} %get-tuple-element.66), calls=%async_computation | async-start | bytes 131072 | tf_op jit(solution)/shard_map/all_to_all | solution.py:465
  38.6 21.2 %collective-permute-start.6 = (f32[5,4,64,128]{3,2,1,0:T(8,128)S(1)}, f32[5,4,64,128]{3,2,1,0:T(8,128)S(1)}, u32[]{:S(2)}, u32[]{:S(2)}) collective-permute-start(f32[5,4,64,128]{3,2,1,0:T(8,128)S(1)} %get-tuple-element.67), channel_id=1, source_target_pairs={{0,256},{128,384},{256,0},{384,128},{1,257},{129,385},{257,1},{385... | collective-permute-start | bytes 1966088 | tf_op jit(solution)/shard_map/ppermute | solution.py:464
  47.0 21.6 %all-to-all-start.1 = ((f32[32,2,128]{2,1,0:T(2,128)}), f32[32,2,128]{2,1,0:T(2,128)S(1)}, u32[]{:S(2)}, u32[]{:S(2)}) async-start(f32[32,2,128]{2,1,0:T(2,128)} %bitcast.1), calls=%async_computation.1 | async-start | bytes 65536 | tf_op jit(solution)/shard_map/all_to_all | solution.py:468
